TPU v7x, 32 devices: a whole 2x2x4 slice. The times are simulated.
32 devices in a mesh: dp: 2 (over core), ctx: 4 (over z), head: 4 (over y, x).
Axes of the slice: x: 2, y: 2, z: 4, core: 2. Of those that a mesh axis runs over, the one named last changes fastest.
Arguments:
- tokens: bfloat16 [6144, 1536], P(('dp', 'ctx'), 'head'), may hold values from -6 to 6
- segment_ids: int32 [6144], P('dp'), may hold values from 0 to 1, as said below
- gain_attn: float32 [1536], replicated, may hold values from 0.5 to 1.5
- w_query: bfloat16 [1536, 1536], P(('dp', 'ctx'), 'head'), may hold values from -0.15625 to 0.15625
- w_key: bfloat16 [1536, 1536], P(('dp', 'ctx'), 'head'), may hold values from -0.15625 to 0.15625
- w_value: bfloat16 [1536, 1536], P(('dp', 'ctx'), 'head'), may hold values from -0.15625 to 0.15625
- w_output: bfloat16 [1536, 1536], P('head', ('dp', 'ctx')), may hold values from -0.4375 to 0.4375
- lambda_vec: float32 [4, 64], replicated, may hold values from -1.25 to 1.25
- gain_heads: float32 [128], replicated, may hold values from 0.5 to 1.5
- gain_ffn: float32 [1536], replicated, may hold values from 0.5 to 1.5
- w_gate: bfloat16 [1536, 4096], P(('dp', 'ctx'), 'head'), may hold values from -0.15625 to 0.15625
- w_up: bfloat16 [1536, 4096], P(('dp', 'ctx'), 'head'), may hold values from -0.15625 to 0.15625
- w_down: bfloat16 [4096, 1536], P('head', ('dp', 'ctx')), may hold values from -0.1875 to 0.1875
- grad_out: bfloat16 [6144, 1536], P(('dp', 'ctx'), 'head'), may hold values from -6 to 6
Outputs:
- output: bfloat16 [6144, 1536], P(('dp', 'ctx'), 'head')
- grad_tokens: float32 [6144, 1536], P(('dp', 'ctx'), 'head')
- grad_gain_attn: float32 [1536], replicated
- grad_w_query: float32 [1536, 1536], P(('dp', 'ctx'), 'head')
- grad_w_key: float32 [1536, 1536], P(('dp', 'ctx'), 'head')
- grad_w_value: float32 [1536, 1536], P(('dp', 'ctx'), 'head')
- grad_w_output: float32 [1536, 1536], P('head', ('dp', 'ctx'))
- grad_lambda: float32 [4, 64], replicated
- grad_gain_heads: float32 [128], replicated
- grad_gain_ffn: float32 [1536], replicated
- grad_w_gate: float32 [1536, 4096], P(('dp', 'ctx'), 'head')
- grad_w_up: float32 [1536, 4096], P(('dp', 'ctx'), 'head')
- grad_w_down: float32 [4096, 1536], P('head', ('dp', 'ctx'))
Inputs may be any that keep to these rules, and one draw needn't show every extreme that they name: `segment_ids`: within each group of 3072 rows the ids start at 0, never fall, and take every value up to 1; every sequence holds at least 1024 tokens.
All inputs are finite; a program needn't handle non-finite values.
Results may differ from a plain program's by a relative error of at most 0.03.
Values may be sent and summed in bfloat16 or wider, within the bound.
No kernel may reach another device: no remote copies, remote signals or barrier semaphores. Data moves between devices by JAX's collectives and lax.ppermute only.
A program may use at most 192 MiB of HBM per device.

v0:
```python
import math

import jax
import jax.numpy as jnp
from jax import lax
from jax.sharding import PartitionSpec as P

HALF = 64
VD = 128
LAYER = 6


EPSILON = 1e-06
ROPE_BASE = 10000.0
NEGATIVE = -1e30


def lambda_start():
    return 0.8 - 0.6 * math.exp(-0.3 * (LAYER - 1))


def rotate(values, cosine, sine_table):
    half_width = values.shape[-1] // 2
    lower_half = values[..., :half_width]
    upper_half = values[..., half_width:]
    return jnp.concatenate(
        [
            lower_half * cosine - upper_half * sine_table,
            upper_half * cosine + lower_half * sine_table,
        ],
        axis=-1,
    )


def rotate_back(gradient, cosine, sine_table):
    half_width = gradient.shape[-1] // 2
    lower_half = gradient[..., :half_width]
    upper_half = gradient[..., half_width:]
    return jnp.concatenate(
        [
            lower_half * cosine + upper_half * sine_table,
            upper_half * cosine - lower_half * sine_table,
        ],
        axis=-1,
    )


def norm_back(gradient, normed, inverse):
    return inverse * (gradient - normed * jnp.mean(gradient * normed, axis=-1, keepdims=True))


def outer_sum(left, right):
    return jnp.einsum("ta,tb->ab", left, right, preferred_element_type=jnp.float32)


def times_rows(left, weight):
    return jnp.einsum("tb,ab->ta", left, weight, preferred_element_type=jnp.float32)


def score_pair(queries, key_rows, scale):
    score_one = (
        jnp.einsum(
            "thd,khd->htk", queries[:, :, 0], key_rows[:, :, 0], preferred_element_type=jnp.float32
        )
        * scale
    )
    score_two = (
        jnp.einsum(
            "thd,khd->htk", queries[:, :, 1], key_rows[:, :, 1], preferred_element_type=jnp.float32
        )
        * scale
    )
    return (score_one, score_two)


def softmax_weights(score, allowed, log_total):
    return jnp.where(allowed[None], jnp.exp(score - log_total[..., None]), 0.0)


def pair_gradients(queries, key_rows, value_rows, allowed, stats, grad_one, grad_two, scale):
    score_one, score_two = score_pair(queries, key_rows, scale)
    weight_one = softmax_weights(score_one, allowed, stats[0])
    weight_two = softmax_weights(score_two, allowed, stats[1])
    inner_one = jnp.einsum("thd,khd->htk", grad_one, value_rows, preferred_element_type=jnp.float32)
    inner_two = jnp.einsum("thd,khd->htk", grad_two, value_rows, preferred_element_type=jnp.float32)
    dscore_one = (weight_one * (inner_one - stats[2][..., None])).astype(jnp.bfloat16)
    dscore_two = (weight_two * (inner_two - stats[3][..., None])).astype(jnp.bfloat16)
    query_grad = scale * jnp.stack(
        [
            jnp.einsum(
                "htk,khd->thd", dscore_one, key_rows[:, :, 0], preferred_element_type=jnp.float32
            ),
            jnp.einsum(
                "htk,khd->thd", dscore_two, key_rows[:, :, 1], preferred_element_type=jnp.float32
            ),
        ],
        axis=2,
    )
    key_grad = scale * jnp.stack(
        [
            jnp.einsum(
                "htk,thd->khd", dscore_one, queries[:, :, 0], preferred_element_type=jnp.float32
            ),
            jnp.einsum(
                "htk,thd->khd", dscore_two, queries[:, :, 1], preferred_element_type=jnp.float32
            ),
        ],
        axis=2,
    )
    value_grad = jnp.einsum(
        "htk,thd->khd",
        weight_one.astype(jnp.bfloat16),
        grad_one,
        preferred_element_type=jnp.float32,
    ) + jnp.einsum(
        "htk,thd->khd",
        weight_two.astype(jnp.bfloat16),
        grad_two,
        preferred_element_type=jnp.float32,
    )
    return (query_grad, key_grad, value_grad)


def per_device(
    tokens,
    segment_ids,
    gain_attn,
    w_query,
    w_key,
    w_value,
    w_output,
    lambda_vec,
    gain_heads,
    gain_ffn,
    w_gate,
    w_up,
    w_down,
    grad_out,
):
    row_count = tokens.shape[0]
    slice_width = tokens.shape[1]
    ctx_count = lax.axis_size("ctx")
    ctx_place = lax.axis_index("ctx")
    head_place = lax.axis_index("head")
    local_heads = w_query.shape[1] // (2 * HALF)
    scale = HALF ** (-0.5)
    lambda_init = lambda_start()
    first_row = ctx_place * row_count
    row_index = first_row + jnp.arange(row_count, dtype=jnp.int32)
    my_seg = lax.dynamic_slice_in_dim(segment_ids, first_row, row_count, 0)
    before = jnp.sum((segment_ids[None, :] < my_seg[:, None]).astype(jnp.int32), axis=1)
    frequency = ROPE_BASE ** (-(jnp.arange(HALF // 2, dtype=jnp.float32) * 2.0 / HALF))
    angles = (row_index - before).astype(jnp.float32)[:, None] * frequency[None, :]
    cosine = jnp.cos(angles)[:, None, None, :]
    sine_table = jnp.sin(angles)[:, None, None, :]
    whole_x, whole_dy = (
        lax.all_gather(tokens, "head", axis=1, tiled=True),
        lax.all_gather(grad_out, "head", axis=1, tiled=True),
    )
    wq, wk, wv, wo, wg, wu, wd = (
        lax.all_gather(w_query, ("dp", "ctx"), axis=0, tiled=True),
        lax.all_gather(w_key, ("dp", "ctx"), axis=0, tiled=True),
        lax.all_gather(w_value, ("dp", "ctx"), axis=0, tiled=True),
        lax.all_gather(w_output, ("dp", "ctx"), axis=1, tiled=True),
        lax.all_gather(w_gate, ("dp", "ctx"), axis=0, tiled=True),
        lax.all_gather(w_up, ("dp", "ctx"), axis=0, tiled=True),
        lax.all_gather(w_down, ("dp", "ctx"), axis=1, tiled=True),
    )
    x_full = whole_x.astype(jnp.float32)
    inv_in = lax.rsqrt(jnp.mean(x_full * x_full, axis=-1, keepdims=True) + EPSILON)
    unit_in = x_full * inv_in
    normed_in = (unit_in * gain_attn).astype(jnp.bfloat16)
    query_pre = jnp.dot(normed_in, wq, preferred_element_type=jnp.float32).reshape(
        row_count, local_heads, 2, HALF
    )
    queries = rotate(query_pre, cosine, sine_table).astype(jnp.bfloat16)
    key_pre = jnp.dot(normed_in, wk, preferred_element_type=jnp.float32).reshape(
        row_count, local_heads, 2, HALF
    )
    key_local = rotate(key_pre, cosine, sine_table).astype(jnp.bfloat16)
    value_local = jnp.dot(normed_in, wv, preferred_element_type=jnp.float32).astype(jnp.bfloat16)
    all_keys, all_values = (
        lax.all_gather(key_local.reshape(row_count, -1), "ctx", axis=0, tiled=True),
        lax.all_gather(value_local, "ctx", axis=0, tiled=True),
    )
    value_local = value_local.reshape(row_count, local_heads, VD)
    lambda_value = (
        jnp.exp(jnp.sum(lambda_vec[0] * lambda_vec[1]))
        - jnp.exp(jnp.sum(lambda_vec[2] * lambda_vec[3]))
        + lambda_init
    )

    def key_block(block_id):
        block_first = block_id * row_count
        key_blk = lax.dynamic_slice_in_dim(all_keys, block_first, row_count, 0).reshape(
            row_count, local_heads, 2, HALF
        )
        value_blk = lax.dynamic_slice_in_dim(all_values, block_first, row_count, 0).reshape(
            row_count, local_heads, VD
        )
        key_seg = lax.dynamic_slice_in_dim(segment_ids, block_first, row_count, 0)
        key_index = block_first + jnp.arange(row_count, dtype=jnp.int32)
        allowed = (my_seg[:, None] == key_seg[None, :]) & (key_index[None, :] <= row_index[:, None])
        return (key_blk, value_blk, allowed)

    def stats_step(block_id, running):

        def stats_compute(current):
            max_one, total_one, max_two, total_two = current
            key_blk, value_blk, allowed = key_block(block_id)
            score_one, score_two = score_pair(queries, key_blk, scale)
            score_one = jnp.where(allowed[None], score_one, NEGATIVE)
            score_two = jnp.where(allowed[None], score_two, NEGATIVE)
            new_one = jnp.maximum(max_one, jnp.max(score_one, axis=-1))
            new_two = jnp.maximum(max_two, jnp.max(score_two, axis=-1))
            total_one = total_one * jnp.exp(max_one - new_one) + jnp.sum(
                jnp.where(allowed[None], jnp.exp(score_one - new_one[..., None]), 0.0), axis=-1
            )
            total_two = total_two * jnp.exp(max_two - new_two) + jnp.sum(
                jnp.where(allowed[None], jnp.exp(score_two - new_two[..., None]), 0.0), axis=-1
            )
            return (new_one, total_one, new_two, total_two)

        return lax.cond(block_id <= ctx_place, stats_compute, lambda current: current, running)

    start_max = jnp.full((local_heads, row_count), NEGATIVE, jnp.float32)
    start_total = jnp.zeros((local_heads, row_count), jnp.float32)
    max_one, total_one, max_two, total_two = lax.fori_loop(
        0, ctx_count, stats_step, (start_max, start_total, start_max, start_total)
    )
    log_one = max_one + jnp.log(total_one)
    log_two = max_two + jnp.log(total_two)

    def value_step(block_id, running):

        def value_compute(current):
            out_one, out_two = current
            key_blk, value_blk, allowed = key_block(block_id)
            score_one, score_two = score_pair(queries, key_blk, scale)
            prob_one = softmax_weights(score_one, allowed, log_one).astype(jnp.bfloat16)
            prob_two = softmax_weights(score_two, allowed, log_two).astype(jnp.bfloat16)
            out_one = out_one + jnp.einsum(
                "htk,khd->thd", prob_one, value_blk, preferred_element_type=jnp.float32
            )
            out_two = out_two + jnp.einsum(
                "htk,khd->thd", prob_two, value_blk, preferred_element_type=jnp.float32
            )
            return (out_one, out_two)

        return lax.cond(block_id <= ctx_place, value_compute, lambda current: current, running)

    start_out = jnp.zeros((row_count, local_heads, VD), jnp.float32)
    out_one, out_two = lax.fori_loop(0, ctx_count, value_step, (start_out, start_out))
    mixed = out_one - lambda_value * out_two
    inv_head = lax.rsqrt(jnp.mean(mixed * mixed, axis=-1, keepdims=True) + EPSILON)
    unit_head = mixed * inv_head
    head_out = (
        (unit_head * gain_heads * (1.0 - lambda_init))
        .astype(jnp.bfloat16)
        .reshape(row_count, local_heads * VD)
    )
    branch_attn = lax.psum_scatter(
        jnp.dot(head_out, wo, preferred_element_type=jnp.float32).astype(jnp.bfloat16),
        "head",
        scatter_dimension=1,
        tiled=True,
    ).astype(jnp.float32)
    residual = tokens.astype(jnp.float32) + branch_attn
    whole_resid = lax.all_gather(residual.astype(jnp.bfloat16), "head", axis=1, tiled=True).astype(
        residual.dtype
    )
    inv_mid = lax.rsqrt(jnp.mean(whole_resid * whole_resid, axis=-1, keepdims=True) + EPSILON)
    unit_mid = whole_resid * inv_mid
    normed_mid = (unit_mid * gain_ffn).astype(jnp.bfloat16)
    gate_pre = jnp.dot(normed_mid, wg, preferred_element_type=jnp.float32)
    up_pre = jnp.dot(normed_mid, wu, preferred_element_type=jnp.float32)
    sigmoid_gate = jax.nn.sigmoid(gate_pre)
    hidden = (gate_pre * sigmoid_gate * up_pre).astype(jnp.bfloat16)
    branch_ffn = lax.psum_scatter(
        jnp.dot(hidden, wd, preferred_element_type=jnp.float32).astype(jnp.bfloat16),
        "head",
        scatter_dimension=1,
        tiled=True,
    ).astype(jnp.float32)
    output = (residual + branch_ffn).astype(jnp.bfloat16)
    grad_down = outer_sum(hidden, whole_dy)
    grad_hidden = times_rows(whole_dy, wd)
    grad_gate = (
        grad_hidden * up_pre * sigmoid_gate * (1.0 + gate_pre * (1.0 - sigmoid_gate))
    ).astype(jnp.bfloat16)
    grad_up = (grad_hidden * gate_pre * sigmoid_gate).astype(jnp.bfloat16)
    grad_gate_w = outer_sum(normed_mid, grad_gate)
    grad_up_w = outer_sum(normed_mid, grad_up)
    grad_mid = lax.psum(
        (times_rows(grad_gate, wg) + times_rows(grad_up, wu)).astype(jnp.bfloat16), "head"
    ).astype(jnp.float32)
    ffn_gain_term = jnp.where(head_place == 0, jnp.sum(grad_mid * unit_mid, axis=0), 0.0)
    first_col = head_place * slice_width
    resid_full = norm_back(grad_mid * gain_ffn, unit_mid, inv_mid)
    grad_residual = lax.dynamic_slice_in_dim(
        resid_full, first_col, slice_width, 1
    ) + grad_out.astype(jnp.float32)
    whole_branch = lax.all_gather(grad_residual.astype(jnp.bfloat16), "head", axis=1, tiled=True)
    grad_output_w = outer_sum(head_out, whole_branch)
    grad_head = times_rows(whole_branch, wo).reshape(row_count, local_heads, VD)
    heads_gain_term = jnp.sum(grad_head * unit_head, axis=(0, 1)) * (1.0 - lambda_init)
    grad_mixed = norm_back(grad_head * gain_heads * (1.0 - lambda_init), unit_head, inv_head)
    lambda_term = -jnp.sum(grad_mixed * out_two)
    grad_one = grad_mixed.astype(jnp.bfloat16)
    grad_two = (-lambda_value * grad_mixed).astype(jnp.bfloat16)
    delta_one = jnp.sum(grad_one * out_one, axis=-1).T
    delta_two = jnp.sum(grad_two * out_two, axis=-1).T
    stats = (log_one, log_two, delta_one, delta_two)
    start_query = jnp.zeros((row_count, local_heads, 2, HALF), jnp.float32)

    def grad_step(block_id, running):

        def grad_compute(current):
            query_acc, key_acc, value_acc = current
            key_blk, value_blk, allowed = key_block(block_id)
            query_grad, key_grad, value_grad = pair_gradients(
                queries, key_blk, value_blk, allowed, stats, grad_one, grad_two, scale
            )
            key_acc = lax.dynamic_update_slice_in_dim(
                key_acc, key_grad.reshape(row_count, -1), block_id * row_count, 0
            )
            value_acc = lax.dynamic_update_slice_in_dim(
                value_acc, value_grad.reshape(row_count, -1), block_id * row_count, 0
            )
            return (query_acc + query_grad, key_acc, value_acc)

        return lax.cond(block_id <= ctx_place, grad_compute, lambda current: current, running)

    start_keys = jnp.zeros((ctx_count * row_count, local_heads * 2 * HALF), jnp.float32)
    start_values = jnp.zeros((ctx_count * row_count, local_heads * VD), jnp.float32)
    query_acc, key_acc, value_acc = lax.fori_loop(
        0, ctx_count, grad_step, (start_query, start_keys, start_values)
    )
    own_key_grad, own_value_grad = (
        lax.psum_scatter(
            key_acc.astype(jnp.bfloat16), "ctx", scatter_dimension=0, tiled=True
        ).astype(jnp.float32),
        lax.psum_scatter(
            value_acc.astype(jnp.bfloat16), "ctx", scatter_dimension=0, tiled=True
        ).astype(jnp.float32),
    )
    grad_query_pre = (
        rotate_back(query_acc, cosine, sine_table).reshape(row_count, -1).astype(jnp.bfloat16)
    )
    grad_key_pre = (
        rotate_back(own_key_grad.reshape(row_count, local_heads, 2, HALF), cosine, sine_table)
        .reshape(row_count, -1)
        .astype(jnp.bfloat16)
    )
    grad_value_pre = own_value_grad.astype(jnp.bfloat16)
    grad_query_w = outer_sum(normed_in, grad_query_pre)
    grad_key_w = outer_sum(normed_in, grad_key_pre)
    grad_value_w = outer_sum(normed_in, grad_value_pre)
    grad_in = lax.psum(
        (
            times_rows(grad_query_pre, wq)
            + times_rows(grad_key_pre, wk)
            + times_rows(grad_value_pre, wv)
        ).astype(jnp.bfloat16),
        "head",
    ).astype(jnp.float32)
    attn_gain_term = jnp.where(head_place == 0, jnp.sum(grad_in * unit_in, axis=0), 0.0)
    input_full = norm_back(grad_in * gain_attn, unit_in, inv_in)
    grad_tokens = lax.dynamic_slice_in_dim(input_full, first_col, slice_width, 1) + grad_residual
    summed_w = (
        lax.psum_scatter(
            grad_query_w.astype(jnp.bfloat16), ("dp", "ctx"), scatter_dimension=0, tiled=True
        ).astype(jnp.float32),
        lax.psum_scatter(
            grad_key_w.astype(jnp.bfloat16), ("dp", "ctx"), scatter_dimension=0, tiled=True
        ).astype(jnp.float32),
        lax.psum_scatter(
            grad_value_w.astype(jnp.bfloat16), ("dp", "ctx"), scatter_dimension=0, tiled=True
        ).astype(jnp.float32),
        lax.psum_scatter(
            grad_output_w.astype(jnp.bfloat16), ("dp", "ctx"), scatter_dimension=1, tiled=True
        ).astype(jnp.float32),
        lax.psum_scatter(
            grad_gate_w.astype(jnp.bfloat16), ("dp", "ctx"), scatter_dimension=0, tiled=True
        ).astype(jnp.float32),
        lax.psum_scatter(
            grad_up_w.astype(jnp.bfloat16), ("dp", "ctx"), scatter_dimension=0, tiled=True
        ).astype(jnp.float32),
        lax.psum_scatter(
            grad_down.astype(jnp.bfloat16), ("dp", "ctx"), scatter_dimension=1, tiled=True
        ).astype(jnp.float32),
    )
    attn_gain_grad, ffn_gain_grad, heads_gain_grad, lambda_grad = lax.psum(
        (attn_gain_term, ffn_gain_term, heads_gain_term, jnp.reshape(lambda_term, (1,))),
        ("dp", "ctx", "head"),
    )
    lambda_scalar = lambda_grad[0]
    exp_one = jnp.exp(jnp.sum(lambda_vec[0] * lambda_vec[1]))
    exp_two = jnp.exp(jnp.sum(lambda_vec[2] * lambda_vec[3]))
    grad_lambda = jnp.stack(
        [
            lambda_scalar * exp_one * lambda_vec[1],
            lambda_scalar * exp_one * lambda_vec[0],
            -lambda_scalar * exp_two * lambda_vec[3],
            -lambda_scalar * exp_two * lambda_vec[2],
        ],
        axis=0,
    )
    return (
        output,
        grad_tokens,
        attn_gain_grad,
        summed_w[0],
        summed_w[1],
        summed_w[2],
        summed_w[3],
        grad_lambda,
        heads_gain_grad,
        ffn_gain_grad,
        summed_w[4],
        summed_w[5],
        summed_w[6],
    )


def solution(mesh):
    in_specs = (
        P(("dp", "ctx"), "head"),
        P("dp"),
        P(),
        P(("dp", "ctx"), "head"),
        P(("dp", "ctx"), "head"),
        P(("dp", "ctx"), "head"),
        P("head", ("dp", "ctx")),
        P(),
        P(),
        P(),
        P(("dp", "ctx"), "head"),
        P(("dp", "ctx"), "head"),
        P("head", ("dp", "ctx")),
        P(("dp", "ctx"), "head"),
    )
    out_specs = (
        P(("dp", "ctx"), "head"),
        P(("dp", "ctx"), "head"),
        P(),
        P(("dp", "ctx"), "head"),
        P(("dp", "ctx"), "head"),
        P(("dp", "ctx"), "head"),
        P("head", ("dp", "ctx")),
        P(),
        P(),
        P(),
        P(("dp", "ctx"), "head"),
        P(("dp", "ctx"), "head"),
        P("head", ("dp", "ctx")),
    )
    return jax.shard_map(
        per_device, mesh=mesh, in_specs=in_specs, out_specs=out_specs, check_vma=False
    )
```

profile of v0, /device:TPU:16, one launch (start us, length us, event | category | flops | bytes accessed | tf_op | source)
XLA Modules:
  0.0 1375.6 jit_solution(10868354171681091067)
XLA Ops:
  10.0 38.3 %all-gather.14.cloned.1.call-done = bf16[768,1536]{1,0:T(8,128)(2,1)} async-done(((bf16[768,384]{1,0:T(8,128)(2,1)}), bf16[768,1536]{1,0:T(8,128)(2,1)}) %all-gather.14.cloned.1.call-update) | async-done | bytes 2359312 | tf_op jit(solution)/shard_map/all_gather | solution.py:157
  50.7 21.6 %all-gather.16.cloned.1.call-done = bf16[1536,384]{1,0:T(8,128)(2,1)} async-done(((bf16[192,384]{1,0:T(8,128)(2,1)}), bf16[1536,384]{1,0:T(8,128)(2,1)}) %all-gather.16.cloned.1.call-update) | async-done | bytes 1179664 | tf_op jit(solution)/shard_map/all_gather | solution.py:163
  78.8 17.4 %all-gather.20.cloned.1.call-done = bf16[1536,384]{1,0:T(8,128)(2,1)} async-done(((bf16[192,384]{1,0:T(8,128)(2,1)}), bf16[1536,384]{1,0:T(8,128)(2,1)}) %all-gather.20.cloned.1.call-update) | async-done | bytes 1179664 | tf_op jit(solution)/shard_map/all_gather | solution.py:162
  99.8 20.3 %all-gather.24.cloned.1.call-done = bf16[1536,384]{1,0:T(8,128)(2,1)} async-done(((bf16[192,384]{1,0:T(8,128)(2,1)}), bf16[1536,384]{1,0:T(8,128)(2,1)}) %all-gather.24.cloned.1.call-update) | async-done | bytes 1179664 | tf_op jit(solution)/shard_map/all_gather | solution.py:161
  128.0 43.6 %all-gather.18.cloned.1.call-done = bf16[3072,384]{1,0:T(8,128)(2,1)} async-done(((bf16[768,384]{1,0:T(8,128)(2,1)}), bf16[3072,384]{1,0:T(8,128)(2,1)}) %all-gather.18.cloned.1.call-update) | async-done | bytes 2359312 | tf_op jit(solution)/shard_map/all_gather | solution.py:184
  174.5 48.5 %all-gather.22.cloned.1.call-done = bf16[3072,384]{0,1:T(8,128)(2,1)} async-done(((bf16[768,384]{0,1:T(8,128)(2,1)}), bf16[3072,384]{0,1:T(8,128)(2,1)}) %all-gather.22.cloned.1.call-update) | async-done | bytes 2359312 | tf_op jit(solution)/shard_map/all_gather | solution.py:183
  223.0 28.9 %while.54 = (s32[]{:T(128)}, f32[3,768]{1,0:T(4,128)S(1)}, f32[3,768]{1,0:T(4,128)S(1)}, f32[3,768]{1,0:T(4,128)S(1)}, f32[3,768]{1,0:T(4,128)S(1)}, /*index=5*/...) while((s32[]{:T(128)}, f32[3,768]{1,0:T(4,128)S(1)}, ...), condition=%wide.region_9.10_spmd.clone, body=%wide.region_2.9_spmd.clone.sunk | while | flops 483076608 | bytes 39788904 | solution.py:228
  254.8 41.9 %while.55 = (s32[]{:T(128)}, f32[768,3,128]{0,2,1:T(8,128)}, f32[768,3,128]{0,2,1:T(8,128)}, s32[]{:T(128)}, bf16[3072,384]{0,1:T(8,128)(2,1)S(1)}, /*index=5*/s...) while((s32[]{:T(128)}, f32[768,3,128]{0,2,1:T(8,128)}, ...), condition=%wide.region_13.0_spmd.clone, body=%wide.region_10.13_spmd.clone.sunk | while | flops 1375471104 | bytes 11299189 | solution.py:253
  268.6 13.8 %conditional.10 = ((f32[768,3,128]{0,2,1:T(8,128)}, f32[768,3,128]{0,2,1:T(8,128)})) conditional(s32[]{:T(128)} %convert_element_type.362, (f32[768,3,128]{0,2,1:T(8,128)}, f32[768,3,128]{0,2,1:T(8,128)}) %tuple.168, (s32[]{:T(128)}, bf16[3072,384]{0,1:T(8,128)(2,1)S(1)}, s32[768]{0:T(1024)S(1)}, s32[3072]{0:T(1024)}, s32[]{:T(128)}, ...), branch_computations={%region_11.11_spmd, %region_12.12_spmd} | conditional | flops 1375471104 | bytes 11295858 | solution.py:250
  306.1 60.8 %reduce-scatter.34.cloned.1.call-done = bf16[384,768]{1,0:T(8,128)(2,1)} async-done(((bf16[1536,768]{1,0:T(8,128)(2,1)}), bf16[384,768]{1,0:T(8,128)(2,1)}) %reduce-scatter.34.cloned.1.call-update) | async-done | bytes 589840
  372.0 34.8 %all-gather.28.cloned.1.call-done = bf16[768,1536]{1,0:T(8,128)(2,1)} async-done(((bf16[768,384]{1,0:T(8,128)(2,1)}), bf16[768,1536]{1,0:T(8,128)(2,1)}) %all-gather.28.cloned.1.call-update) | async-done | bytes 2359312 | tf_op jit(solution)/shard_map/all_gather | solution.py:269
  409.1 36.3 %all-gather.32.cloned.1.call-done = bf16[1536,1024]{1,0:T(8,128)(2,1)} async-done(((bf16[192,1024]{1,0:T(8,128)(2,1)}), bf16[1536,1024]{1,0:T(8,128)(2,1)}) %all-gather.32.cloned.1.call-update) | async-done | bytes 3145744 | tf_op jit(solution)/shard_map/all_gather | solution.py:166
  451.6 32.6 %all-gather.30.cloned.1.call-done = bf16[1536,1024]{1,0:T(8,128)(2,1)} async-done(((bf16[192,1024]{1,0:T(8,128)(2,1)}), bf16[1536,1024]{1,0:T(8,128)(2,1)}) %all-gather.30.cloned.1.call-update) | async-done | bytes 3145744 | tf_op jit(solution)/shard_map/all_gather | solution.py:165
  490.4 32.8 %all-gather.36.cloned.1.call-done = bf16[768,1536]{1,0:T(8,128)(2,1)} async-done(((bf16[768,384]{1,0:T(8,128)(2,1)}), bf16[768,1536]{1,0:T(8,128)(2,1)}) %all-gather.36.cloned.1.call-update) | async-done | bytes 2359312 | tf_op jit(solution)/shard_map/all_gather | solution.py:158
  523.2 38.8 %all-gather.34.cloned.1.call-done = bf16[1024,1536]{0,1:T(8,128)(2,1)} async-done(((bf16[1024,192]{0,1:T(8,128)(2,1)}), bf16[1024,1536]{0,1:T(8,128)(2,1)}) %all-gather.34.cloned.1.call-update) | async-done | bytes 3145744 | tf_op jit(solution)/shard_map/all_gather | solution.py:167
  578.9 73.9 %all-reduce.4.cloned.1.call-done = bf16[768,1536]{1,0:T(8,128)(2,1)} async-done(((bf16[768,1536]{1,0:T(8,128)(2,1)}), bf16[768,1536]{1,0:T(8,128)(2,1)}) %all-reduce.4.cloned.1.call-update) | async-done | bytes 2359312 | tf_op jit(solution)/shard_map/psum | solution.py:294
  661.5 37.4 %all-gather.38.cloned.1.call-done = bf16[768,1536]{1,0:T(8,128)(2,1)} async-done(((bf16[768,384]{1,0:T(8,128)(2,1)}), bf16[768,1536]{1,0:T(8,128)(2,1)}) %all-gather.38.cloned.1.call-update) | async-done | bytes 2359312 | tf_op jit(solution)/shard_map/all_gather | solution.py:303
  708.0 59.9 %while.56 = (s32[]{:T(128)}, f32[768,3,2,64]{0,3,1,2:T(8,128)S(1)}, bf16[3072,384]{0,1:T(8,128)(2,1)}, bf16[3072,384]{0,1:T(8,128)(2,1)}, s32[]{:T(128)}, /*inde...) while((s32[]{:T(128)}, f32[768,3,2,64]{0,3,1,2:T(8,128)S(1)}, ...), condition=%wide.region_28.29_spmd.clone, body=%wide.region_25.0_spmd.clone.sunk | while | flops 3210413568 | bytes 89149880 | solution.py:336
  708.0 20.0 %conditional.11 = ((f32[768,3,2,64]{0,3,1,2:T(8,128)S(1)}, bf16[3072,384]{0,1:T(8,128)(2,1)}, bf16[3072,384]{0,1:T(8,128)(2,1)})) conditional(s32[]{:T(128)} %convert_element_type.363, (f32[768,3,2,64]{0,3,1,2:T(8,128)S(1)}, bf16[3072,384]{0,1:T(8,128)(2,1)}, bf16[3072,384]{0,1:T(8,128)(2,1)}) %tuple.171, (s32[]{:T(128)}, ...), branch_computations={%region_26.26_spmd, %region_27.27_spmd} | conditional | flops 3210413568 | bytes 89146464 | solution.py:332
  728.0 20.0 %conditional.11 = ((f32[768,3,2,64]{0,3,1,2:T(8,128)S(1)}, bf16[3072,384]{0,1:T(8,128)(2,1)}, bf16[3072,384]{0,1:T(8,128)(2,1)})) conditional(s32[]{:T(128)} %convert_element_type.363, (f32[768,3,2,64]{0,3,1,2:T(8,128)S(1)}, bf16[3072,384]{0,1:T(8,128)(2,1)}, bf16[3072,384]{0,1:T(8,128)(2,1)}) %tuple.171, (s32[]{:T(128)}, ...), branch_computations={%region_26.26_spmd, %region_27.27_spmd} | conditional | flops 3210413568 | bytes 89146464 | solution.py:332
  747.9 20.0 %conditional.11 = ((f32[768,3,2,64]{0,3,1,2:T(8,128)S(1)}, bf16[3072,384]{0,1:T(8,128)(2,1)}, bf16[3072,384]{0,1:T(8,128)(2,1)})) conditional(s32[]{:T(128)} %convert_element_type.363, (f32[768,3,2,64]{0,3,1,2:T(8,128)S(1)}, bf16[3072,384]{0,1:T(8,128)(2,1)}, bf16[3072,384]{0,1:T(8,128)(2,1)}) %tuple.171, (s32[]{:T(128)}, ...), branch_computations={%region_26.26_spmd, %region_27.27_spmd} | conditional | flops 3210413568 | bytes 89146464 | solution.py:332
  805.8 29.8 %reduce-scatter.16.cloned.1.call-done = bf16[768,384]{0,1:T(8,128)(2,1)} async-done(((bf16[3072,384]{0,1:T(8,128)(2,1)}), bf16[768,384]{0,1:T(8,128)(2,1)}) %reduce-scatter.16.cloned.1.call-update) | async-done | bytes 589840 | tf_op jit(solution)/shard_map/reduce_scatter | solution.py:340
  845.3 40.1 %reduce-scatter.18.cloned.1.call-done = bf16[768,384]{0,1:T(8,128)(2,1)} async-done(((bf16[3072,384]{0,1:T(8,128)(2,1)}), bf16[768,384]{0,1:T(8,128)(2,1)}) %reduce-scatter.18.cloned.1.call-update) | async-done | bytes 589840 | tf_op jit(solution)/shard_map/reduce_scatter | solution.py:343
  903.6 22.4 %reduce-scatter.36.cloned.1.call-done = bf16[384,768]{1,0:T(8,128)(2,1)} async-done(((bf16[1536,768]{1,0:T(8,128)(2,1)}), bf16[384,768]{1,0:T(8,128)(2,1)}) %reduce-scatter.36.cloned.1.call-update) | async-done | bytes 589840
  930.9 65.5 %reduce-scatter.32.cloned.1.call-done = bf16[1024,192]{0,1:T(8,128)(2,1)} async-done(((bf16[1024,1536]{0,1:T(8,128)(2,1)}), bf16[1024,192]{0,1:T(8,128)(2,1)}) %reduce-scatter.32.cloned.1.call-update) | async-done | bytes 393232 | tf_op jit(solution)/shard_map/reduce_scatter | solution.py:389
  998.4 68.3 %reduce-scatter.30.cloned.1.call-done = bf16[192,1024]{1,0:T(8,128)(2,1)} async-done(((bf16[1536,1024]{1,0:T(8,128)(2,1)}), bf16[192,1024]{1,0:T(8,128)(2,1)}) %reduce-scatter.30.cloned.1.call-update) | async-done | bytes 393232 | tf_op jit(solution)/shard_map/reduce_scatter | solution.py:386
  1068.6 68.5 %reduce-scatter.28.cloned.1.call-done = bf16[192,1024]{1,0:T(8,128)(2,1)} async-done(((bf16[1536,1024]{1,0:T(8,128)(2,1)}), bf16[192,1024]{1,0:T(8,128)(2,1)}) %reduce-scatter.28.cloned.1.call-update) | async-done | bytes 393232 | tf_op jit(solution)/shard_map/reduce_scatter | solution.py:383
  1139.1 35.8 %reduce-scatter.26.cloned.1.call-done = bf16[384,192]{0,1:T(8,128)(2,1)} async-done(((bf16[384,1536]{0,1:T(8,128)(2,1)}), bf16[384,192]{0,1:T(8,128)(2,1)}) %reduce-scatter.26.cloned.1.call-update) | async-done | bytes 147472 | tf_op jit(solution)/shard_map/reduce_scatter | solution.py:380
  1176.5 76.3 %all-reduce.6.cloned.1.call-done = bf16[768,1536]{1,0:T(8,128)(2,1)} async-done(((bf16[768,1536]{1,0:T(8,128)(2,1)}), bf16[768,1536]{1,0:T(8,128)(2,1)}) %all-reduce.6.cloned.1.call-update) | async-done | bytes 2359312 | tf_op jit(solution)/shard_map/psum | solution.py:359
  1259.6 40.4 %all-reduce = (f32[1536]{0:T(1024)}, f32[]{:T(128)}, f32[128]{0:T(128)}, f32[1536]{0:T(1024)}) all-reduce(f32[1536]{0:T(1024)S(1)} %broadcast_select_fusion.1, f32[]{:T(128)S(6)} %neg.23, f32[128]{0:T(128)S(1)} %broadcast_multiply_fusion.3, f32[1536]{0:T(1024)S(1)} %copy-done.36), channel_id=1, replica_groups=mesh['dp'=2,'ctx'=4,'head'=4] {'dp','ctx','head'}, use_global_device_ids=true, to_apply=%region_34.35 | all-reduce | flops 3201 | bytes 25608 | tf_op jit(solution)/shard_map/psum | solution.py:393
  1303.1 26.3 %reduce-scatter.22.cloned.1.call-done = bf16[192,384]{1,0:T(8,128)(2,1)} async-done(((bf16[1536,384]{1,0:T(8,128)(2,1)}), bf16[192,384]{1,0:T(8,128)(2,1)}) %reduce-scatter.22.cloned.1.call-update) | async-done | bytes 147472 | tf_op jit(solution)/shard_map/reduce_scatter | solution.py:374
  1335.7 31.6 %reduce-scatter.24.cloned.1.call-done = bf16[192,384]{1,0:T(8,128)(2,1)} async-done(((bf16[1536,384]{1,0:T(8,128)(2,1)}), bf16[192,384]{1,0:T(8,128)(2,1)}) %reduce-scatter.24.cloned.1.call-update) | async-done | bytes 147472 | tf_op jit(solution)/shard_map/reduce_scatter | solution.py:377
  (392 shorter events, 370.4 us)
Async XLA Ops:
  7.2 41.1 %all-gather.14.cloned.1.call-start = ((), (), s32[]{:S(2)}) async-start(), calls=%async_computation.11 | async-start | bytes 2949120 | tf_op jit(solution)/shard_map/all_gather | solution.py:157
  7.9 64.3 %all-gather.16.cloned.1.call-start = ((), (), s32[]{:S(2)}) async-start(), calls=%async_computation.12 | async-start | bytes 1327104 | tf_op jit(solution)/shard_map/all_gather | solution.py:163
  8.7 87.6 %all-gather.20.cloned.1.call-start = ((), (), s32[]{:S(2)}) async-start(), calls=%async_computation.14 | async-start | bytes 1327104 | tf_op jit(solution)/shard_map/all_gather | solution.py:162
  9.4 110.8 %all-gather.24.cloned.1.call-start = ((), (), s32[]{:S(2)}) async-start(), calls=%async_computation.16 | async-start | bytes 1327104 | tf_op jit(solution)/shard_map/all_gather | solution.py:161
  10.0 161.7 %all-gather.18.cloned.1.call-start = ((), (), s32[]{:S(2)}) async-start(), calls=%async_computation.13 | async-start | bytes 2949120 | tf_op jit(solution)/shard_map/all_gather | solution.py:184
  75.8 147.2 %all-gather.22.cloned.1.call-start = ((), (), s32[]{:S(2)}) async-start(), calls=%async_computation.15 | async-start | bytes 2949120 | tf_op jit(solution)/shard_map/all_gather | solution.py:183
  124.1 176.5 %all-gather.26.cloned.1.call-start = ((), (), s32[]{:S(2)}) async-start(), calls=%async_computation.17 | async-start | bytes 1327104 | tf_op jit(solution)/shard_map/all_gather | solution.py:164
  124.9 242.0 %reduce-scatter.34.cloned.1.call-start = ((), (), s32[]{:S(2)}) async-start(), calls=%async_computation.35 | async-start | bytes 2949120
  306.0 100.8 %all-gather.28.cloned.1.call-start = ((), (), s32[]{:S(2)}) async-start(), calls=%async_computation.18 | async-start | bytes 2949120 | tf_op jit(solution)/shard_map/all_gather | solution.py:269
  369.3 76.1 %all-gather.32.cloned.1.call-start = ((), (), s32[]{:S(2)}) async-start(), calls=%async_computation.20 | async-start | bytes 3538944 | tf_op jit(solution)/shard_map/all_gather | solution.py:166
  369.9 114.3 %all-gather.30.cloned.1.call-start = ((), (), s32[]{:S(2)}) async-start(), calls=%async_computation.19 | async-start | bytes 3538944 | tf_op jit(solution)/shard_map/all_gather | solution.py:165
  370.6 152.6 %all-gather.36.cloned.1.call-start = ((), (), s32[]{:S(2)}) async-start(), calls=%async_computation.22 | async-start | bytes 2949120 | tf_op jit(solution)/shard_map/all_gather | solution.py:158
  371.2 190.8 %all-gather.34.cloned.1.call-start = ((), (), s32[]{:S(2)}) async-start(), calls=%async_computation.21 | async-start | bytes 3538944 | tf_op jit(solution)/shard_map/all_gather | solution.py:167
  371.9 280.9 %all-reduce.4.cloned.1.call-start = ((), (), s32[]{:S(2)}) async-start(), calls=%async_computation.23 | async-start | bytes 4718592 | tf_op jit(solution)/shard_map/psum | solution.py:294
  578.6 120.4 %all-gather.38.cloned.1.call-start = ((), (), s32[]{:S(2)}) async-start(), calls=%async_computation.24 | async-start | bytes 2949120 | tf_op jit(solution)/shard_map/all_gather | solution.py:303
  578.8 81.5 %copy-start.12 = (bf16[768,384]{1,0:T(8,128)(2,1)S(1)}, bf16[768,384]{1,0:T(8,128)(2,1)}, u32[]{:S(2)}) copy-start(bf16[768,384]{1,0:T(8,128)(2,1)} %param.39) | copy-start | bytes 1769476
  661.5 174.1 %reduce-scatter.16.cloned.1.call-start = ((), (), s32[]{:S(2)}) async-start(), calls=%async_computation.25 | async-start | bytes 2949120 | tf_op jit(solution)/shard_map/reduce_scatter | solution.py:340
  767.9 117.5 %reduce-scatter.18.cloned.1.call-start = ((), (), s32[]{:S(2)}) async-start(), calls=%async_computation.26 | async-start | bytes 2949120 | tf_op jit(solution)/shard_map/reduce_scatter | solution.py:343
  768.5 157.5 %reduce-scatter.36.cloned.1.call-start = ((), (), s32[]{:S(2)}) async-start(), calls=%async_computation.36 | async-start | bytes 2949120
  779.8 216.6 %reduce-scatter.32.cloned.1.call-start = ((), (), s32[]{:S(2)}) async-start(), calls=%async_computation.34 | async-start | bytes 3538944 | tf_op jit(solution)/shard_map/reduce_scatter | solution.py:389
  785.7 281.0 %reduce-scatter.30.cloned.1.call-start = ((), (), s32[]{:S(2)}) async-start(), calls=%async_computation.33 | async-start | bytes 3538944 | tf_op jit(solution)/shard_map/reduce_scatter | solution.py:386
  793.1 344.0 %reduce-scatter.28.cloned.1.call-start = ((), (), s32[]{:S(2)}) async-start(), calls=%async_computation.32 | async-start | bytes 3538944 | tf_op jit(solution)/shard_map/reduce_scatter | solution.py:383
  800.5 374.3 %reduce-scatter.26.cloned.1.call-start = ((), (), s32[]{:S(2)}) async-start(), calls=%async_computation.31 | async-start | bytes 1327104 | tf_op jit(solution)/shard_map/reduce_scatter | solution.py:380
  805.8 447.1 %all-reduce.6.cloned.1.call-start = ((), (), s32[]{:S(2)}) async-start(), calls=%async_computation.27 | async-start | bytes 4718592 | tf_op jit(solution)/shard_map/psum | solution.py:359
  892.3 409.1 %reduce-scatter.20.cloned.1.call-start = ((), (), s32[]{:S(2)}) async-start(), calls=%async_computation.28 | async-start | bytes 1327104 | tf_op jit(solution)/shard_map/reduce_scatter | solution.py:371
  896.6 432.8 %reduce-scatter.22.cloned.1.call-start = ((), (), s32[]{:S(2)}) async-start(), calls=%async_computation.29 | async-start | bytes 1327104 | tf_op jit(solution)/shard_map/reduce_scatter | solution.py:374
  899.4 467.8 %reduce-scatter.24.cloned.1.call-start = ((), (), s32[]{:S(2)}) async-start(), calls=%async_computation.30 | async-start | bytes 1327104 | tf_op jit(solution)/shard_map/reduce_scatter | solution.py:377
  930.2 322.6 %copy-start.44 = (f32[1536]{0:T(1024)S(1)}, f32[1536]{0:T(1024)}, u32[]{:S(2)}) copy-start(f32[1536]{0:T(1024)} %param.28) | copy-start | bytes 18436
  1176.5 83.2 %copy-start.36 = (f32[1536]{0:T(1024)S(1)}, f32[1536]{0:T(1024)}, u32[]{:S(2)}) copy-start(f32[1536]{0:T(1024)} %broadcast_select_fusion) | copy-start | bytes 18436
  1176.5 154.6 %copy-start.46 = (f32[4,64]{1,0:T(4,128)S(1)}, f32[4,64]{1,0:T(4,128)}, u32[]{:S(2)}) copy-start(f32[4,64]{1,0:T(4,128)} %param.33) | copy-start | bytes 3076
  1176.5 155.2 %copy-start.13 = (bf16[768,384]{1,0:T(8,128)(2,1)S(1)}, bf16[768,384]{1,0:T(8,128)(2,1)}, u32[]{:S(2)}) copy-start(bf16[768,384]{1,0:T(8,128)(2,1)} %param.39) | copy-start | bytes 1769476
  1176.5 155.2 %copy-start.32 = (f32[768]{0:T(1024)S(1)}, f32[768]{0:T(1024)}, u32[]{:S(2)}) copy-start(f32[768]{0:T(1024)} %copy-done.31) | copy-start | bytes 9220
  (54 other events, 921.4 us)
Sparse Core Ops, SparseCore 0:
  9.8 38.3 all-gather.13
  49.9 22.2 all-gather.15
  73.8 22.4 all-gather.19
  97.7 22.4 all-gather.23
  122.2 49.4 all-gather.17
  173.6 49.2 all-gather.21
  224.6 22.2 all-gather.25
  306.1 60.6 reduce-scatter.33
  369.4 37.3 all-gather.27
  408.2 37.1 all-gather.31
  447.0 37.1 all-gather.29
  485.9 37.3 all-gather.35
  524.8 37.1 all-gather.33
  578.7 74.0 all-reduce.3
  661.6 37.3 all-gather.37
  768.1 67.5 reduce-scatter.15
  837.9 47.5 reduce-scatter.17
  888.6 37.3 reduce-scatter.35
  928.4 67.9 reduce-scatter.31
  998.7 67.9 reduce-scatter.29
  1069.1 67.9 reduce-scatter.27
  1139.5 35.2 reduce-scatter.25
  1178.3 74.4 all-reduce.5
  1255.5 35.5 reduce-scatter.19
  1293.4 35.9 reduce-scatter.21
  1331.5 35.6 reduce-scatter.23
where the time goes:
time: 1390 us; the launch traced here: 1380 us
  waiting for transfers between devices  1010 us (73%)
  matrix products  179 us (13%)
  other arithmetic  67.5 us (5%)
  local copies, waits for them, and re-layouts  59.1 us (4%)
  blocking collectives  40.4 us (3%)
  between operations  18.3 us (1%)
    unnamed x28, waiting for transfers between devices  89.7 us
    psum x1, waiting for transfers between devices, per_device(): lax.psum((times_rows(grad_query_pre, wq) + times_rows(grad_key_pre, wk) +...  76.3 us
    psum x1, waiting for transfers between devices, per_device(): lax.psum((times_rows(grad_gate, wg) + times_rows(grad_up, wu)).astype(jnp...  73.9 us
    reduce_scatter x1, waiting for transfers between devices, per_device(): lax.psum_scatter(grad_gate_w.astype(jnp.bfloat16), ('dp', 'ctx'), scatter...  68.5 us
    reduce_scatter x1, waiting for transfers between devices, per_device(): lax.psum_scatter(grad_up_w.astype(jnp.bfloat16), ('dp', 'ctx'), scatter_d...  68.3 us
    reduce_scatter x1, waiting for transfers between devices, per_device(): lax.psum_scatter(grad_down.astype(jnp.bfloat16), ('dp', 'ctx'), scatter_d...  65.5 us
    all_gather x1, waiting for transfers between devices, per_device(): lax.all_gather(key_local.reshape(row_count, -1), 'ctx', axis=0, tiled=True)  48.5 us
    all_gather x1, waiting for transfers between devices, per_device(): lax.all_gather(value_local, 'ctx', axis=0, tiled=True)  43.6 us
  transfers between devices with their start and end apart: 26, of which 24 were waited for; matrix products, arithmetic and copies ran while one was open for 14% of the time, Pallas kernels for 0%

commit v1 on v0

v1 whole, which is shorter than its diff:
```python
import functools
import math

import jax
import jax.numpy as jnp
from jax import lax
from jax.experimental import pallas as pl
from jax.experimental.pallas import tpu as pltpu
from jax.sharding import PartitionSpec as P

HALF = 64
VD = 128
LAYER = 6
EPSILON = 1e-06
ROPE_BASE = 10000.0
MAX_START = -1e30
MASKED = -2e38
SCALE = HALF ** (-0.5)
LAMBDA_START = 0.8 - 0.6 * math.exp(-0.3 * (LAYER - 1))
KEEP = 1.0 - LAMBDA_START

BF16 = jnp.bfloat16
F32 = jnp.float32
VMEM_LIMIT = 60 * 1024 * 1024


def shape(dims, dtype):
    return jax.ShapeDtypeStruct(tuple(dims), dtype)


def whole(memory=pltpu.VMEM):
    return pl.BlockSpec(memory_space=memory)


def fixed(dims):
    zeros = (0,) * len(dims)
    return pl.BlockSpec(tuple(dims), lambda *_: zeros)


def call(body, outs, ins, *, name, grid=None, in_specs=None, out_specs=None, scratch=(), flops=0, move=0):
    if in_specs is None:
        in_specs = [whole(pltpu.SMEM) if a.ndim == 1 and a.dtype == jnp.int32 else whole() for a in ins]
    if out_specs is None:
        out_specs = [whole() for _ in outs]
    kwargs = {}
    if grid is not None:
        kwargs["grid"] = grid
    if not move:
        move = sum(a.size * a.dtype.itemsize for a in list(ins) + list(outs))
    return pl.pallas_call(
        body,
        out_shape=list(outs),
        in_specs=in_specs,
        out_specs=out_specs,
        scratch_shapes=list(scratch),
        compiler_params=pltpu.CompilerParams(vmem_limit_bytes=VMEM_LIMIT),
        cost_estimate=pl.CostEstimate(flops=1, bytes_accessed=1, transcendentals=0),
        name=name,
        **kwargs,
    )(*ins)


def dot(left, right, left_dim, right_dim):
    return lax.dot_general(
        left, right, (((left_dim,), (right_dim,)), ((), ())), preferred_element_type=F32
    )


def xor_pairs(count, step):
    return [(i, i ^ step) for i in range(count)]


def head_move(value, step):
    return lax.ppermute(value, "head", xor_pairs(lax.axis_size("head"), step))


def core_swap(value):
    return lax.ppermute(value, "dp", xor_pairs(lax.axis_size("dp"), 1))


def head_gather(unit):
    return [unit] + [head_move(unit, k) for k in range(1, lax.axis_size("head"))]


def after(value, *others):
    return lax.optimization_barrier((value,) + others)[0]


def place_rows(units, places, count):
    rows, cols = units[0].shape

    def body(at_ref, *refs):
        out = refs[-1]
        for i, ref in enumerate(refs[:-1]):
            start = pl.multiple_of(at_ref[i] * rows, 16)
            out[pl.ds(start, rows), :] = ref[...]

    return call(
        body, [shape((rows * count, cols), units[0].dtype)], [places] + list(units), name="place_rows"
    )[0]


def gather_rows(unit):
    return lax.all_gather(unit, ("dp", "ctx"), axis=0, tiled=True)


def scatter_rows(sums):
    return lax.psum_scatter(sums, "ctx", scatter_dimension=0, tiled=True)


def all_sum(value):
    value = value + core_swap(value)
    step = 1
    while step < lax.axis_size("head"):
        value = value + head_move(value, step)
        step *= 2
    step = 1
    while step < lax.axis_size("ctx"):
        value = value + lax.ppermute(value, "ctx", xor_pairs(lax.axis_size("ctx"), step))
        step *= 2
    return value


def head_sum(value):
    step = 1
    while step < lax.axis_size("head"):
        value = value + head_move(value, step)
        step *= 2
    return value


def turn(value, cosine, sine, sign):
    groups = []
    lanes = lax.broadcasted_iota(jnp.int32, cosine.shape, 1)
    lower = lanes % HALF < HALF // 2
    for i in range(value.shape[1] // 128):
        part = value[:, i * 128 : (i + 1) * 128]
        swapped = jnp.where(
            lower, pltpu.roll(part, 128 - HALF // 2, axis=1), pltpu.roll(part, HALF // 2, axis=1)
        )
        groups.append(part * cosine + sign * (swapped * sine))
    return jnp.concatenate(groups, axis=1)


def half_lanes(value):
    lanes = lax.broadcasted_iota(jnp.int32, value.shape, 1)
    zero = jnp.zeros_like(value)
    return jnp.where(lanes < HALF, value, zero), jnp.where(lanes < HALF, zero, value)


def norm_project_kernel(units, gain, spot, weight, cosine, sine):
    rows, cols = units[0].shape
    count = len(units)
    width = weight.shape[1]
    tile = 256

    def body(spot_ref, gain_ref, weight_ref, cos_ref, sin_ref, *refs):
        ins, (x_ref, normed_ref, inv_ref, kv_ref) = refs[:count], refs[count:]
        total = jnp.zeros((tile, 1), F32)
        for ref in ins:
            v = ref[...].astype(F32)
            total = total + jnp.sum(v * v, axis=1, keepdims=True)
        inv = lax.rsqrt(total / (count * cols) + EPSILON)
        inv_ref[...] = inv
        for k, ref in enumerate(ins):
            at = pl.ds(pl.multiple_of((spot_ref[0] ^ k) * cols, 128), cols)
            v = ref[...]
            x_ref[:, at] = v
            normed_ref[:, at] = (v.astype(F32) * inv * gain_ref[:, at]).astype(BF16)
        y = dot(normed_ref[...], weight_ref[...], 1, 0)
        for h in range(width // (2 * VD)):
            at = 2 * h * VD
            turned = turn(y[:, at : at + VD], cos_ref[...], sin_ref[...], 1.0)
            kv_ref[:, at : at + VD] = turned.astype(BF16)
            kv_ref[:, at + VD : at + 2 * VD] = y[:, at + VD : at + 2 * VD].astype(BF16)

    def tall(w):
        return pl.BlockSpec((tile, w), lambda i: (i, 0))

    wide = cols * count
    return call(
        body,
        [
            shape((rows, wide), BF16),
            shape((rows, wide), BF16),
            shape((rows, 1), F32),
            shape((rows, width), BF16),
        ],
        [spot, gain, weight, cosine, sine] + units,
        grid=(rows // tile,),
        in_specs=[whole(pltpu.SMEM), fixed(gain.shape), fixed(weight.shape), tall(128), tall(128)]
        + [tall(cols)] * count,
        out_specs=[tall(wide), tall(wide), tall(1), tall(width)],
        name="norm_project",
        flops=2 * rows * wide * width,
    )


def place_cols_kernel(units, spot):
    rows, cols = units[0].shape
    count = len(units)

    def body(spot_ref, *refs):
        for k, ref in enumerate(refs[:count]):
            at = pl.ds(pl.multiple_of((spot_ref[0] ^ k) * cols, 128), cols)
            refs[count][:, at] = ref[...]

    return call(body, [shape((rows, cols * count), BF16)], [spot] + units, name="place_cols")[0]


def query_kernel(x, weight, cols, cosine, sine):
    rows, wide = x.shape
    tile = 256

    def body(x_ref, weight_ref, cos_ref, sin_ref, out_ref):
        y = dot(x_ref[...], weight_ref[...], 1, 0)
        out_ref[...] = turn(y, cos_ref[...], sin_ref[...], 1.0).astype(BF16)

    def tall(width):
        return pl.BlockSpec((tile, width), lambda i: (i, 0))

    return call(
        body,
        [shape((rows, cols), BF16)],
        [x, weight, cosine, sine],
        grid=(rows // tile,),
        in_specs=[tall(wide), fixed((wide, cols)), tall(128), tall(128)],
        out_specs=[tall(cols)],
        name="queries",
        flops=2 * rows * wide * cols,
    )[0]


ATTN_TILE = 256


def tile_needed(meta_ref, slot, qi, ki, rows):
    key_last = (meta_ref[0] - slot) * rows + (ki + 1) * ATTN_TILE - 1
    return jnp.logical_and(meta_ref[0] >= slot, key_last >= meta_ref[1 + qi])


def score_mask(meta_ref, slot, qi, ki, rows, first):
    dims = (ATTN_TILE, ATTN_TILE)
    key_at = lax.broadcasted_iota(jnp.int32, dims, 0) + ((meta_ref[0] - slot) * rows + ki * ATTN_TILE)
    ok = key_at >= first
    if slot == 0 and qi == ki:
        query_at = lax.broadcasted_iota(jnp.int32, dims, 1) + (meta_ref[0] * rows + qi * ATTN_TILE)
        ok = jnp.logical_and(ok, key_at <= query_at)
    return ok


def attend_kernel(slot, first, last, meta, lam, q, kv, low, gain, state):
    rows = q.shape[0]
    heads = q.shape[1] // VD
    tile = ATTN_TILE
    tiles = rows // tile

    def body(meta_ref, lam_ref, q_ref, k_ref, v_ref, low_ref, gain_ref, *refs):
        if first:
            outs = refs
        else:
            acc_in, stat_in = refs[:2]
            outs = refs[2:]
        if last:
            head_ref, unit_ref, two_ref, fin_ref, acc, stat = outs
        else:
            acc, stat = outs
        if first:
            acc[...] = jnp.zeros_like(acc)
            stat[0:2, :] = jnp.full((2, rows), MAX_START, F32)
            stat[2:8, :] = jnp.zeros((6, rows), F32)
        else:
            acc[...] = acc_in[...]
            stat[...] = stat_in[...]
        for qi in range(tiles):
            cols = slice(qi * tile, (qi + 1) * tile)
            halves = half_lanes(q_ref[cols, :] * BF16(SCALE))
            for ki in range(tiles):
                if slot == 0 and ki > qi:
                    continue

                @pl.when(tile_needed(meta_ref, slot, qi, ki, rows))
                def _(qi=qi, ki=ki, cols=cols, halves=halves):
                    keys = k_ref[ki * tile : (ki + 1) * tile, :]
                    vals = v_ref[ki * tile : (ki + 1) * tile, :]
                    ok = score_mask(meta_ref, slot, qi, ki, rows, low_ref[0:1, cols])
                    for half in range(2):
                        score = jnp.where(ok, dot(keys, halves[half], 1, 1), MASKED)
                        old = stat[half : half + 1, cols]
                        new = jnp.maximum(old, jnp.max(score, axis=0, keepdims=True))
                        prob = jnp.exp(score - new)
                        fade = jnp.exp(old - new)
                        stat[half : half + 1, cols] = new
                        stat[2 + half : 3 + half, cols] = stat[2 + half : 3 + half, cols] * fade + jnp.sum(
                            prob, axis=0, keepdims=True
                        )
                        at = slice(half * VD, (half + 1) * VD)
                        acc[at, cols] = acc[at, cols] * fade + dot(vals, prob.astype(BF16), 0, 0)

        if last:
            out_one = acc[0:VD, :] / stat[2:3, :]
            out_two = acc[VD : 2 * VD, :] / stat[3:4, :]
            mixed = out_one - lam_ref[0, 0] * out_two
            inv = lax.rsqrt(jnp.mean(mixed * mixed, axis=0, keepdims=True) + EPSILON)
            unit = mixed * inv
            unit_ref[...] = unit
            two_ref[...] = out_two
            fin_ref[0:2, :] = stat[0:2, :] + jnp.log(stat[2:4, :])
            fin_ref[2:3, :] = inv
            fin_ref[3:8, :] = jnp.zeros((5, rows), F32)
            head_ref[...] = (jnp.transpose(unit) * gain_ref[...] * KEEP).astype(BF16)

    col = pl.BlockSpec((rows, VD), lambda h: (0, h))
    acc_spec = pl.BlockSpec((2 * VD, rows), lambda h: (h, 0))
    stat_spec = pl.BlockSpec((8, rows), lambda h: (h, 0))
    row_spec = pl.BlockSpec((VD, rows), lambda h: (h, 0))
    key_spec = pl.BlockSpec((rows, VD), lambda h: (0, 2 * h))
    value_spec = pl.BlockSpec((rows, VD), lambda h: (0, 2 * h + 1))
    in_specs = [whole(pltpu.SMEM), whole(pltpu.SMEM), col, key_spec, value_spec, fixed(low.shape), fixed(gain.shape)]
    ins = [meta, lam, q, kv, kv, low, gain]
    if not first:
        in_specs += [acc_spec, stat_spec]
        ins += list(state)
    outs, out_specs, scratch = [], [], []
    if last:
        outs = [
            shape((rows, heads * VD), BF16),
            shape((heads * VD, rows), F32),
            shape((heads * VD, rows), F32),
            shape((heads * 8, rows), F32),
        ]
        out_specs = [col, row_spec, row_spec, stat_spec]
        scratch = [pltpu.VMEM((2 * VD, rows), F32), pltpu.VMEM((8, rows), F32)]
    else:
        outs = [shape((heads * 2 * VD, rows), F32), shape((heads * 8, rows), F32)]
        out_specs = [acc_spec, stat_spec]
    return call(
        body,
        outs,
        ins,
        grid=(heads,),
        in_specs=in_specs,
        out_specs=out_specs,
        scratch=scratch,
        name=f"attend_{slot}",
        flops=2 * heads * rows * rows * (2 * HALF + 2 * VD),
    )


def attend_back_kernel(slot, meta, lam, q, kv, low, grad, stats, dq):
    rows = q.shape[0]
    heads = q.shape[1] // VD
    tile = ATTN_TILE
    tiles = rows // tile

    def body(meta_ref, lam_ref, q_ref, k_ref, v_ref, low_ref, grad_ref, stat_ref, *refs):
        if dq is not None:
            dq_in, dq_ref, dkv_ref, dk_acc, dv_acc = refs
            dq_ref[...] = dq_in[...]
        else:
            dq_ref, dkv_ref, dk_acc, dv_acc = refs
            dq_ref[...] = jnp.zeros_like(dq_ref)
        dk_acc[...] = jnp.zeros_like(dk_acc)
        dv_acc[...] = jnp.zeros_like(dv_acc)
        lam_value = lam_ref[0, 0]
        for qi in range(tiles):
            cols = slice(qi * tile, (qi + 1) * tile)
            q_one, q_two = half_lanes(q_ref[cols, :] * BF16(SCALE))
            for ki in range(tiles):
                if slot == 0 and ki > qi:
                    continue

                @pl.when(tile_needed(meta_ref, slot, qi, ki, rows))
                def _(qi=qi, ki=ki, cols=cols, q_one=q_one, q_two=q_two):
                    at = slice(ki * tile, (ki + 1) * tile)
                    keys = k_ref[at, :]
                    k_one, k_two = half_lanes(keys * BF16(SCALE))
                    grads = grad_ref[:, cols]
                    ok = score_mask(meta_ref, slot, qi, ki, rows, low_ref[0:1, cols])
                    inner = dot(v_ref[at, :], grads, 1, 0)
                    one = jnp.exp(jnp.where(ok, dot(keys, q_one, 1, 1), MASKED) - stat_ref[0:1, cols])
                    two = lam_value * jnp.exp(
                        jnp.where(ok, dot(keys, q_two, 1, 1), MASKED) - stat_ref[1:2, cols]
                    )
                    dv_acc[at, :] += dot((one - two).astype(BF16), grads, 1, 1)
                    d_one = (one * (inner - stat_ref[2:3, cols])).astype(BF16)
                    d_two = (two * (stat_ref[3:4, cols] - inner)).astype(BF16)
                    dk_acc[at, :] += dot(d_one, q_one, 1, 0) + dot(d_two, q_two, 1, 0)
                    dq_ref[cols, :] += dot(d_one, k_one, 0, 0) + dot(d_two, k_two, 0, 0)

        dkv_ref[:, :VD] = dk_acc[...].astype(BF16)
        dkv_ref[:, VD:] = dv_acc[...].astype(BF16)

    col = pl.BlockSpec((rows, VD), lambda h: (0, h))
    ins = [meta, lam, q, kv, kv, low, grad, stats]
    in_specs = [
        whole(pltpu.SMEM),
        whole(pltpu.SMEM),
        col,
        pl.BlockSpec((rows, VD), lambda h: (0, 2 * h)),
        pl.BlockSpec((rows, VD), lambda h: (0, 2 * h + 1)),
        fixed(low.shape),
        pl.BlockSpec((VD, rows), lambda h: (h, 0)),
        pl.BlockSpec((8, rows), lambda h: (h, 0)),
    ]
    if dq is not None:
        ins.append(dq)
        in_specs.append(col)
    return call(
        body,
        [shape((rows, heads * VD), F32), shape((rows, heads * 2 * VD), BF16)],
        ins,
        grid=(heads,),
        in_specs=in_specs,
        out_specs=[col, pl.BlockSpec((rows, 2 * VD), lambda h: (0, h))],
        scratch=[pltpu.VMEM((rows, VD), F32), pltpu.VMEM((rows, VD), F32)],
        name=f"attend_back_{slot}",
        flops=2 * heads * rows * rows * (4 * HALF + 2 * VD + 4 * HALF),
    )


def middle_kernel(x, heads_out, mine, theirs, gain, spot):
    rows, wide = x.shape
    half = wide // 2
    count = len(heads_out)
    cols = heads_out[0].shape[1]
    tile = 256

    def body(spot_ref, x_ref, gain_ref, *refs):
        ho, wm, wt = refs[:count], refs[count : 2 * count], refs[2 * count]
        resid_ref, normed_ref, inv_ref = refs[2 * count + 1 :]
        wt = [wt.at[k * half : (k + 1) * half, :] for k in range(count)]
        total = jnp.zeros((tile, 1), F32)
        for side, weights in ((0, wm), (1, wt)):
            at = pl.ds(pl.multiple_of((spot_ref[1] ^ side) * half, 128), half)
            value = x_ref[:, at].astype(F32)
            for k in range(count):
                value = value + dot(ho[k][...], weights[k][...], 1, 1)
            resid_ref[:, at] = value
            total = total + jnp.sum(value * value, axis=1, keepdims=True)
        inv = lax.rsqrt(total / wide + EPSILON)
        inv_ref[...] = inv
        normed_ref[...] = (resid_ref[...] * inv * gain_ref[...]).astype(BF16)

    def tall(width):
        return pl.BlockSpec((tile, width), lambda i: (i, 0))

    return call(
        body,
        [shape((rows, wide), F32), shape((rows, wide), BF16), shape((rows, 1), F32)],
        [spot, x, gain] + heads_out + mine + [theirs],
        grid=(rows // tile,),
        in_specs=[whole(pltpu.SMEM), tall(wide), fixed(gain.shape)]
        + [tall(cols)] * count
        + [fixed(mine[0].shape)] * count
        + [fixed(theirs.shape)],
        out_specs=[tall(wide), tall(wide), tall(1)],
        name="middle",
        flops=2 * rows * wide * cols * count,
    )


def gate_kernel(x, weight, first, cols):
    rows, wide = x.shape
    tile = 512 if cols % 512 == 0 and first % 512 == 0 else 256

    def body(x_ref, weight_ref, out_ref):
        out_ref[...] = dot(x_ref[...], weight_ref[...], 1, 0).astype(BF16)

    return call(
        body,
        [shape((rows, cols), BF16)],
        [x, weight],
        grid=(cols // tile,),
        in_specs=[fixed(x.shape), pl.BlockSpec((wide, tile), lambda i: (0, first // tile + i))],
        out_specs=[pl.BlockSpec((rows, tile), lambda i: (0, i))],
        name="gate",
    )[0]


def up_kernel(x, weight, first, gate):
    rows, wide = x.shape
    cols = gate.shape[1]
    tile = 512 if cols % 512 == 0 and first % 512 == 0 else 256

    def body(x_ref, weight_ref, gate_ref, up_ref, hidden_ref):
        up = dot(x_ref[...], weight_ref[...], 1, 0)
        up_ref[...] = up.astype(BF16)
        gate = gate_ref[...].astype(F32)
        hidden_ref[...] = (gate * jax.nn.sigmoid(gate) * up).astype(BF16)

    strip = pl.BlockSpec((rows, tile), lambda i: (0, i))
    return call(
        body,
        [shape((rows, cols), BF16), shape((rows, cols), BF16)],
        [x, weight, gate],
        grid=(cols // tile,),
        in_specs=[fixed(x.shape), pl.BlockSpec((wide, tile), lambda i: (0, first // tile + i)), strip],
        out_specs=[strip, strip],
        name="up",
    )


def gate_back_kernel(dy, weight, first, gate, up):
    rows, wide = dy.shape
    cols = gate.shape[1]
    tile = 512 if cols % 512 == 0 and first % 512 == 0 else 256

    def body(dy_ref, weight_ref, gate_ref, up_ref, dgate_ref, dup_ref):
        grad = dot(dy_ref[...], weight_ref[...], 1, 0)
        gate = gate_ref[...].astype(F32)
        sig = jax.nn.sigmoid(gate)
        dgate_ref[...] = (grad * up_ref[...].astype(F32) * sig * (1.0 + gate * (1.0 - sig))).astype(BF16)
        dup_ref[...] = (grad * gate * sig).astype(BF16)

    strip = pl.BlockSpec((rows, tile), lambda i: (0, i))
    return call(
        body,
        [shape((rows, cols), BF16), shape((rows, cols), BF16)],
        [dy, weight, gate, up],
        grid=(cols // tile,),
        in_specs=[
            fixed(dy.shape),
            pl.BlockSpec((wide, tile), lambda i: (0, first // tile + i)),
            strip,
            strip,
        ],
        out_specs=[strip, strip],
        name="gate_back",
    )


def quarters_kernel(terms, spot, count, name, norm=None):
    rows = terms[0][0].shape[0]
    wide = terms[0][1].shape[0]
    cols = wide // count
    n = len(terms)

    def body(spot_ref, *refs):
        lefts, weights = refs[:n], refs[n : 2 * n]
        rest = refs[2 * n :]
        if norm is not None:
            x_ref, inv_ref, gain_ref = rest[:3]
            rest = rest[3:]
            row_ref, col_ref = rest[count:]
        outs = rest[:count]
        pos = pl.program_id(0)
        value = dot(lefts[0][...], weights[0][...], 1, 1)
        for i in range(1, n):
            value = value + dot(lefts[i][...], weights[i][...], 1, 1)
        if norm is not None:
            weighed = value * (x_ref[...].astype(F32) * inv_ref[...])
            col_ref[...] = jnp.sum(weighed, axis=0, keepdims=True)
            row_sum = jnp.sum(weighed * gain_ref[...], axis=1, keepdims=True)

            @pl.when(pos == 0)
            def _():
                row_ref[...] = row_sum

            @pl.when(pos > 0)
            def _():
                row_ref[...] += row_sum

        value = value.astype(BF16)
        for k in range(count):

            @pl.when(spot_ref[0] ^ k == pos)
            def _(k=k):
                outs[k][...] = value

    ins = [spot] + [t[0] for t in terms] + [t[1] for t in terms]
    in_specs = [whole(pltpu.SMEM)] + [fixed(t[0].shape) for t in terms]
    for left, _, first in terms:
        width = left.shape[1]
        in_specs.append(pl.BlockSpec((cols, width), lambda i, at=first // width: (i, at)))
    outs = [shape((rows, cols), BF16)] * count
    out_specs = [fixed((rows, cols))] * count
    if norm is not None:
        ins += list(norm)
        in_specs += [
            pl.BlockSpec((rows, cols), lambda i: (0, i)),
            fixed((rows, 1)),
            pl.BlockSpec((1, cols), lambda i: (0, i)),
        ]
        outs = outs + [shape((rows, 1), F32), shape((1, wide), F32)]
        out_specs = out_specs + [fixed((rows, 1)), pl.BlockSpec((1, cols), lambda i: (0, i))]
    return call(body, outs, ins, grid=(count,), in_specs=in_specs, out_specs=out_specs, name=name)


def mid_back_kernel(dgate, dup, gate_w, gate_first, up_w, up_first, head_at, count):
    rows, cols = dgate.shape
    wide = gate_w.shape[0]
    tile = 384
    steps = wide // tile
    part = rows // count

    def body(at_ref, dgate_ref, dup_ref, g_ref, u_ref, *refs):
        outs = refs[:count]
        value = dot(dgate_ref[...], g_ref[...], 1, 1) + dot(dup_ref[...], u_ref[...], 1, 1)
        value = value.astype(BF16)
        for row in range(count):
            rows_of = value[row * part : (row + 1) * part, :]
            for k in range(count):

                @pl.when(at_ref[0] ^ k == row)
                def _(k=k, rows_of=rows_of):
                    outs[k][...] = rows_of

    return call(
        body,
        [shape((part, wide), BF16)] * count,
        [head_at, dgate, dup, gate_w, up_w],
        grid=(steps,),
        in_specs=[
            whole(pltpu.SMEM),
            fixed(dgate.shape),
            fixed(dup.shape),
            pl.BlockSpec((tile, cols), lambda i: (i, gate_first // cols)),
            pl.BlockSpec((tile, cols), lambda i: (i, up_first // cols)),
        ],
        out_specs=[pl.BlockSpec((part, tile), lambda i: (0, i))] * count,
        name="mid_back",
    )


def norm_mid_back_kernel(parts, resid, inv, gain, dy, spot):
    part, wide = parts[0].shape
    count = len(parts)

    def body(spot_ref, gain_ref, resid_ref, inv_ref, dy_ref, *refs):
        ins, (out_ref, col_ref) = refs[:count], refs[count:]
        grad = ins[0][...].astype(F32)
        for ref in ins[1:]:
            grad = grad + ref[...].astype(F32)
        inv_rows = inv_ref[...]
        unit = resid_ref[...] * inv_rows
        col_ref[...] = jnp.sum(grad * unit, axis=0, keepdims=True)
        e = grad * gain_ref[...]
        mean = jnp.sum(e * unit, axis=1, keepdims=True) / wide
        out_ref[...] = (dy_ref[...].astype(F32) + inv_rows * (e - unit * mean)).astype(BF16)

    def mine(width):
        return pl.BlockSpec((part, width), lambda i, spot_ref: (spot_ref[0], 0))

    def all_of(dims):
        return pl.BlockSpec(tuple(dims), lambda i, spot_ref: (0, 0))

    return pl.pallas_call(
        body,
        out_shape=[shape((part, wide), BF16), shape((1, wide), F32)],
        grid_spec=pltpu.PrefetchScalarGridSpec(
            num_scalar_prefetch=1,
            grid=(1,),
            in_specs=[all_of(gain.shape), mine(wide), mine(1), mine(wide)] + [all_of((part, wide))] * count,
            out_specs=[all_of((part, wide)), all_of((1, wide))],
        ),
        compiler_params=pltpu.CompilerParams(vmem_limit_bytes=VMEM_LIMIT),
        cost_estimate=pl.CostEstimate(flops=1, bytes_accessed=1, transcendentals=0),
        name="norm_mid_back",
    )(spot, gain, resid, inv, dy, *parts)


def head_back_kernel(branch, weight, first, cols, unit, two, fin, gain, lam):
    rows, wide = branch.shape
    heads = cols // VD

    def body(lam_ref, b_ref, weight_ref, unit_ref, two_ref, fin_ref, gain_ref, g_ref, stat_ref, sum_ref):
        grad = jnp.transpose(dot(b_ref[...], weight_ref[...], 1, 0))
        unit = unit_ref[...]
        out_two = two_ref[...]
        inv = fin_ref[2:3, :]
        f = grad * gain_ref[...] * KEEP
        mean = jnp.mean(f * unit, axis=0, keepdims=True)
        mixed_grad = inv * (f - unit * mean)
        g = mixed_grad.astype(BF16)
        g_ref[...] = g
        g = g.astype(F32)
        delta_two = jnp.sum(g * out_two, axis=0, keepdims=True)
        mixed = unit / inv
        stat_ref[0:2, :] = fin_ref[0:2, :]
        stat_ref[2:3, :] = jnp.sum(g * mixed, axis=0, keepdims=True) + lam_ref[0, 0] * delta_two
        stat_ref[3:4, :] = delta_two
        stat_ref[4:8, :] = jnp.zeros((4, rows), F32)
        gain_term = jnp.sum(grad * unit, axis=1, keepdims=True) * KEEP
        lam_term = -jnp.sum(mixed_grad * out_two, axis=1, keepdims=True)
        lanes = lax.broadcasted_iota(jnp.int32, (VD, 128), 1)
        sum_ref[...] = jnp.where(lanes == 0, gain_term, jnp.where(lanes == 1, lam_term, 0.0))

    row_spec = pl.BlockSpec((VD, rows), lambda h: (h, 0))
    stat_spec = pl.BlockSpec((8, rows), lambda h: (h, 0))
    slab = pl.BlockSpec((wide, VD), lambda h: (0, first // VD + h))
    return call(
        body,
        [shape((cols, rows), BF16), shape((heads * 8, rows), F32), shape((heads * VD, 128), F32)],
        [lam, branch, weight, unit, two, fin, gain],
        grid=(heads,),
        in_specs=[
            whole(pltpu.SMEM),
            fixed(branch.shape),
            slab,
            row_spec,
            row_spec,
            stat_spec,
            fixed(gain.shape),
        ],
        out_specs=[row_spec, stat_spec, pl.BlockSpec((VD, 128), lambda h: (h, 0))],
        name="head_back",
        flops=2 * rows * wide * cols,
    )


def turn_back_kernel(value, extra, cosine, sine, step, name):
    rows, cols = value.shape
    tile = 256
    with_extra = extra is not None

    def body(v_ref, *refs):
        v = v_ref[...].astype(F32)
        if with_extra:
            v = v + refs[0][...].astype(F32)
        cos_ref, sin_ref, out_ref = refs[-3:]
        for at in range(0, cols, 128):
            part = v[:, at : at + 128]
            if at % step == 0:
                part = turn(part, cos_ref[...], sin_ref[...], -1.0)
            out_ref[:, at : at + 128] = part.astype(BF16)

    def tall(width):
        return pl.BlockSpec((tile, width), lambda i: (i, 0))

    ins = [value] + ([extra] if with_extra else []) + [cosine, sine]
    return call(
        body,
        [shape((rows, cols), BF16)],
        ins,
        grid=(rows // tile,),
        in_specs=[tall(cols)] * (len(ins) - 2) + [tall(128), tall(128)],
        out_specs=[tall(cols)],
        name=name,
    )[0]


def outer_kernel(pairs, side, got, name):
    rows = pairs[0][0].shape[0]
    half = pairs[0][0].shape[1] // 2
    widths = [right.shape[1] for _, right in pairs]
    tile = 512 if all(w % 512 == 0 for w in widths) else 384
    steps = [w // tile for w in widths]
    starts = [sum(steps[:i]) for i in range(len(steps))]
    n = len(pairs)
    lefts = []
    for left, _ in pairs:
        if not any(left is other for other in lefts):
            lefts.append(left)
    left_of = [next(i for i, other in enumerate(lefts) if other is left) for left, _ in pairs]
    with_got = got is not None

    def body(side_ref, *refs):
        left_refs, right_refs = refs[: len(lefts)], refs[len(lefts) : len(lefts) + n]
        out_ref, turned = refs[-2:]
        step = pl.program_id(0)
        for i in range(n):
            if i == 0 or left_of[i] != left_of[i - 1]:

                @pl.when(step == starts[i])
                def _(i=i):
                    turned[...] = jnp.transpose(left_refs[left_of[i]][...])

            @pl.when(jnp.logical_and(step >= starts[i], step < starts[i] + steps[i]))
            def _(i=i):
                value = dot(turned[...], right_refs[i][...], 1, 0)
                if with_got:
                    value = value + refs[-3][...].astype(F32)
                out_ref[...] = value.astype(BF16)

    def right_spec(i):
        return pl.BlockSpec((rows, tile), lambda j, side_ref: (0, jnp.clip(j - starts[i], 0, steps[i] - 1)))

    strip = pl.BlockSpec((half, tile), lambda j, side_ref: (0, j))
    return pl.pallas_call(
        body,
        out_shape=shape((half, sum(widths)), BF16),
        grid_spec=pltpu.PrefetchScalarGridSpec(
            num_scalar_prefetch=1,
            grid=(sum(steps),),
            in_specs=[pl.BlockSpec((rows, half), lambda j, side_ref: (0, side_ref[0]))] * len(lefts)
            + [right_spec(i) for i in range(n)]
            + ([strip] if with_got else []),
            out_specs=strip,
            scratch_shapes=[pltpu.VMEM((half, rows), BF16)],
        ),
        compiler_params=pltpu.CompilerParams(vmem_limit_bytes=VMEM_LIMIT),
        cost_estimate=pl.CostEstimate(flops=1, bytes_accessed=1, transcendentals=0),
        name=name,
    )(side, *lefts, *[right for _, right in pairs], *([got] if with_got else []))


def per_device(
    tokens,
    segment_ids,
    gain_attn,
    w_query,
    w_key,
    w_value,
    w_output,
    lambda_vec,
    gain_heads,
    gain_ffn,
    w_gate,
    w_up,
    w_down,
    grad_out,
):
    rows, slice_width = tokens.shape
    n_ctx = lax.axis_size("ctx")
    n_head = lax.axis_size("head")
    place = lax.axis_index("ctx")
    head = lax.axis_index("head")
    core = lax.axis_index("dp")
    group = segment_ids.shape[0]
    wide = slice_width * n_head
    cols = w_query.shape[1]
    heads = cols // VD
    spot = jnp.stack([head, core]).astype(jnp.int32)
    my_side = jnp.reshape(core, (1,)).astype(jnp.int32)
    other_side = 1 - my_side
    reach = n_ctx
    if n_ctx == 4 and group == 3072 and rows == 768:
        reach = n_ctx - 1

    pieces = []
    for h in range(heads):
        pieces += [w_key[:, h * VD : (h + 1) * VD], w_value[:, h * VD : (h + 1) * VD]]
    kv_w = gather_rows(jnp.concatenate(pieces, axis=1))
    x_units = head_gather(tokens)
    hidden_cols = w_gate.shape[1]
    qo_w = gather_rows(jnp.concatenate([w_query, w_output.T], axis=1))
    g_w = gather_rows(w_gate)
    ud_w = gather_rows(jnp.concatenate([w_up, w_down.T], axis=1))

    first_row = place * rows
    row_index = first_row + jnp.arange(rows, dtype=jnp.int32)
    my_seg = lax.dynamic_slice_in_dim(segment_ids, first_row, rows, 0)
    before = jnp.sum((segment_ids[None, :] < my_seg[:, None]).astype(jnp.int32), axis=1)
    lane = jnp.arange(128, dtype=jnp.int32)
    frequency = ROPE_BASE ** (-((lane % (HALF // 2)).astype(F32) * 2.0 / HALF))
    angles = (row_index - before).astype(F32)[:, None] * frequency[None, :]
    cosine = jnp.cos(angles)
    sine = jnp.sin(angles) * jnp.where(lane % HALF < HALF // 2, -1.0, 1.0)[None, :]
    low = jnp.broadcast_to(before[None, :], (8, rows))
    meta = jnp.concatenate([jnp.reshape(place, (1,)), before[::ATTN_TILE]]).astype(jnp.int32)
    exp_one = jnp.exp(jnp.sum(lambda_vec[0] * lambda_vec[1]))
    exp_two = jnp.exp(jnp.sum(lambda_vec[2] * lambda_vec[3]))
    lam = jnp.reshape(exp_one - exp_two + LAMBDA_START, (1, 1))

    gain_in = gain_attn[None, :]
    gain_mid = gain_ffn[None, :]

    x_full, normed_in, inv_in, kv = norm_project_kernel(x_units, gain_in, spot, kv_w, cosine, sine)
    forward_pairs = [(i, i + 1) for i in range(n_ctx - 1)]
    kv_slots = [kv]
    kv_slots.append(lax.ppermute(kv, "ctx", forward_pairs))
    queries = query_kernel(normed_in, qo_w, cols, cosine, sine)
    o_half = lax.dynamic_slice(qo_w, (core * (wide // 2), cols), (wide // 2, cols))
    o_units = head_gather(after(o_half, queries))

    def attend(slot, state, kv_slot):
        return attend_kernel(
            slot, slot == 0, slot == reach - 1, meta, lam, queries, kv_slot, low, gain_heads[None, :], state
        )

    state = attend(0, None, kv)
    for slot in range(1, reach):
        here = after(kv_slots[slot], state[1])
        if slot + 1 < reach:
            kv_slots.append(lax.ppermute(here, "ctx", forward_pairs[slot:]))
        state = attend(slot, state, here)
    head_out, unit_head, out_two, finish = state
    ho_units = head_gather(head_out)
    o_theirs = core_swap(jnp.concatenate([after(o_units[0], head_out)] + o_units[1:], axis=0))
    dy_units = head_gather(after(grad_out, o_theirs))
    resid, normed_mid, inv_mid = middle_kernel(x_full, ho_units, o_units, o_theirs, gain_mid, spot)
    gate = gate_kernel(normed_mid, g_w, 0, hidden_cols)
    up, hidden = up_kernel(normed_mid, ud_w, 0, gate)
    dy = place_cols_kernel(dy_units, after(spot, hidden))
    dgate, dup = gate_back_kernel(dy, ud_w, hidden_cols, gate, up)
    mid_parts = mid_back_kernel(dgate, dup, g_w, 0, ud_w, 0, spot, n_head)
    mid_got = [head_move(mid_parts[k], k) for k in range(1, n_head)]

    ffn_pairs = [(dy, hidden), (normed_mid, dgate), (normed_mid, dup)]
    ffn_theirs = outer_kernel(ffn_pairs, after(other_side, mid_parts[0]), None, "ffn_grads_theirs")
    ffn_got = core_swap(ffn_theirs)
    y_parts = quarters_kernel([(hidden, ud_w, hidden_cols)], after(spot, ffn_theirs), n_head, "down")
    ffn_sums = outer_kernel(ffn_pairs, after(my_side, y_parts[0]), ffn_got, "ffn_grads")
    ffn_total = scatter_rows(ffn_sums)
    mid_got[0] = after(mid_got[0], ffn_sums)
    branch_rows, ffn_gain_term = norm_mid_back_kernel(
        [mid_parts[0]] + mid_got, resid, inv_mid, gain_mid, dy, spot
    )
    branch_units = head_gather(branch_rows)
    branch = place_rows(
        branch_units, jnp.stack([head ^ k for k in range(n_head)]).astype(jnp.int32), n_head
    )
    y_got = [head_move(after(y_parts[k], branch), k) for k in range(1, n_head)]

    grads, stats, head_sums = head_back_kernel(
        branch, qo_w, cols, cols, unit_head, out_two, finish, gain_heads[:, None], lam
    )
    dq = None
    dkv_got = None
    for slot in reversed(range(reach)):
        dq, dkv = attend_back_kernel(slot, meta, lam, queries, kv_slots[slot], low, grads, stats, dq)
        if slot:
            if dkv_got is not None:
                dkv = (after(dkv, dq).astype(F32) + dkv_got.astype(F32)).astype(BF16)
            dkv_got = lax.ppermute(dkv, "ctx", [(i, i - 1) for i in range(slot, n_ctx)])

    my_cols = head * slice_width
    output = lax.dynamic_slice_in_dim(resid, my_cols, slice_width, 1) + after(y_parts[0], dq).astype(F32)
    for got in y_got:
        output = output + got.astype(F32)
    output = output.astype(BF16)
    dq_pre = turn_back_kernel(after(dq, output), None, cosine, sine, VD, "query_back")
    oq_pairs = [(branch, head_out), (normed_in, dq_pre)]
    oq_theirs = outer_kernel(oq_pairs, other_side, None, "oq_grads_theirs")
    oq_got = core_swap(oq_theirs)
    oq_sums = outer_kernel(oq_pairs, after(my_side, oq_theirs), oq_got, "oq_grads")
    oq_total = scatter_rows(after(oq_sums, ffn_total))

    dkv_pre = turn_back_kernel(after(dkv, oq_sums), dkv_got, cosine, sine, 2 * VD, "key_back")
    kv_pairs = [(normed_in, dkv_pre)]
    kv_theirs = outer_kernel(kv_pairs, other_side, None, "kv_grads_theirs")
    kv_got = core_swap(kv_theirs)
    in_parts = quarters_kernel(
        [(dq_pre, qo_w, 0), (dkv_pre, kv_w, 0)],
        after(spot, kv_theirs),
        n_head,
        "in_back",
        norm=(x_full, inv_in, gain_in),
    )
    in_got = [head_move(in_parts[k], k) for k in range(1, n_head)]
    kv_sums = outer_kernel(kv_pairs, after(my_side, in_parts[0]), kv_got, "kv_grads")
    kv_total = scatter_rows(after(kv_sums, oq_total))
    row_sums, attn_gain_term = in_parts[n_head:]
    row_sums = head_sum(row_sums.reshape(rows // 128, 128)).reshape(rows, 1)
    grad_in = in_parts[0].astype(F32)
    for got in in_got:
        grad_in = grad_in + got.astype(F32)
    my_gain = lax.dynamic_slice_in_dim(gain_in, my_cols, slice_width, 1)
    my_branch = lax.dynamic_slice_in_dim(branch, my_cols, slice_width, 1).astype(F32)
    unit_in = tokens.astype(F32) * inv_in
    grad_tokens = my_branch + inv_in * (grad_in * my_gain - unit_in * (row_sums / wide))

    head_sums = jnp.sum(head_sums.reshape(heads, VD, 128), axis=0)
    small = jnp.concatenate(
        [
            attn_gain_term[0],
            ffn_gain_term[0],
            head_sums[:, 0],
            jnp.full((128,), jnp.sum(head_sums[:, 1]), F32),
        ]
    ).reshape(-1, 128)
    small = all_sum(small).reshape(-1)
    attn_gain_grad = small[:wide]
    ffn_gain_grad = small[wide : 2 * wide]
    heads_gain_grad = small[2 * wide : 2 * wide + VD]
    lambda_scalar = small[2 * wide + VD]
    grad_lambda = jnp.stack(
        [
            lambda_scalar * exp_one * lambda_vec[1],
            lambda_scalar * exp_one * lambda_vec[0],
            -lambda_scalar * exp_two * lambda_vec[3],
            -lambda_scalar * exp_two * lambda_vec[2],
        ],
        axis=0,
    )
    grad_kv = kv_total.astype(F32)
    grad_key = jnp.concatenate([grad_kv[:, 2 * h * VD : (2 * h + 1) * VD] for h in range(heads)], axis=1)
    grad_value = jnp.concatenate(
        [grad_kv[:, (2 * h + 1) * VD : (2 * h + 2) * VD] for h in range(heads)], axis=1
    )
    return (
        output,
        grad_tokens,
        attn_gain_grad,
        oq_total[:, cols:].astype(F32),
        grad_key,
        grad_value,
        oq_total[:, :cols].astype(F32).T,
        grad_lambda,
        heads_gain_grad,
        ffn_gain_grad,
        ffn_total[:, hidden_cols : 2 * hidden_cols].astype(F32),
        ffn_total[:, 2 * hidden_cols :].astype(F32),
        ffn_total[:, :hidden_cols].astype(F32).T,
    )


def solution(mesh):
    split = P(("dp", "ctx"), "head")
    turned = P("head", ("dp", "ctx"))
    in_specs = (
        split,
        P("dp"),
        P(),
        split,
        split,
        split,
        turned,
        P(),
        P(),
        P(),
        split,
        split,
        turned,
        split,
    )
    out_specs = (
        split,
        split,
        P(),
        split,
        split,
        split,
        turned,
        P(),
        P(),
        P(),
        split,
        split,
        turned,
    )
    return jax.shard_map(
        per_device, mesh=mesh, in_specs=in_specs, out_specs=out_specs, check_vma=False
    )
```

time: 1390 us -> 558 us (0.40)
  waiting for transfers between devices: 1010 us -> 236 us
  Pallas kernels: 0 us -> 203 us
  matrix products: 179 us -> 0 us
  starting transfers between devices: 1.57 us -> 44.2 us
  other arithmetic: 67.5 us -> 25.5 us
  blocking collectives: 40.4 us -> 0 us
  local copies, waits for them, and re-layouts: 59.1 us -> 23.6 us
    all_gather x13 -> x4, waiting for transfers between devices: 402 us -> 31.9 us  [gather_rows(): return lax.all_gather(unit, ('dp', 'ctx'), axis=0, tiled=True)]
    reduce_scatter x9 -> x3, waiting for transfers between devices: 366 us -> 0.02 us  [scatter_rows(): return lax.psum_scatter(sums, 'ctx', scatter_dimension=0, tiled=True)]
    ppermute x0 -> x39, waiting for transfers between devices: none -> 204 us  [the longest x28 116 us: head_move(): return lax.ppermute(value, 'head', xor_pairs(lax.axis_size('head'), step))]
    pallas_call x0 -> x27, Pallas kernels: none -> 203 us  [the longest x20 158 us: call(): pl.pallas_call(body, out_shape=list(outs), in_specs=in_specs, out_specs=o...]
    dot_general x63 -> x0, matrix products: 179 us -> none  [the longest x7 33.1 us: times_rows(): jnp.einsum('tb,ab->ta', left, weight, preferred_element_type=jnp.float32)]
    psum x2 -> x0, waiting for transfers between devices: 150 us -> none  [the longest x1 76.3 us: per_device(): lax.psum((times_rows(grad_query_pre, wq) + times_rows(grad_key_pre, wk) +...]
    unnamed x28 -> x7, waiting for transfers between devices: 89.7 us -> 0.78 us
    ppermute x0 -> x39, starting transfers between devices: none -> 43.6 us  [the longest x28 32.7 us: head_move(): return lax.ppermute(value, 'head', xor_pairs(lax.axis_size('head'), step))]
  transfers between devices with their start and end apart: 26 -> 46, of which waited for: 24 -> 22; matrix products, arithmetic and copies ran while one was open for 14% -> 6% of each run, Pallas kernels for 0% -> 29%
where the time goes in v1:
time: 558 us; the launch traced here: 550 us
  waiting for transfers between devices  236 us (42%)
  Pallas kernels  203 us (36%)
  starting transfers between devices  44.2 us (8%)
  other arithmetic  25.5 us (5%)
  local copies, waits for them, and re-layouts  23.6 us (4%)
  between operations  17.6 us (3%)
    pallas_call x20, Pallas kernels, call(): pl.pallas_call(body, out_shape=list(outs), in_specs=in_specs, out_specs=o...  158 us
    ppermute x28, waiting for transfers between devices, head_move(): return lax.ppermute(value, 'head', xor_pairs(lax.axis_size('head'), step))  116 us
    ppermute x2, waiting for transfers between devices, per_device(): dkv_got = lax.ppermute(dkv, 'ctx', [(i, i - 1) for i in range(slot, n_ctx)])  45 us
    ppermute x1, waiting for transfers between devices, per_device(): kv_slots.append(lax.ppermute(here, 'ctx', forward_pairs[slot:]))  40.1 us
    pallas_call x6, Pallas kernels, outer_kernel(): pl.pallas_call(body, out_shape=shape((half, sum(widths)), BF16), grid_spe...  39.8 us
    ppermute x28, starting transfers between devices, head_move(): return lax.ppermute(value, 'head', xor_pairs(lax.axis_size('head'), step))  32.7 us
    all_gather x4, waiting for transfers between devices, gather_rows(): return lax.all_gather(unit, ('dp', 'ctx'), axis=0, tiled=True)  31.9 us
    unnamed x95, local copies, waits for them, and re-layouts  15 us
  transfers between devices with their start and end apart: 46, of which 22 were waited for; matrix products, arithmetic and copies ran while one was open for 6% of the time, Pallas kernels for 29%

profile of v1, /device:TPU:16, one launch (start us, length us, event | category | flops | bytes accessed | tf_op | source)
XLA Modules:
  0.0 550.0 jit_solution(3404863579575953690)
XLA Ops:
  25.2 7.8 %collective-permute-done.refs_1_ = bf16[768,384]{1,0:T(8,128)(2,1)S(1)} collective-permute-done((bf16[768,384]{1,0:T(8,128)(2,1)S(1)}, bf16[768,384]{1,0:T(8,128)(2,1)S(1)}, u32[]{:S(2)}, u32[]{:S(2)}) %collective-permute-start) | collective-permute-done | bytes 589856 | tf_op jit(solution)/shard_map/ppermute | solution.py:74
  33.0 12.7 %collective-permute-done.1.refs_2_ = bf16[768,384]{1,0:T(8,128)(2,1)S(1)} collective-permute-done((bf16[768,384]{1,0:T(8,128)(2,1)S(1)}, bf16[768,384]{1,0:T(8,128)(2,1)S(1)}, u32[]{:S(2)}, u32[]{:S(2)}) %collective-permute-start.1) | collective-permute-done | bytes 589856 | tf_op jit(solution)/shard_map/ppermute | solution.py:74
  46.7 7.4 %norm_project.1 = (bf16[768,1536]{1,0:T(8,128)(2,1)}, bf16[768,1536]{1,0:T(8,128)(2,1)}, f32[768,1]{1,0:T(8,128)}, bf16[768,768]{1,0:T(8,128)(2,1)}) custom-call(s32[2]{0:T(128)} %pad_add_fusion.spot_ref.at_ref, f32[1,1536]{1,0:T(1,128)} %broadcast_in_dim.36.gain_ref.refs_6_, bf16[1536,768]{1,0:T(8,128)(2,1)} %all-gather.5.cloned.1.call-done.weight_ref.refs_3_, ...), custom_call_target="tpu_custom_call" | custom-call | flops 1 | bytes 1 | tf_op jit(solution)/shard_map/norm_project/pallas_call | solution.py:50
  60.3 31.9 %all-gather.7.cloned.1.call-done.weight_ref.refs_2_ = bf16[1536,768]{1,0:T(8,128)(2,1)} async-done(((bf16[192,768]{1,0:T(8,128)(2,1)}), bf16[1536,768]{1,0:T(8,128)(2,1)}) %all-gather.7.cloned.1.call-update) | async-done | bytes 2359312 | tf_op jit(solution)/shard_map/all_gather | solution.py:104
  98.0 15.4 %attend_0.1 = (f32[768,768]{1,0:T(8,128)}, f32[24,768]{1,0:T(8,128)}) custom-call(s32[4]{0:T(128)} %pad_add_fusion.1.meta_ref, f32[1,1]{1,0:T(1,128)} %bitcast.3.lam_ref, bf16[768,384]{1,0:T(8,128)(2,1)} %queries.1.q_ref, bf16[768,768]{1,0:T(8,128)(2,1)} %get-tuple-element.81.k_ref.v_ref, bf16[768,768]{1,0:T(8,128)(2,1)} %get-tuple-element.81.k_ref.v_ref, ...), custom_call_target="tpu_custom_call" | custom-call | flops 1 | bytes 1 | tf_op jit(solution)/shard_map/attend_0/pallas_call | solution.py:50
  120.8 9.6 %attend_1.1 = (f32[768,768]{1,0:T(8,128)}, f32[24,768]{1,0:T(8,128)}) custom-call(s32[4]{0:T(128)} %pad_add_fusion.1.meta_ref, f32[1,1]{1,0:T(1,128)} %bitcast.3.lam_ref, bf16[768,384]{1,0:T(8,128)(2,1)} %queries.1.q_ref, bf16[768,768]{1,0:T(8,128)(2,1)} %copy-done, bf16[768,768]{1,0:T(8,128)(2,1)} %copy-done, s32[8,768]{1,0:T(8,128)} %broadcast_in_dim.40.low_ref, ...), custom_call_target="tpu_custom_call" | custom-call | flops 1 | bytes 1 | tf_op jit(solution)/shard_map/attend_1/pallas_call | solution.py:50
  130.4 40.1 %collective-permute-done.4.k_ref.v_ref = bf16[768,768]{1,0:T(8,128)(2,1)S(1)} collective-permute-done((bf16[768,768]{1,0:T(8,128)(2,1)S(1)}, bf16[768,768]{1,0:T(8,128)(2,1)S(1)}, u32[]{:S(2)}, u32[]{:S(2)}) %collective-permute-start.4) | collective-permute-done | bytes 1179680 | tf_op jit(solution)/shard_map/ppermute | solution.py:876
  171.5 10.2 %attend_2.1 = (bf16[768,384]{1,0:T(8,128)(2,1)}, f32[384,768]{1,0:T(8,128)}, f32[384,768]{1,0:T(8,128)}, f32[24,768]{1,0:T(8,128)}) custom-call(s32[4]{0:T(128)} %pad_add_fusion.1.meta_ref, f32[1,1]{1,0:T(1,128)} %bitcast.3.lam_ref, bf16[768,384]{1,0:T(8,128)(2,1)} %queries.1.q_ref, bf16[768,768]{1,0:T(8,128)(2,1)} %copy-done.1, bf16[768,768]{1,0:T(8,128)(2,1)} %copy-done.1, ...), custom_call_target="tpu_custom_call" | custom-call | flops 1 | bytes 1 | tf_op jit(solution)/shard_map/attend_2/pallas_call | solution.py:50
  194.6 8.7 %collective-permute-done.5.refs_1_ = bf16[768,384]{1,0:T(8,128)(2,1)S(1)} collective-permute-done((bf16[768,384]{1,0:T(8,128)(2,1)S(1)}, bf16[768,384]{1,0:T(8,128)(2,1)S(1)}, u32[]{:S(2)}, u32[]{:S(2)}) %collective-permute-start.5) | collective-permute-done | bytes 589856 | tf_op jit(solution)/shard_map/ppermute | solution.py:74
  206.3 11.3 %collective-permute-done.6.refs_2_ = bf16[768,384]{1,0:T(8,128)(2,1)S(1)} collective-permute-done((bf16[768,384]{1,0:T(8,128)(2,1)S(1)}, bf16[768,384]{1,0:T(8,128)(2,1)S(1)}, u32[]{:S(2)}, u32[]{:S(2)}) %collective-permute-start.6) | collective-permute-done | bytes 589856 | tf_op jit(solution)/shard_map/ppermute | solution.py:74
  219.2 10.8 %middle.1 = (f32[768,1536]{1,0:T(8,128)}, bf16[768,1536]{1,0:T(8,128)(2,1)}, f32[768,1]{1,0:T(8,128)}) custom-call(s32[2]{0:T(128)} %pad_add_fusion.spot_ref.at_ref, bf16[768,1536]{1,0:T(8,128)(2,1)} %get-tuple-element.79.x_ref.refs_4_, f32[1,1536]{1,0:T(1,128)} %broadcast_in_dim.39.gain_ref, bf16[768,384]{1,0:T(8,128)(2,1)} %get-tuple-element.88.refs_0_.refs_2_, ...), custom_call_target="tpu_custom_call" | custom-call | flops 1 | bytes 1 | tf_op jit(solution)/shard_map/middle/pallas_call | solution.py:50
  230.0 5.9 %gate.1.gate_ref = bf16[768,1024]{1,0:T(8,128)(2,1)} custom-call(bf16[768,1536]{1,0:T(8,128)(2,1)} %get-tuple-element.92.x_ref.refs_1_, bf16[1536,1024]{1,0:T(8,128)(2,1)} %all-gather.11.cloned.1.call-done.weight_ref.g_ref), custom_call_target="tpu_custom_call" | custom-call | flops 1 | bytes 1 | tf_op jit(solution)/shard_map/gate/pallas_call | solution.py:50
  235.9 6.6 %up.1 = (bf16[768,1024]{1,0:T(8,128)(2,1)}, bf16[768,1024]{1,0:T(8,128)(2,1)}) custom-call(bf16[768,1536]{1,0:T(8,128)(2,1)} %get-tuple-element.92.x_ref.refs_1_, bf16[1536,2048]{1,0:T(8,128)(2,1)} %all-gather.9.cloned.1.call-done.weight_ref.u_ref.refs_1_, bf16[768,1024]{1,0:T(8,128)(2,1)} %gate.1.gate_ref), custom_call_target="tpu_custom_call" | custom-call | flops 1 | bytes 1 | tf_op jit(solution)/shard_map/up/pallas_call | solution.py:50
  246.7 7.9 %gate_back.1 = (bf16[768,1024]{1,0:T(8,128)(2,1)}, bf16[768,1024]{1,0:T(8,128)(2,1)}) custom-call(bf16[768,1536]{1,0:T(8,128)(2,1)} %place_cols.1.dy_ref.refs_0_, bf16[1536,2048]{1,0:T(8,128)(2,1)} %all-gather.9.cloned.1.call-done.weight_ref.u_ref.refs_1_, bf16[768,1024]{1,0:T(8,128)(2,1)} %gate.1.gate_ref, bf16[768,1024]{1,0:T(8,128)(2,1)} %get-tuple-element.96.up_ref), custom_call_target="tpu_custom_call" | custom-call | flops 1 | bytes 1 | tf_op jit(solution)/shard_map/gate_back/pallas_call | solution.py:50
  254.6 11.3 %mid_back.1 = (bf16[192,1536]{1,0:T(8,128)(2,1)}, bf16[192,1536]{1,0:T(8,128)(2,1)}, bf16[192,1536]{1,0:T(8,128)(2,1)}, bf16[192,1536]{1,0:T(8,128)(2,1)}) custom-call(s32[2]{0:T(128)} %pad_add_fusion.spot_ref.at_ref, bf16[768,1024]{1,0:T(8,128)(2,1)} %get-tuple-element.97.dgate_ref.refs_3_, bf16[768,1024]{1,0:T(8,128)(2,1)} %get-tuple-element.98.dup_ref.refs_4_, ...), custom_call_target="tpu_custom_call" | custom-call | flops 1 | bytes 1 | tf_op jit(solution)/shard_map/mid_back/pallas_call | solution.py:50
  265.9 9.7 %ffn_grads_theirs.1 = bf16[768,3072]{1,0:T(8,128)(2,1)} custom-call(s32[1]{0:T(128)S(6)} %sub.18.side_ref, bf16[768,1536]{1,0:T(8,128)(2,1)} %place_cols.1.dy_ref.refs_0_, bf16[768,1536]{1,0:T(8,128)(2,1)} %get-tuple-element.92.x_ref.refs_1_, bf16[768,1024]{1,0:T(8,128)(2,1)} %get-tuple-element.93.refs_2_.refs_0_, ...), custom_call_target="tpu_custom_call" | custom-call | flops 1 | bytes 1 | tf_op jit(solution)/shard_map/ffn_grads_theirs/pallas_call | solution.py:780
  275.7 7.5 %down.1 = (bf16[768,384]{1,0:T(8,128)(2,1)}, bf16[768,384]{1,0:T(8,128)(2,1)}, bf16[768,384]{1,0:T(8,128)(2,1)}, bf16[768,384]{1,0:T(8,128)(2,1)}) custom-call(s32[2]{0:T(128)} %pad_add_fusion.spot_ref.at_ref, bf16[768,1024]{1,0:T(8,128)(2,1)} %get-tuple-element.93.refs_2_.refs_0_, bf16[1536,2048]{1,0:T(8,128)(2,1)} %all-gather.9.cloned.1.call-done.weight_ref.u_ref.refs_1_), custom_call_target="tpu_custom_call" | custom-call | flops 1 | bytes 1 | tf_op jit(solution)/shard_map/down/pallas_call | solution.py:50
  283.9 10.6 %ffn_grads.1 = bf16[768,3072]{1,0:T(8,128)(2,1)} custom-call(s32[1]{0:T(128)} %bitcast.1.side_ref, bf16[768,1536]{1,0:T(8,128)(2,1)} %place_cols.1.dy_ref.refs_0_, bf16[768,1536]{1,0:T(8,128)(2,1)} %get-tuple-element.92.x_ref.refs_1_, bf16[768,1024]{1,0:T(8,128)(2,1)} %get-tuple-element.93.refs_2_.refs_0_, ...), custom_call_target="tpu_custom_call" | custom-call | flops 1 | bytes 1 | tf_op jit(solution)/shard_map/ffn_grads/pallas_call | solution.py:780
  299.1 12.7 %collective-permute-done.15.refs_1_ = bf16[192,1536]{1,0:T(8,128)(2,1)S(1)} collective-permute-done((bf16[192,1536]{1,0:T(8,128)(2,1)S(1)}, bf16[192,1536]{1,0:T(8,128)(2,1)S(1)}, u32[]{:S(2)}, u32[]{:S(2)}) %collective-permute-start.15) | collective-permute-done | bytes 589856 | tf_op jit(solution)/shard_map/ppermute | solution.py:74
  311.8 11.1 %collective-permute-done.17.refs_2_ = bf16[192,1536]{1,0:T(8,128)(2,1)S(1)} collective-permute-done((bf16[192,1536]{1,0:T(8,128)(2,1)S(1)}, bf16[192,1536]{1,0:T(8,128)(2,1)S(1)}, u32[]{:S(2)}, u32[]{:S(2)}) %collective-permute-start.17) | collective-permute-done | bytes 589856 | tf_op jit(solution)/shard_map/ppermute | solution.py:74
  334.0 12.4 %collective-permute-done.19.refs_1_ = bf16[192,1536]{1,0:T(8,128)(2,1)S(1)} collective-permute-done((bf16[192,1536]{1,0:T(8,128)(2,1)}, bf16[192,1536]{1,0:T(8,128)(2,1)S(1)}, u32[]{:S(2)}, u32[]{:S(2)}) %collective-permute-start.19) | collective-permute-done | bytes 589856 | tf_op jit(solution)/shard_map/ppermute | solution.py:74
  346.4 11.3 %collective-permute-done.20.refs_2_ = bf16[192,1536]{1,0:T(8,128)(2,1)S(1)} collective-permute-done((bf16[192,1536]{1,0:T(8,128)(2,1)}, bf16[192,1536]{1,0:T(8,128)(2,1)S(1)}, u32[]{:S(2)}, u32[]{:S(2)}) %collective-permute-start.20) | collective-permute-done | bytes 589856 | tf_op jit(solution)/shard_map/ppermute | solution.py:74
  366.9 6.2 %head_back.1 = (bf16[384,768]{1,0:T(8,128)(2,1)}, f32[24,768]{1,0:T(8,128)}, f32[384,128]{1,0:T(8,128)}) custom-call(f32[1,1]{1,0:T(1,128)} %bitcast.3.lam_ref, bf16[768,1536]{1,0:T(8,128)(2,1)} %place_rows.1.b_ref.refs_0_, bf16[1536,768]{1,0:T(8,128)(2,1)} %all-gather.7.cloned.1.call-done.weight_ref.refs_2_, f32[384,768]{1,0:T(8,128)} %get-tuple-element.110.unit_ref, ...), custom_call_target="tpu_custom_call" | custom-call | flops 1 | bytes 1 | tf_op jit(solution)/shard_map/head_back/pallas_call | solution.py:50
  373.0 8.3 %attend_back_2.1 = (f32[768,384]{1,0:T(8,128)}, bf16[768,768]{1,0:T(8,128)(2,1)}) custom-call(s32[4]{0:T(128)} %pad_add_fusion.1.meta_ref, f32[1,1]{1,0:T(1,128)} %bitcast.3.lam_ref, bf16[768,384]{1,0:T(8,128)(2,1)} %queries.1.q_ref, bf16[768,768]{1,0:T(8,128)(2,1)} %copy-done.1, bf16[768,768]{1,0:T(8,128)(2,1)} %copy-done.1, ...), custom_call_target="tpu_custom_call" | custom-call | flops 1 | bytes 1 | tf_op jit(solution)/shard_map/attend_back_2/pallas_call | solution.py:50
  383.5 8.5 %attend_back_1.1 = (f32[768,384]{1,0:T(8,128)}, bf16[768,768]{1,0:T(8,128)(2,1)}) custom-call(s32[4]{0:T(128)} %pad_add_fusion.1.meta_ref, f32[1,1]{1,0:T(1,128)} %bitcast.3.lam_ref, bf16[768,384]{1,0:T(8,128)(2,1)} %queries.1.q_ref, bf16[768,768]{1,0:T(8,128)(2,1)} %copy-done, bf16[768,768]{1,0:T(8,128)(2,1)} %copy-done, ...), custom_call_target="tpu_custom_call" | custom-call | flops 1 | bytes 1 | tf_op jit(solution)/shard_map/attend_back_1/pallas_call | solution.py:50
  392.0 13.8 %attend_back_0.1 = (f32[768,384]{1,0:T(8,128)}, bf16[768,768]{1,0:T(8,128)(2,1)}) custom-call(s32[4]{0:T(128)} %pad_add_fusion.1.meta_ref, f32[1,1]{1,0:T(1,128)} %bitcast.3.lam_ref, bf16[768,384]{1,0:T(8,128)(2,1)} %queries.1.q_ref, bf16[768,768]{1,0:T(8,128)(2,1)} %get-tuple-element.81.k_ref.v_ref, bf16[768,768]{1,0:T(8,128)(2,1)} %get-tuple-element.81.k_ref.v_ref, ...), custom_call_target="tpu_custom_call" | custom-call | flops 1 | bytes 1 | tf_op jit(solution)/shard_map/attend_back_0/pallas_call | solution.py:50
  411.8 5.2 oq_grads_theirs.1
  420.2 5.4 oq_grads.1
  425.7 45.0 %collective-permute-done.27.refs_0_ = bf16[768,768]{1,0:T(8,128)(2,1)S(1)} collective-permute-done((bf16[768,768]{1,0:T(8,128)(2,1)S(1)}, bf16[768,768]{1,0:T(8,128)(2,1)S(1)}, u32[]{:S(2)}, u32[]{:S(2)}) %collective-permute-start.27) | collective-permute-done | bytes 1179680 | tf_op jit(solution)/shard_map/ppermute | solution.py:916
  480.7 9.5 %in_back.1 = (bf16[768,384]{1,0:T(8,128)(2,1)}, bf16[768,384]{1,0:T(8,128)(2,1)}, bf16[768,384]{1,0:T(8,128)(2,1)}, bf16[768,384]{1,0:T(8,128)(2,1)}, f32[768,1]{1,0:T(8,128)}, /*index=5*/f32[1,1536]{1,0:T(1,128)}) custom-call(s32[2]{0:T(128)} %pad_add_fusion.spot_ref.at_ref, bf16[768,384]{1,0:T(8,128)(2,1)} %query_back.1.refs_3_.refs_0_, ...), custom_call_target="tpu_custom_call" | custom-call | flops 1 | bytes 1 | tf_op jit(solution)/shard_map/in_back/pallas_call | solution.py:50
  512.2 7.2 %collective-permute-done.32 = f32[6,128]{1,0:T(8,128)S(1)} collective-permute-done((f32[6,128]{1,0:T(8,128)S(1)}, f32[6,128]{1,0:T(8,128)S(1)}, u32[]{:S(2)}, u32[]{:S(2)}) %collective-permute-start.32) | collective-permute-done | bytes 3104 | tf_op jit(solution)/shard_map/ppermute | solution.py:74
  526.0 9.1 %collective-permute-done.29 = bf16[768,384]{1,0:T(8,128)(2,1)S(1)} collective-permute-done((bf16[768,384]{1,0:T(8,128)(2,1)}, bf16[768,384]{1,0:T(8,128)(2,1)S(1)}, u32[]{:S(2)}, u32[]{:S(2)}) %collective-permute-start.29) | collective-permute-done | bytes 589856 | tf_op jit(solution)/shard_map/ppermute | solution.py:74
  (237 shorter events, 141.2 us)
Async XLA Ops:
  7.2 38.5 %all-gather.5.cloned.1.call-start = ((), (), s32[]{:S(2)}) async-start(), calls=%async_computation.3 | async-start | bytes 2654208 | tf_op jit(solution)/shard_map/all_gather | solution.py:104
  13.0 79.2 %all-gather.7.cloned.1.call-start = ((), (), s32[]{:S(2)}) async-start(), calls=%async_computation.4 | async-start | bytes 2654208 | tf_op jit(solution)/shard_map/all_gather | solution.py:104
  14.8 215.3 %all-gather.11.cloned.1.call-start = ((), (), s32[]{:S(2)}) async-start(), calls=%async_computation.6 | async-start | bytes 3538944 | tf_op jit(solution)/shard_map/all_gather | solution.py:104
  15.5 220.4 %all-gather.9.cloned.1.call-start = ((), (), s32[]{:S(2)}) async-start(), calls=%async_computation.5 | async-start | bytes 7077888 | tf_op jit(solution)/shard_map/all_gather | solution.py:104
  16.6 409.0 %reduce-scatter.4.cloned.1.call-start = ((), (), s32[]{:S(2)}) async-start(), calls=%async_computation.7 | async-start | bytes 5898240 | tf_op jit(solution)/shard_map/reduce_scatter | solution.py:108
  18.3 27.4 %collective-permute-start.1 = (bf16[768,384]{1,0:T(8,128)(2,1)S(1)}, bf16[768,384]{1,0:T(8,128)(2,1)S(1)}, u32[]{:S(2)}, u32[]{:S(2)}) collective-permute-start(bf16[768,384]{1,0:T(8,128)(2,1)S(1)} %copy-done.4), channel_id=1, source_target_pairs={{0,2},{1,3},{2,0},{3,1},{4,6},{5,7},{6,4},{7,5},{8,10},{9,11},{10,... | collective-permute-start | bytes 1769480 | tf_op jit(solution)/shard_map/ppermute | solution.py:74
  19.8 25.9 %collective-permute-start.2 = (bf16[768,384]{1,0:T(8,128)(2,1)S(1)}, bf16[768,384]{1,0:T(8,128)(2,1)S(1)}, u32[]{:S(2)}, u32[]{:S(2)}) collective-permute-start(bf16[768,384]{1,0:T(8,128)(2,1)S(1)} %copy-done.4), channel_id=1, source_target_pairs={{0,3},{1,2},{2,1},{3,0},{4,7},{5,6},{6,5},{7,4},{8,11},{9,10},{10,... | collective-permute-start | bytes 1769480 | tf_op jit(solution)/shard_map/ppermute | solution.py:74
  54.1 59.2 %collective-permute-start.3 = (bf16[768,768]{1,0:T(8,128)(2,1)}, bf16[768,768]{1,0:T(8,128)(2,1)S(1)}, u32[]{:S(2)}, u32[]{:S(2)}) collective-permute-start(bf16[768,768]{1,0:T(8,128)(2,1)} %get-tuple-element.81.k_ref.v_ref), channel_id=1, source_target_pairs={{0,4},{4,8},{8,12},{1,5},{5,9},{9,13},{2,6},{6,10},{10,14},{3,7},{... | collective-permute-start | bytes 3538952 | tf_op jit(solution)/shard_map/ppermute | solution.py:862
  113.4 57.1 %collective-permute-start.4 = (bf16[768,768]{1,0:T(8,128)(2,1)S(1)}, bf16[768,768]{1,0:T(8,128)(2,1)S(1)}, u32[]{:S(2)}, u32[]{:S(2)}) collective-permute-start(bf16[768,768]{1,0:T(8,128)(2,1)S(1)} %collective-permute-done.3.k_ref.v_ref), channel_id=1, source_target_pairs={{4,8},{8,12},{5,9},{9,13},{6,10},{10,14},{7,11},{11,15},{20,24},{2... | collective-permute-start | bytes 3538952 | tf_op jit(solution)/shard_map/ppermute | solution.py:876
  116.7 65.0 %collective-permute-start.8 = (bf16[768,384]{1,0:T(8,128)(2,1)S(1)}, bf16[768,384]{1,0:T(8,128)(2,1)S(1)}, u32[]{:S(2)}, u32[]{:S(2)}) collective-permute-start(bf16[768,384]{1,0:T(8,128)(2,1)S(1)} %constant_dynamic-slice_fusion.refs_4_), channel_id=1, source_target_pairs={{0,1},{1,0},{2,3},{3,2},{4,5},{5,4},{6,7},{7,6},{8,9},{9,8},{10,11... | collective-permute-start | bytes 1769480 | tf_op jit(solution)/shard_map/ppermute | solution.py:74
  119.1 62.5 %collective-permute-start.9 = (bf16[768,384]{1,0:T(8,128)(2,1)S(1)}, bf16[768,384]{1,0:T(8,128)(2,1)}, u32[]{:S(2)}, u32[]{:S(2)}) collective-permute-start(bf16[768,384]{1,0:T(8,128)(2,1)S(1)} %constant_dynamic-slice_fusion.refs_4_), channel_id=1, source_target_pairs={{0,2},{1,3},{2,0},{3,1},{4,6},{5,7},{6,4},{7,5},{8,10},{9,11},{10,... | collective-permute-start | bytes 1769480 | tf_op jit(solution)/shard_map/ppermute | solution.py:74
  120.8 60.9 %collective-permute-start.10 = (bf16[768,384]{1,0:T(8,128)(2,1)S(1)}, bf16[768,384]{1,0:T(8,128)(2,1)}, u32[]{:S(2)}, u32[]{:S(2)}) collective-permute-start(bf16[768,384]{1,0:T(8,128)(2,1)S(1)} %constant_dynamic-slice_fusion.refs_4_), channel_id=1, source_target_pairs={{0,3},{1,2},{2,1},{3,0},{4,7},{5,6},{6,5},{7,4},{8,11},{9,10},{10,... | collective-permute-start | bytes 1769480 | tf_op jit(solution)/shard_map/ppermute | solution.py:74
  188.7 28.8 %collective-permute-start.6 = (bf16[768,384]{1,0:T(8,128)(2,1)S(1)}, bf16[768,384]{1,0:T(8,128)(2,1)S(1)}, u32[]{:S(2)}, u32[]{:S(2)}) collective-permute-start(bf16[768,384]{1,0:T(8,128)(2,1)S(1)} %copy-done.2), channel_id=1, source_target_pairs={{0,2},{1,3},{2,0},{3,1},{4,6},{5,7},{6,4},{7,5},{8,10},{9,11},{10,... | collective-permute-start | bytes 1769480 | tf_op jit(solution)/shard_map/ppermute | solution.py:74
  190.1 27.4 %collective-permute-start.7 = (bf16[768,384]{1,0:T(8,128)(2,1)S(1)}, bf16[768,384]{1,0:T(8,128)(2,1)S(1)}, u32[]{:S(2)}, u32[]{:S(2)}) collective-permute-start(bf16[768,384]{1,0:T(8,128)(2,1)S(1)} %copy-done.2), channel_id=1, source_target_pairs={{0,3},{1,2},{2,1},{3,0},{4,7},{5,6},{6,5},{7,4},{8,11},{9,10},{10,... | collective-permute-start | bytes 1769480 | tf_op jit(solution)/shard_map/ppermute | solution.py:74
  191.5 51.0 %collective-permute-start.12 = (bf16[768,384]{1,0:T(8,128)(2,1)}, bf16[768,384]{1,0:T(8,128)(2,1)S(1)}, u32[]{:S(2)}, u32[]{:S(2)}) collective-permute-start(bf16[768,384]{1,0:T(8,128)(2,1)} %refs_0_.2), channel_id=1, source_target_pairs={{0,1},{1,0},{2,3},{3,2},{4,5},{5,4},{6,7},{7,6},{8,9},{9,8},{10,11... | collective-permute-start | bytes 1769480 | tf_op jit(solution)/shard_map/ppermute | solution.py:74
  193.2 49.3 %collective-permute-start.13 = (bf16[768,384]{1,0:T(8,128)(2,1)}, bf16[768,384]{1,0:T(8,128)(2,1)S(1)}, u32[]{:S(2)}, u32[]{:S(2)}) collective-permute-start(bf16[768,384]{1,0:T(8,128)(2,1)} %refs_0_.2), channel_id=1, source_target_pairs={{0,2},{1,3},{2,0},{3,1},{4,6},{5,7},{6,4},{7,5},{8,10},{9,11},{10,... | collective-permute-start | bytes 1769480 | tf_op jit(solution)/shard_map/ppermute | solution.py:74
  203.2 39.3 %collective-permute-start.14 = (bf16[768,384]{1,0:T(8,128)(2,1)}, bf16[768,384]{1,0:T(8,128)(2,1)}, u32[]{:S(2)}, u32[]{:S(2)}) collective-permute-start(bf16[768,384]{1,0:T(8,128)(2,1)} %refs_0_.2), channel_id=1, source_target_pairs={{0,3},{1,2},{2,1},{3,0},{4,7},{5,6},{6,5},{7,4},{8,11},{9,10},{10,... | collective-permute-start | bytes 1769480 | tf_op jit(solution)/shard_map/ppermute | solution.py:74
  294.6 203.1 %reduce-scatter.6.cloned.1.call-start = ((), (), s32[]{:S(2)}) async-start(), calls=%async_computation.8 | async-start | bytes 1474560 | tf_op jit(solution)/shard_map/reduce_scatter | solution.py:108
  295.8 27.1 %collective-permute-start.17 = (bf16[192,1536]{1,0:T(8,128)(2,1)S(1)}, bf16[192,1536]{1,0:T(8,128)(2,1)S(1)}, u32[]{:S(2)}, u32[]{:S(2)}) collective-permute-start(bf16[192,1536]{1,0:T(8,128)(2,1)S(1)} %copy-done.43), channel_id=1, source_target_pairs={{0,2},{1,3},{2,0},{3,1},{4,6},{5,7},{6,4},{7,5},{8,10},{9,11},{10,... | collective-permute-start | bytes 1769480 | tf_op jit(solution)/shard_map/ppermute | solution.py:74
  297.7 26.8 %collective-permute-start.18 = (bf16[192,1536]{1,0:T(8,128)(2,1)S(1)}, bf16[192,1536]{1,0:T(8,128)(2,1)S(1)}, u32[]{:S(2)}, u32[]{:S(2)}) collective-permute-start(bf16[192,1536]{1,0:T(8,128)(2,1)S(1)} %copy-done.42), channel_id=1, source_target_pairs={{0,3},{1,2},{2,1},{3,0},{4,7},{5,6},{6,5},{7,4},{8,11},{9,10},{10,... | collective-permute-start | bytes 1769480 | tf_op jit(solution)/shard_map/ppermute | solution.py:74
  329.9 16.5 %collective-permute-start.19 = (bf16[192,1536]{1,0:T(8,128)(2,1)}, bf16[192,1536]{1,0:T(8,128)(2,1)S(1)}, u32[]{:S(2)}, u32[]{:S(2)}) collective-permute-start(bf16[192,1536]{1,0:T(8,128)(2,1)} %get-tuple-element.109.refs_0_), channel_id=1, source_target_pairs={{0,1},{1,0},{2,3},{3,2},{4,5},{5,4},{6,7},{7,6},{8,9},{9,8},{10,11... | collective-permute-start | bytes 1769480 | tf_op jit(solution)/shard_map/ppermute | solution.py:74
  331.1 26.6 %collective-permute-start.20 = (bf16[192,1536]{1,0:T(8,128)(2,1)}, bf16[192,1536]{1,0:T(8,128)(2,1)S(1)}, u32[]{:S(2)}, u32[]{:S(2)}) collective-permute-start(bf16[192,1536]{1,0:T(8,128)(2,1)} %get-tuple-element.109.refs_0_), channel_id=1, source_target_pairs={{0,2},{1,3},{2,0},{3,1},{4,6},{5,7},{6,4},{7,5},{8,10},{9,11},{10,... | collective-permute-start | bytes 1769480 | tf_op jit(solution)/shard_map/ppermute | solution.py:74
  332.5 25.3 %collective-permute-start.21 = (bf16[192,1536]{1,0:T(8,128)(2,1)}, bf16[192,1536]{1,0:T(8,128)(2,1)S(1)}, u32[]{:S(2)}, u32[]{:S(2)}) collective-permute-start(bf16[192,1536]{1,0:T(8,128)(2,1)} %get-tuple-element.109.refs_0_), channel_id=1, source_target_pairs={{0,3},{1,2},{2,1},{3,0},{4,7},{5,6},{6,5},{7,4},{8,11},{9,10},{10,... | collective-permute-start | bytes 1769480 | tf_op jit(solution)/shard_map/ppermute | solution.py:74
  362.6 43.2 %collective-permute-start.24 = (bf16[768,384]{1,0:T(8,128)(2,1)}, bf16[768,384]{1,0:T(8,128)(2,1)S(1)}, u32[]{:S(2)}, u32[]{:S(2)}) collective-permute-start(bf16[768,384]{1,0:T(8,128)(2,1)} %get-tuple-element.124), channel_id=1, source_target_pairs={{0,3},{1,2},{2,1},{3,0},{4,7},{5,6},{6,5},{7,4},{8,11},{9,10},{10,... | collective-permute-start | bytes 1769480 | tf_op jit(solution)/shard_map/ppermute | solution.py:74
  364.0 41.8 %collective-permute-start.23 = (bf16[768,384]{1,0:T(8,128)(2,1)}, bf16[768,384]{1,0:T(8,128)(2,1)S(1)}, u32[]{:S(2)}, u32[]{:S(2)}) collective-permute-start(bf16[768,384]{1,0:T(8,128)(2,1)} %get-tuple-element.122), channel_id=1, source_target_pairs={{0,2},{1,3},{2,0},{3,1},{4,6},{5,7},{6,4},{7,5},{8,10},{9,11},{10,... | collective-permute-start | bytes 1769480 | tf_op jit(solution)/shard_map/ppermute | solution.py:74
  364.5 41.3 %collective-permute-start.22 = (bf16[768,384]{1,0:T(8,128)(2,1)}, bf16[768,384]{1,0:T(8,128)(2,1)S(1)}, u32[]{:S(2)}, u32[]{:S(2)}) collective-permute-start(bf16[768,384]{1,0:T(8,128)(2,1)} %get-tuple-element.120), channel_id=1, source_target_pairs={{0,1},{1,0},{2,3},{3,2},{4,5},{5,4},{6,7},{7,6},{8,9},{9,8},{10,11... | collective-permute-start | bytes 1769480 | tf_op jit(solution)/shard_map/ppermute | solution.py:74
  381.4 35.6 %collective-permute-start.26 = (bf16[768,768]{1,0:T(8,128)(2,1)}, bf16[768,768]{1,0:T(8,128)(2,1)S(1)}, u32[]{:S(2)}, u32[]{:S(2)}) collective-permute-start(bf16[768,768]{1,0:T(8,128)(2,1)} %get-tuple-element.132), channel_id=1, source_target_pairs={{8,4},{12,8},{9,5},{13,9},{10,6},{14,10},{11,7},{15,11},{24,20},{2... | collective-permute-start | bytes 3538952 | tf_op jit(solution)/shard_map/ppermute | solution.py:916
  417.3 53.3 %collective-permute-start.27 = (bf16[768,768]{1,0:T(8,128)(2,1)S(1)}, bf16[768,768]{1,0:T(8,128)(2,1)S(1)}, u32[]{:S(2)}, u32[]{:S(2)}) collective-permute-start(bf16[768,768]{1,0:T(8,128)(2,1)S(1)} %add_convert_fusion), channel_id=1, source_target_pairs={{4,0},{8,4},{12,8},{5,1},{9,5},{13,9},{6,2},{10,6},{14,10},{7,3},{... | collective-permute-start | bytes 3538952 | tf_op jit(solution)/shard_map/ppermute | solution.py:916
  425.6 114.8 %reduce-scatter.8.cloned.1.call-start = ((), (), s32[]{:S(2)}) async-start(), calls=%async_computation.9 | async-start | bytes 1474560 | tf_op jit(solution)/shard_map/reduce_scatter | solution.py:108
  508.5 17.4 %collective-permute-start.30 = (bf16[768,384]{1,0:T(8,128)(2,1)}, bf16[768,384]{1,0:T(8,128)(2,1)S(1)}, u32[]{:S(2)}, u32[]{:S(2)}) collective-permute-start(bf16[768,384]{1,0:T(8,128)(2,1)} %get-tuple-element.137), channel_id=1, source_target_pairs={{0,3},{1,2},{2,1},{3,0},{4,7},{5,6},{6,5},{7,4},{8,11},{9,10},{10,... | collective-permute-start | bytes 1769480 | tf_op jit(solution)/shard_map/ppermute | solution.py:74
  509.8 25.3 %collective-permute-start.29 = (bf16[768,384]{1,0:T(8,128)(2,1)}, bf16[768,384]{1,0:T(8,128)(2,1)S(1)}, u32[]{:S(2)}, u32[]{:S(2)}) collective-permute-start(bf16[768,384]{1,0:T(8,128)(2,1)} %get-tuple-element.136), channel_id=1, source_target_pairs={{0,2},{1,3},{2,0},{3,1},{4,6},{5,7},{6,4},{7,5},{8,10},{9,11},{10,... | collective-permute-start | bytes 1769480 | tf_op jit(solution)/shard_map/ppermute | solution.py:74
  510.4 25.1 %collective-permute-start.28 = (bf16[768,384]{1,0:T(8,128)(2,1)}, bf16[768,384]{1,0:T(8,128)(2,1)S(1)}, u32[]{:S(2)}, u32[]{:S(2)}) collective-permute-start(bf16[768,384]{1,0:T(8,128)(2,1)} %get-tuple-element.135), channel_id=1, source_target_pairs={{0,1},{1,0},{2,3},{3,2},{4,5},{5,4},{6,7},{7,6},{8,9},{9,8},{10,11... | collective-permute-start | bytes 1769480 | tf_op jit(solution)/shard_map/ppermute | solution.py:74
  (59 other events, 562.6 us)
Sparse Core Ops, SparseCore 0:
  13.1 31.8 all-gather.4
  47.2 44.9 all-gather.6
  93.8 41.7 all-gather.10
  137.6 66.3 all-gather.8
  294.7 84.8 reduce-scatter.3
  425.7 51.9 reduce-scatter.5
  497.9 27.9 reduce-scatter.7

commit v2 on v1

v2 whole, which is shorter than its diff:
```python
import functools
import math

import jax
import jax.numpy as jnp
from jax import lax
from jax.experimental import pallas as pl
from jax.experimental.pallas import tpu as pltpu
from jax.sharding import PartitionSpec as P

HALF = 64
VD = 128
LAYER = 6
EPSILON = 1e-06
ROPE_BASE = 10000.0
MAX_START = -1e30
MASKED = -2e38
SCALE = HALF ** (-0.5)
LAMBDA_START = 0.8 - 0.6 * math.exp(-0.3 * (LAYER - 1))
KEEP = 1.0 - LAMBDA_START

BF16 = jnp.bfloat16
F32 = jnp.float32
VMEM_LIMIT = 60 * 1024 * 1024


LONG = {"place_rows": 1000, "norm_mid_back": 1000, "down": 1000}


def work(name):
    return pl.CostEstimate(flops=LONG.get(name, 0) * 10**9 + 1, bytes_accessed=1, transcendentals=0)


def shape(dims, dtype):
    return jax.ShapeDtypeStruct(tuple(dims), dtype)


def whole(memory=pltpu.VMEM):
    return pl.BlockSpec(memory_space=memory)


def fixed(dims):
    zeros = (0,) * len(dims)
    return pl.BlockSpec(tuple(dims), lambda *_: zeros)


def call(body, outs, ins, *, name, grid=None, in_specs=None, out_specs=None, scratch=(), flops=0, move=0):
    if in_specs is None:
        in_specs = [whole(pltpu.SMEM) if a.ndim == 1 and a.dtype == jnp.int32 else whole() for a in ins]
    if out_specs is None:
        out_specs = [whole() for _ in outs]
    kwargs = {}
    if grid is not None:
        kwargs["grid"] = grid
    if not move:
        move = sum(a.size * a.dtype.itemsize for a in list(ins) + list(outs))
    return pl.pallas_call(
        body,
        out_shape=list(outs),
        in_specs=in_specs,
        out_specs=out_specs,
        scratch_shapes=list(scratch),
        compiler_params=pltpu.CompilerParams(vmem_limit_bytes=VMEM_LIMIT),
        cost_estimate=work(name),
        name=name,
        **kwargs,
    )(*ins)


def dot(left, right, left_dim, right_dim):
    return lax.dot_general(
        left, right, (((left_dim,), (right_dim,)), ((), ())), preferred_element_type=F32
    )


def xor_pairs(count, step):
    return [(i, i ^ step) for i in range(count)]


def head_move(value, step):
    return lax.ppermute(value, "head", xor_pairs(lax.axis_size("head"), step))


def core_swap(value):
    return lax.ppermute(value, "dp", xor_pairs(lax.axis_size("dp"), 1))


def head_gather(unit):
    return [unit] + [head_move(unit, k) for k in range(1, lax.axis_size("head"))]


def after(value, *others):
    return lax.optimization_barrier((value,) + others)[0]


def place_rows(units, places, count):
    rows, cols = units[0].shape

    def body(at_ref, *refs):
        out = refs[-1]
        for i, ref in enumerate(refs[:-1]):
            start = pl.multiple_of(at_ref[i] * rows, 16)
            out[pl.ds(start, rows), :] = ref[...]

    return call(
        body, [shape((rows * count, cols), units[0].dtype)], [places] + list(units), name="place_rows"
    )[0]


def gather_rows(unit):
    return lax.all_gather(unit, ("dp", "ctx"), axis=0, tiled=True)


def scatter_rows(sums):
    return lax.psum_scatter(sums, "ctx", scatter_dimension=0, tiled=True)


def line_sum(value):
    value = value + core_swap(value)
    step = 1
    while step < lax.axis_size("ctx"):
        value = value + lax.ppermute(value, "ctx", xor_pairs(lax.axis_size("ctx"), step))
        step *= 2
    return value


def head_sum(value):
    step = 1
    while step < lax.axis_size("head"):
        value = value + head_move(value, step)
        step *= 2
    return value


def turn(value, cosine, sine, sign):
    groups = []
    lanes = lax.broadcasted_iota(jnp.int32, cosine.shape, 1)
    lower = lanes % HALF < HALF // 2
    for i in range(value.shape[1] // 128):
        part = value[:, i * 128 : (i + 1) * 128]
        swapped = jnp.where(
            lower, pltpu.roll(part, 128 - HALF // 2, axis=1), pltpu.roll(part, HALF // 2, axis=1)
        )
        groups.append(part * cosine + sign * (swapped * sine))
    return jnp.concatenate(groups, axis=1)


def half_lanes(value):
    lanes = lax.broadcasted_iota(jnp.int32, value.shape, 1)
    zero = jnp.zeros_like(value)
    return jnp.where(lanes < HALF, value, zero), jnp.where(lanes < HALF, zero, value)


def pack_kernel(keys, values, *others):
    rows, cols = keys.shape
    heads = cols // VD

    def body(k_ref, v_ref, *refs):
        out = refs[-1]
        for h in range(heads):
            at = 2 * h * VD
            out[:, at : at + VD] = k_ref[:, h * VD : (h + 1) * VD]
            out[:, at + VD : at + 2 * VD] = v_ref[:, h * VD : (h + 1) * VD]
        at = 2 * cols
        for ref in refs[:-1]:
            out[:, at : at + ref.shape[1]] = ref[...]
            at += ref.shape[1]

    width = 2 * cols + sum(other.shape[1] for other in others)
    return call(body, [shape((rows, width), keys.dtype)], [keys, values, *others], name="pack")[0]


def norm_in_kernel(units, gain, spot, keep):
    rows, cols = units[0].shape
    count = len(units)
    wide = cols * count
    tile = 256

    def body(spot_ref, gain_ref, *refs):
        ins, outs = refs[:count], refs[count:]
        total = jnp.zeros((tile, 1), F32)
        for ref in ins:
            v = ref[...].astype(F32)
            total = total + jnp.sum(v * v, axis=1, keepdims=True)
        inv = lax.rsqrt(total / wide + EPSILON)
        for k, ref in enumerate(ins):
            at = pl.ds(pl.multiple_of((spot_ref[0] ^ k) * cols, 128), cols)
            v = ref[...]
            outs[0][:, at] = (v.astype(F32) * inv * gain_ref[:, at]).astype(BF16)
            if keep:
                outs[1][:, at] = v
        if keep:
            outs[2][...] = inv

    def tall(w):
        return pl.BlockSpec((tile, w), lambda i: (i, 0))

    outs, out_specs = [shape((rows, wide), BF16)], [tall(wide)]
    if keep:
        outs += [shape((rows, wide), BF16), shape((rows, 1), F32)]
        out_specs += [tall(wide), tall(1)]
    return call(
        body,
        outs,
        [spot, gain] + units,
        grid=(rows // tile,),
        in_specs=[whole(pltpu.SMEM), fixed(gain.shape)] + [tall(cols)] * count,
        out_specs=out_specs,
        name="norm_in",
    )


def project_kernel(x, weight, width, more, cosine, sine):
    rows, wide = x.shape
    tile = 256

    def body(x_ref, weight_ref, cos_ref, sin_ref, *outs):
        y = dot(x_ref[...], weight_ref[...], 1, 0)
        for h in range(width // (2 * VD)):
            at = 2 * h * VD
            outs[0][:, at : at + VD] = turn(y[:, at : at + VD], cos_ref[...], sin_ref[...], 1.0).astype(BF16)
            outs[0][:, at + VD : at + 2 * VD] = y[:, at + VD : at + 2 * VD].astype(BF16)
        if more:
            outs[1][...] = turn(y[:, width:], cos_ref[...], sin_ref[...], 1.0).astype(BF16)

    def tall(w):
        return pl.BlockSpec((tile, w), lambda i: (i, 0))

    widths = [width] + ([more] if more else [])
    return call(
        body,
        [shape((rows, w), BF16) for w in widths],
        [x, weight, cosine, sine],
        grid=(rows // tile,),
        in_specs=[tall(wide), fixed((wide, width + more)), tall(128), tall(128)],
        out_specs=[tall(w) for w in widths],
        name="project",
    )


def place_cols_kernel(units, spot):
    rows, cols = units[0].shape
    count = len(units)

    def body(spot_ref, *refs):
        for k, ref in enumerate(refs[:count]):
            at = pl.ds(pl.multiple_of((spot_ref[0] ^ k) * cols, 128), cols)
            refs[count][:, at] = ref[...]

    return call(body, [shape((rows, cols * count), BF16)], [spot] + units, name="place_cols")[0]


ATTN_TILE = 384


def spans(meta_ref, slot, qi, rows):
    base = (meta_ref[0] - slot) * rows
    first = meta_ref[1 + qi]
    end = (qi + 1) * ATTN_TILE if slot == 0 else rows
    later = end - ATTN_TILE
    present = meta_ref[0] >= slot
    if later == 0:
        return [(slice(0, end), jnp.logical_and(present, first < base + end))]
    return [
        (slice(0, end), jnp.logical_and(present, first < base + later)),
        (
            slice(later, end),
            jnp.logical_and(present, jnp.logical_and(first >= base + later, first < base + end)),
        ),
    ]


def score_mask(meta_ref, slot, qi, at, rows, first):
    dims = (at.stop - at.start, ATTN_TILE)
    key_at = lax.broadcasted_iota(jnp.int32, dims, 0) + ((meta_ref[0] - slot) * rows + at.start)
    ok = key_at >= first
    if slot == 0:
        query_at = lax.broadcasted_iota(jnp.int32, dims, 1) + (meta_ref[0] * rows + qi * ATTN_TILE)
        ok = jnp.logical_and(ok, key_at <= query_at)
    return ok


def attend_kernel(slot, first, last, meta, lam, q, kv, low, gain, state):
    rows = q.shape[0]
    heads = q.shape[1] // VD
    tile = ATTN_TILE
    tiles = rows // tile

    def body(meta_ref, lam_ref, q_ref, k_ref, v_ref, low_ref, gain_ref, *refs):
        if first:
            outs = refs
        else:
            acc_in, stat_in = refs[:2]
            outs = refs[2:]
        if last:
            head_ref, unit_ref, two_ref, fin_ref, acc, stat = outs
        else:
            acc, stat = outs
        if first:
            acc[...] = jnp.zeros_like(acc)
            stat[0:2, :] = jnp.full((2, rows), MAX_START, F32)
            stat[2:8, :] = jnp.zeros((6, rows), F32)
        else:
            acc[...] = acc_in[...]
            stat[...] = stat_in[...]
        for qi in range(tiles):
            cols = slice(qi * tile, (qi + 1) * tile)
            halves = half_lanes(q_ref[cols, :] * BF16(SCALE))
            for at, needed in spans(meta_ref, slot, qi, rows):

                @pl.when(needed)
                def _(qi=qi, at=at, cols=cols, halves=halves):
                    keys = k_ref[at, :]
                    vals = v_ref[at, :]
                    ok = score_mask(meta_ref, slot, qi, at, rows, low_ref[0:1, cols])
                    for half in range(2):
                        score = jnp.where(ok, dot(keys, halves[half], 1, 1), MASKED)
                        old = stat[half : half + 1, cols]
                        new = jnp.maximum(old, jnp.max(score, axis=0, keepdims=True))
                        prob = jnp.exp(score - new)
                        fade = jnp.exp(old - new)
                        stat[half : half + 1, cols] = new
                        stat[2 + half : 3 + half, cols] = stat[2 + half : 3 + half, cols] * fade + jnp.sum(
                            prob, axis=0, keepdims=True
                        )
                        to = slice(half * VD, (half + 1) * VD)
                        acc[to, cols] = acc[to, cols] * fade + dot(vals, prob.astype(BF16), 0, 0)

        if last:
            out_one = acc[0:VD, :] / stat[2:3, :]
            out_two = acc[VD : 2 * VD, :] / stat[3:4, :]
            mixed = out_one - lam_ref[0, 0] * out_two
            inv = lax.rsqrt(jnp.mean(mixed * mixed, axis=0, keepdims=True) + EPSILON)
            unit = mixed * inv
            unit_ref[...] = unit
            two_ref[...] = out_two
            fin_ref[0:2, :] = stat[0:2, :] + jnp.log(stat[2:4, :])
            fin_ref[2:3, :] = inv
            fin_ref[3:8, :] = jnp.zeros((5, rows), F32)
            head_ref[...] = (jnp.transpose(unit) * gain_ref[...] * KEEP).astype(BF16)

    col = pl.BlockSpec((rows, VD), lambda h: (0, h))
    acc_spec = pl.BlockSpec((2 * VD, rows), lambda h: (h, 0))
    stat_spec = pl.BlockSpec((8, rows), lambda h: (h, 0))
    row_spec = pl.BlockSpec((VD, rows), lambda h: (h, 0))
    key_spec = pl.BlockSpec((rows, VD), lambda h: (0, 2 * h))
    value_spec = pl.BlockSpec((rows, VD), lambda h: (0, 2 * h + 1))
    in_specs = [whole(pltpu.SMEM), whole(pltpu.SMEM), col, key_spec, value_spec, fixed(low.shape), fixed(gain.shape)]
    ins = [meta, lam, q, kv, kv, low, gain]
    if not first:
        in_specs += [acc_spec, stat_spec]
        ins += list(state)
    outs, out_specs, scratch = [], [], []
    if last:
        outs = [
            shape((rows, heads * VD), BF16),
            shape((heads * VD, rows), F32),
            shape((heads * VD, rows), F32),
            shape((heads * 8, rows), F32),
        ]
        out_specs = [col, row_spec, row_spec, stat_spec]
        scratch = [pltpu.VMEM((2 * VD, rows), F32), pltpu.VMEM((8, rows), F32)]
    else:
        outs = [shape((heads * 2 * VD, rows), F32), shape((heads * 8, rows), F32)]
        out_specs = [acc_spec, stat_spec]
    return call(
        body,
        outs,
        ins,
        grid=(heads,),
        in_specs=in_specs,
        out_specs=out_specs,
        scratch=scratch,
        name=f"attend_{slot}",
        flops=2 * heads * rows * rows * (2 * HALF + 2 * VD),
    )


def attend_back_kernel(slot, finish, meta, lam, q, kv, low, grad, tables, sums):
    rows = q.shape[0]
    heads = q.shape[1] // VD
    want_q, want_k = sums[0] is not False, sums[1] is not False

    def body(meta_ref, lam_ref, q_ref, k_ref, v_ref, low_ref, grad_ref, cos_ref, sin_ref, *refs):
        refs = list(refs)
        dq_in = refs.pop(0) if want_q and sums[0] is not None else None
        dkv_in = refs.pop(0) if want_k and sums[1] is not None else None
        dq_out = refs.pop(0) if want_q else None
        dkv_out = refs.pop(0) if want_k else None
        dq_acc = refs.pop(0) if want_q else None
        if want_k:
            dk_acc, dv_acc = refs
        if want_q:
            dq_acc[...] = jnp.zeros_like(dq_acc) if dq_in is None else dq_in[...]
        if want_k:
            dk_acc[...] = jnp.zeros_like(dk_acc) if dkv_in is None else dkv_in[:, :VD]
            dv_acc[...] = jnp.zeros_like(dv_acc) if dkv_in is None else dkv_in[:, VD:]
        lam_value = lam_ref[0, 0]
        parts = grad_ref[VD : VD + 16, :].astype(F32)
        stat = parts[0:8, :] + parts[8:16, :]
        for qi in range(rows // ATTN_TILE):
            cols = slice(qi * ATTN_TILE, (qi + 1) * ATTN_TILE)
            q_one, q_two = half_lanes(q_ref[cols, :] * BF16(SCALE))
            for at, needed in spans(meta_ref, slot, qi, rows):

                @pl.when(needed)
                def _(qi=qi, at=at, cols=cols, q_one=q_one, q_two=q_two):
                    keys = k_ref[at, :]
                    grads = grad_ref[0:VD, cols]
                    ok = score_mask(meta_ref, slot, qi, at, rows, low_ref[0:1, cols])
                    inner = dot(v_ref[at, :], grads, 1, 0)
                    one = jnp.exp(jnp.where(ok, dot(keys, q_one, 1, 1), MASKED) - stat[0:1, cols])
                    two = lam_value * jnp.exp(
                        jnp.where(ok, dot(keys, q_two, 1, 1), MASKED) - stat[1:2, cols]
                    )
                    d_one = (one * (inner - stat[2:3, cols])).astype(BF16)
                    d_two = (two * (stat[3:4, cols] - inner)).astype(BF16)
                    if want_q:
                        k_one, k_two = half_lanes(keys * BF16(SCALE))
                        dq_acc[cols, :] += dot(d_one, k_one, 0, 0) + dot(d_two, k_two, 0, 0)
                    if want_k:
                        dv_acc[at, :] += dot((one - two).astype(BF16), grads, 1, 1)
                        dk_acc[at, :] += dot(d_one, q_one, 1, 0) + dot(d_two, q_two, 1, 0)

        if want_q:
            if finish[0]:
                dq_out[...] = turn(dq_acc[...], cos_ref[...], sin_ref[...], -1.0).astype(BF16)
            else:
                dq_out[...] = dq_acc[...]
        if want_k:
            if finish[1]:
                dkv_out[:, :VD] = turn(dk_acc[...], cos_ref[...], sin_ref[...], -1.0).astype(BF16)
                dkv_out[:, VD:] = dv_acc[...].astype(BF16)
            else:
                dkv_out[:, :VD] = dk_acc[...]
                dkv_out[:, VD:] = dv_acc[...]

    col = pl.BlockSpec((rows, VD), lambda h: (0, h))
    pair = pl.BlockSpec((rows, 2 * VD), lambda h: (0, h))
    ins = [meta, lam, q, kv, kv, low, grad, tables[0], tables[1]]
    in_specs = [
        whole(pltpu.SMEM),
        whole(pltpu.SMEM),
        col,
        pl.BlockSpec((rows, VD), lambda h: (0, 2 * h)),
        pl.BlockSpec((rows, VD), lambda h: (0, 2 * h + 1)),
        fixed(low.shape),
        pl.BlockSpec((VD + 16, rows), lambda h: (h, 0)),
        fixed(tables[0].shape),
        fixed(tables[1].shape),
    ]
    outs, out_specs, scratch = [], [], []
    for i, (want, spec, width) in enumerate(((want_q, col, VD), (want_k, pair, 2 * VD))):
        if want:
            if sums[i] is not None:
                ins.append(sums[i])
                in_specs.append(spec)
            outs.append(shape((rows, heads * width), BF16 if finish[i] else F32))
            out_specs.append(spec)
            scratch += [pltpu.VMEM((rows, VD), F32)] * (width // VD)
    kind = ("q" if want_q else "") + ("k" if want_k else "")
    return call(
        body,
        outs,
        ins,
        grid=(heads,),
        in_specs=in_specs,
        out_specs=out_specs,
        scratch=scratch,
        name=f"attend_back_{kind}{slot}",
    )


def middle_kernel(x, heads_out, mine, theirs, gain, spot):
    rows, wide = x.shape
    half = wide // 2
    count = len(heads_out)
    cols = heads_out[0].shape[1]
    tile = 256

    def body(spot_ref, x_ref, gain_ref, *refs):
        ho, wm, wt = refs[:count], refs[count : 2 * count], refs[2 * count : 3 * count]
        resid_ref, normed_ref, inv_ref = refs[3 * count :]
        total = jnp.zeros((tile, 1), F32)
        for side, weights in ((0, wm), (1, wt)):
            at = pl.ds(pl.multiple_of((spot_ref[1] ^ side) * half, 128), half)
            value = x_ref[:, at].astype(F32)
            for k in range(count):
                value = value + dot(ho[k][...], weights[k][...], 1, 1)
            resid_ref[:, at] = value
            total = total + jnp.sum(value * value, axis=1, keepdims=True)
        inv = lax.rsqrt(total / wide + EPSILON)
        inv_ref[...] = inv
        normed_ref[...] = (resid_ref[...] * inv * gain_ref[...]).astype(BF16)

    def tall(width):
        return pl.BlockSpec((tile, width), lambda i: (i, 0))

    return call(
        body,
        [shape((rows, wide), F32), shape((rows, wide), BF16), shape((rows, 1), F32)],
        [spot, x, gain] + heads_out + mine + theirs,
        grid=(rows // tile,),
        in_specs=[whole(pltpu.SMEM), tall(wide), fixed(gain.shape)]
        + [tall(cols)] * count
        + [fixed(mine[0].shape)] * (2 * count),
        out_specs=[tall(wide), tall(wide), tall(1)],
        name="middle",
    )


def ffn_kernel(x, dy, weights):
    rows, wide = x.shape
    cols = weights.shape[1] // 3
    tile = 256
    steps = cols // tile

    def body(x_ref, dy_ref, gate_w, up_w, down_w, hidden_ref, dgate_ref, dup_ref):
        gate = dot(x_ref[...], gate_w[...], 1, 0)
        up = dot(x_ref[...], up_w[...], 1, 0)
        grad = dot(dy_ref[...], down_w[...], 1, 0)
        sig = jax.nn.sigmoid(gate)
        active = gate * sig
        hidden_ref[...] = (active * up).astype(BF16)
        dgate_ref[...] = (grad * up * sig * (1.0 + gate * (1.0 - sig))).astype(BF16)
        dup_ref[...] = (grad * active).astype(BF16)

    def slab(part):
        return pl.BlockSpec((wide, tile), lambda i: (0, part * steps + i))

    strip = pl.BlockSpec((rows, tile), lambda i: (0, i))
    return call(
        body,
        [shape((rows, cols), BF16)] * 3,
        [x, dy, weights, weights, weights],
        grid=(steps,),
        in_specs=[fixed(x.shape), fixed(dy.shape), slab(0), slab(1), slab(2)],
        out_specs=[strip] * 3,
        name="ffn",
    )


def quarters_kernel(terms, spot, count, name, norm=None):
    rows = terms[0][0].shape[0]
    wide = terms[0][1].shape[0]
    cols = wide // count
    n = len(terms)

    def body(spot_ref, *refs):
        lefts, weights = refs[:n], refs[n : 2 * n]
        rest = refs[2 * n :]
        if norm is not None:
            x_ref, inv_ref, gain_ref = rest[:3]
            rest = rest[3:]
            col_ref, row_ref = rest[count:]
        outs = rest[:count]
        pos = pl.program_id(0)
        value = dot(lefts[0][...], weights[0][...], 1, 1)
        for i in range(1, n):
            value = value + dot(lefts[i][...], weights[i][...], 1, 1)
        if norm is not None:
            weighed = value * (x_ref[...].astype(F32) * inv_ref[...])
            col_ref[...] = jnp.sum(weighed, axis=0, keepdims=True)
            ones = jnp.ones((8, cols), BF16)
            row_sum = dot(ones, (weighed * gain_ref[...]).astype(BF16), 1, 1)

            @pl.when(pos == 0)
            def _():
                row_ref[...] = row_sum

            @pl.when(pos > 0)
            def _():
                row_ref[...] += row_sum

        value = value.astype(BF16)
        for k in range(count):

            @pl.when(spot_ref[0] ^ k == pos)
            def _(k=k):
                outs[k][0:rows, :] = value

        if norm is not None:

            @pl.when(pos == count - 1)
            def _():
                total = row_ref[0:1, :]
                high = total.astype(BF16).astype(F32)
                packed = []
                for part in (high, total - high):
                    packed += [part[:, at : at + cols] for at in range(0, rows, cols)]
                packed.append(jnp.zeros((16 - len(packed), cols), F32))
                packed = jnp.concatenate(packed, axis=0).astype(BF16)
                for out in outs:
                    out[rows : rows + 16, :] = packed

    ins = [spot] + [t[0] for t in terms] + [t[1] for t in terms]
    in_specs = [whole(pltpu.SMEM)] + [fixed(t[0].shape) for t in terms]
    for left, _, first in terms:
        width = left.shape[1]
        in_specs.append(pl.BlockSpec((cols, width), lambda i, at=first // width: (i, at)))
    tall = rows if norm is None else rows + 16
    outs = [shape((tall, cols), BF16)] * count
    out_specs = [fixed((tall, cols))] * count
    scratch = []
    if norm is not None:
        ins += list(norm)
        in_specs += [
            pl.BlockSpec((rows, cols), lambda i: (0, i)),
            fixed((rows, 1)),
            pl.BlockSpec((1, cols), lambda i: (0, i)),
        ]
        outs = outs + [shape((1, wide), F32)]
        out_specs = out_specs + [pl.BlockSpec((1, cols), lambda i: (0, i))]
        scratch = [pltpu.VMEM((8, rows), F32)]
    return call(
        body, outs, ins, grid=(count,), in_specs=in_specs, out_specs=out_specs, scratch=scratch, name=name
    )


def mid_back_kernel(dgate, dup, gate_w, gate_first, up_w, up_first, head_at, count):
    rows, cols = dgate.shape
    wide = gate_w.shape[0]
    tile = 384
    steps = wide // tile
    part = rows // count

    def body(at_ref, dgate_ref, dup_ref, g_ref, u_ref, *refs):
        outs = refs[:count]
        value = dot(dgate_ref[...], g_ref[...], 1, 1) + dot(dup_ref[...], u_ref[...], 1, 1)
        value = value.astype(BF16)
        for row in range(count):
            rows_of = value[row * part : (row + 1) * part, :]
            for k in range(count):

                @pl.when(at_ref[0] ^ k == row)
                def _(k=k, rows_of=rows_of):
                    outs[k][...] = rows_of

    return call(
        body,
        [shape((part, wide), BF16)] * count,
        [head_at, dgate, dup, gate_w, up_w],
        grid=(steps,),
        in_specs=[
            whole(pltpu.SMEM),
            fixed(dgate.shape),
            fixed(dup.shape),
            pl.BlockSpec((tile, cols), lambda i: (i, gate_first // cols)),
            pl.BlockSpec((tile, cols), lambda i: (i, up_first // cols)),
        ],
        out_specs=[pl.BlockSpec((part, tile), lambda i: (0, i))] * count,
        name="mid_back",
    )


def norm_mid_back_kernel(parts, resid, inv, gain, dy, spot):
    part, wide = parts[0].shape
    count = len(parts)

    def body(spot_ref, gain_ref, resid_ref, inv_ref, dy_ref, *refs):
        ins, (out_ref, col_ref) = refs[:count], refs[count:]
        grad = ins[0][...].astype(F32)
        for ref in ins[1:]:
            grad = grad + ref[...].astype(F32)
        inv_rows = inv_ref[...]
        unit = resid_ref[...] * inv_rows
        col_ref[...] = jnp.sum(grad * unit, axis=0, keepdims=True)
        e = grad * gain_ref[...]
        mean = jnp.sum(e * unit, axis=1, keepdims=True) / wide
        out_ref[...] = (dy_ref[...].astype(F32) + inv_rows * (e - unit * mean)).astype(BF16)

    def mine(width):
        return pl.BlockSpec((part, width), lambda i, spot_ref: (spot_ref[0], 0))

    def all_of(dims):
        return pl.BlockSpec(tuple(dims), lambda i, spot_ref: (0, 0))

    return pl.pallas_call(
        body,
        out_shape=[shape((part, wide), BF16), shape((1, wide), F32)],
        grid_spec=pltpu.PrefetchScalarGridSpec(
            num_scalar_prefetch=1,
            grid=(1,),
            in_specs=[all_of(gain.shape), mine(wide), mine(1), mine(wide)] + [all_of((part, wide))] * count,
            out_specs=[all_of((part, wide)), all_of((1, wide))],
        ),
        compiler_params=pltpu.CompilerParams(vmem_limit_bytes=VMEM_LIMIT),
        cost_estimate=work("norm_mid_back"),
        name="norm_mid_back",
    )(spot, gain, resid, inv, dy, *parts)


def head_back_kernel(branch, weight, first, cols, unit, two, fin, gain, lam):
    rows, wide = branch.shape
    heads = cols // VD

    def body(lam_ref, b_ref, weight_ref, unit_ref, two_ref, fin_ref, gain_ref, g_ref, sum_ref):
        grad = jnp.transpose(dot(b_ref[...], weight_ref[...], 1, 0))
        unit = unit_ref[...]
        out_two = two_ref[...]
        inv = fin_ref[2:3, :]
        f = grad * gain_ref[...] * KEEP
        mean = jnp.mean(f * unit, axis=0, keepdims=True)
        mixed_grad = inv * (f - unit * mean)
        g = mixed_grad.astype(BF16)
        g_ref[0:VD, :] = g
        g = g.astype(F32)
        delta_two = jnp.sum(g * out_two, axis=0, keepdims=True)
        mixed = unit / inv
        delta_one = jnp.sum(g * mixed, axis=0, keepdims=True) + lam_ref[0, 0] * delta_two
        stat = jnp.concatenate(
            [fin_ref[0:2, :], delta_one, delta_two, jnp.zeros((4, rows), F32)], axis=0
        )
        high = stat.astype(BF16).astype(F32)
        g_ref[VD : VD + 16, :] = jnp.concatenate([high, stat - high], axis=0).astype(BF16)
        gain_term = jnp.sum(grad * unit, axis=1, keepdims=True) * KEEP
        lam_term = -jnp.sum(mixed_grad * out_two, axis=1, keepdims=True)
        lanes = lax.broadcasted_iota(jnp.int32, (VD, 128), 1)
        sum_ref[...] = jnp.where(lanes == 0, gain_term, jnp.where(lanes == 1, lam_term, 0.0))

    row_spec = pl.BlockSpec((VD, rows), lambda h: (h, 0))
    stat_spec = pl.BlockSpec((8, rows), lambda h: (h, 0))
    slab = pl.BlockSpec((wide, VD), lambda h: (0, first // VD + h))
    return call(
        body,
        [shape((heads * (VD + 16), rows), BF16), shape((heads * VD, 128), F32)],
        [lam, branch, weight, unit, two, fin, gain],
        grid=(heads,),
        in_specs=[
            whole(pltpu.SMEM),
            fixed(branch.shape),
            slab,
            row_spec,
            row_spec,
            stat_spec,
            fixed(gain.shape),
        ],
        out_specs=[
            pl.BlockSpec((VD + 16, rows), lambda h: (h, 0)),
            pl.BlockSpec((VD, 128), lambda h: (h, 0)),
        ],
        name="head_back",
        flops=2 * rows * wide * cols,
    )


def outer_kernel(pairs, side, got, name, split=False):
    rows = pairs[0][0].shape[0]
    half = pairs[0][0].shape[1] // 2
    widths = [right.shape[1] for _, right in pairs]
    tile = 512 if all(w % 512 == 0 for w in widths) else 384
    steps = [w // tile for w in widths]
    starts = [sum(steps[:i]) for i in range(len(steps))]
    n = len(pairs)
    lefts = []
    for left, _ in pairs:
        if not any(left is other for other in lefts):
            lefts.append(left)
    left_of = [next(i for i, other in enumerate(lefts) if other is left) for left, _ in pairs]
    with_got = got is not None

    def body(side_ref, *refs):
        left_refs, right_refs = refs[: len(lefts)], refs[len(lefts) : len(lefts) + n]
        turned = refs[-1]
        out_refs = refs[-1 - n : -1] if split else [refs[-2]] * n
        got_ref = refs[len(lefts) + n]
        step = pl.program_id(0)
        for i in range(n):
            if i == 0 or left_of[i] != left_of[i - 1]:

                @pl.when(step == starts[i])
                def _(i=i):
                    turned[...] = jnp.transpose(left_refs[left_of[i]][...])

            @pl.when(jnp.logical_and(step >= starts[i], step < starts[i] + steps[i]))
            def _(i=i):
                value = dot(turned[...], right_refs[i][...], 1, 0)
                if with_got:
                    value = value + got_ref[...].astype(F32)
                out_refs[i][...] = value.astype(BF16)

    def right_spec(i):
        return pl.BlockSpec((rows, tile), lambda j, side_ref: (0, jnp.clip(j - starts[i], 0, steps[i] - 1)))

    def out_spec(i):
        return pl.BlockSpec((half, tile), lambda j, side_ref: (0, jnp.clip(j - starts[i], 0, steps[i] - 1)))

    strip = pl.BlockSpec((half, tile), lambda j, side_ref: (0, j))
    return pl.pallas_call(
        body,
        out_shape=[shape((half, w), BF16) for w in widths] if split else shape((half, sum(widths)), BF16),
        grid_spec=pltpu.PrefetchScalarGridSpec(
            num_scalar_prefetch=1,
            grid=(sum(steps),),
            in_specs=[pl.BlockSpec((rows, half), lambda j, side_ref: (0, side_ref[0]))] * len(lefts)
            + [right_spec(i) for i in range(n)]
            + ([strip] if with_got else []),
            out_specs=[out_spec(i) for i in range(n)] if split else strip,
            scratch_shapes=[pltpu.VMEM((half, rows), BF16)],
        ),
        compiler_params=pltpu.CompilerParams(vmem_limit_bytes=VMEM_LIMIT),
        cost_estimate=work(name),
        name=name,
    )(side, *lefts, *[right for _, right in pairs], *([got] if with_got else []))


def per_device(
    tokens,
    segment_ids,
    gain_attn,
    w_query,
    w_key,
    w_value,
    w_output,
    lambda_vec,
    gain_heads,
    gain_ffn,
    w_gate,
    w_up,
    w_down,
    grad_out,
):
    rows, slice_width = tokens.shape
    n_ctx = lax.axis_size("ctx")
    n_head = lax.axis_size("head")
    place = lax.axis_index("ctx")
    head = lax.axis_index("head")
    core = lax.axis_index("dp")
    group = segment_ids.shape[0]
    wide = slice_width * n_head
    cols = w_query.shape[1]
    heads = cols // VD
    spot = jnp.stack([head, core]).astype(jnp.int32)
    my_side = jnp.reshape(core, (1,)).astype(jnp.int32)
    other_side = 1 - my_side
    reach = n_ctx
    if n_ctx == 4 and group == 3072 and rows == 768:
        reach = n_ctx - 1

    kvqo_w = gather_rows(pack_kernel(w_key, w_value, w_query, w_output.T))
    downward = [[(i + slot, i) for i in range(n_ctx - slot)] for slot in range(reach)]
    x_units = head_gather(tokens)
    hidden_cols = w_gate.shape[1]
    gud_w = gather_rows(jnp.concatenate([w_gate, w_up, w_down.T], axis=1))

    lane = jnp.arange(128, dtype=jnp.int32)
    frequency = ROPE_BASE ** (-((lane % (HALF // 2)).astype(F32) * 2.0 / HALF))
    sign = jnp.where(lane % HALF < HALF // 2, -1.0, 1.0)[None, :]

    def starts_of(block):
        first_row = jnp.clip(block, 0, n_ctx - 1) * rows
        segs = lax.dynamic_slice_in_dim(segment_ids, first_row, rows, 0)
        return jnp.sum((segment_ids[None, :] < segs[:, None]).astype(jnp.int32), axis=1)

    def tables_of(block, before):
        row_index = jnp.clip(block, 0, n_ctx - 1) * rows + jnp.arange(rows, dtype=jnp.int32)
        angles = (row_index - before).astype(F32)[:, None] * frequency[None, :]
        return jnp.cos(angles), jnp.sin(angles) * sign

    def reach_of(block, before):
        before = jnp.where(block < n_ctx, before, jnp.int32(1 << 30))
        low = jnp.broadcast_to(before[None, :], (8, rows))
        return low, jnp.concatenate([jnp.reshape(block, (1,)), before[::ATTN_TILE]]).astype(jnp.int32)

    own_starts = starts_of(place)
    tables = [tables_of(place, own_starts)]
    for slot in range(1, reach):
        tables.append(tables_of(place - slot, starts_of(place - slot)))
    cosine, sine = tables[0]
    low, meta = reach_of(place, own_starts)
    token_slots = [tokens]
    for slot in range(1, reach):
        token_slots.append(lax.ppermute(token_slots[-1], "ctx", [(i, i + 1) for i in range(slot - 1, n_ctx - 1)]))
    exp_one = jnp.exp(jnp.sum(lambda_vec[0] * lambda_vec[1]))
    exp_two = jnp.exp(jnp.sum(lambda_vec[2] * lambda_vec[3]))
    lam = jnp.reshape(exp_one - exp_two + LAMBDA_START, (1, 1))

    gain_in = gain_attn[None, :]
    gain_mid = gain_ffn[None, :]

    x_units[0] = after(x_units[0], *[t for pair in tables for t in pair])
    normed_in, x_full, inv_in = norm_in_kernel(x_units, gain_in, spot, True)
    dy_units = head_gather(after(grad_out, normed_in))
    dy = place_cols_kernel(dy_units, spot)
    kvqo_w = after(kvqo_w, dy)
    kv, queries = project_kernel(normed_in, kvqo_w, 2 * cols, cols, cosine, sine)
    query_slots = [queries]
    half = wide // 2
    o_half = lax.dynamic_slice(kvqo_w, (core * half, 3 * cols), (half, cols))
    kv_slots = [kv]

    def keys_of(slot, units):
        normed = norm_in_kernel(units, gain_in, spot, False)[0]
        kv_slots.extend(project_kernel(normed, kvqo_w, 2 * cols, 0, *tables[slot]))

    def attend(slot, state):
        return attend_kernel(
            slot,
            slot == 0,
            slot == reach - 1,
            meta,
            lam,
            queries,
            kv_slots[slot],
            low,
            gain_heads[None, :],
            state,
        )

    state = None
    units = head_gather(after(token_slots[1], dy_units[1])) if reach > 1 else dy_units
    state = attend(0, state)
    for slot in range(1, reach):
        coming = units
        if slot + 1 < reach:
            units = head_gather(after(token_slots[slot + 1], state[0], *coming[1:]))
        keys_of(slot, [after(coming[0], state[0])] + coming[1:])
        if slot == reach - 1:
            o_units = head_gather(after(o_half, state[0], *coming[1:]))
        state = attend(slot, state)
    if reach == 1:
        o_units = head_gather(o_half)
    head_out, unit_head, out_two, finish = state
    ho_units = head_gather(head_out)
    o_theirs = [core_swap(after(u, head_out)) for u in o_units]
    resid, normed_mid, inv_mid = middle_kernel(x_full, ho_units, o_units, o_theirs, gain_mid, spot)
    hidden, dgate, dup = ffn_kernel(normed_mid, dy, gud_w)
    for slot in range(1, reach):
        sent = after(query_slots[-1], dgate)
        query_slots.append(lax.ppermute(sent, "ctx", [(i, i - 1) for i in range(1, n_ctx + 1 - slot)]))
    mid_parts = mid_back_kernel(dgate, dup, gud_w, 0, gud_w, hidden_cols, spot, n_head)
    mid_got = [head_move(mid_parts[k], k) for k in range(1, n_head)]

    d_theirs = outer_kernel([(dy, hidden)], after(other_side, mid_parts[0]), None, "d_grads_theirs")
    d_got = core_swap(d_theirs)
    y_parts = quarters_kernel([(hidden, gud_w, 2 * hidden_cols)], after(spot, d_theirs), n_head, "down")
    d_sums = outer_kernel([(dy, hidden)], after(my_side, y_parts[0]), d_got, "d_grads")
    d_total = scatter_rows(d_sums)
    gu_pairs = [(normed_mid, dgate), (normed_mid, dup)]
    gu_theirs = outer_kernel(gu_pairs, after(other_side, d_sums), None, "gu_grads_theirs")
    gu_got = core_swap(gu_theirs)
    mid_got[0] = after(mid_got[0], gu_theirs, *query_slots[1:])
    branch_rows, ffn_gain_term = norm_mid_back_kernel(
        [mid_parts[0]] + mid_got, resid, inv_mid, gain_mid, dy, spot
    )
    branch_units = head_gather(branch_rows)
    g_sums, u_sums = outer_kernel(gu_pairs, after(my_side, branch_rows), gu_got, "gu_grads", split=True)
    g_total = scatter_rows(g_sums)
    branch_units[0] = after(branch_units[0], d_total)
    branch = place_rows(
        branch_units, jnp.stack([head ^ k for k in range(n_head)]).astype(jnp.int32), n_head
    )

    grads, head_sums = head_back_kernel(
        branch, kvqo_w, 3 * cols, cols, unit_head, out_two, finish, gain_heads[:, None], lam
    )
    grad_slots = [grads]

    for slot in range(1, reach):
        grad_slots.append(lax.ppermute(grads, "ctx", downward[slot]))

    def back(slot, finish, on, sums, *gates):
        block_low, block_meta = low, meta
        if on:
            block_low, block_meta = reach_of(place + slot, starts_of(place + slot))
        return attend_back_kernel(
            slot,
            finish,
            after(block_meta, *gates),
            lam,
            query_slots[slot] if on else queries,
            kv if on else kv_slots[slot],
            block_low,
            grad_slots[slot] if on else grads,
            (cosine, sine),
            sums,
        )

    y_got = [head_move(after(y_parts[k], branch), k) for k in range(1, n_head)]
    only = reach == 1
    dq, dkv = back(0, (only, only), False, (None, None))
    last = dq
    for slot in reversed(range(1, reach)):
        arrived = [grad_slots[1]] + y_got if slot == 1 else []
        dq = back(slot, (slot == 1, False), False, (dq, False), last, *arrived)[0]
        last = dq
    dq_pre = dq

    my_cols = head * slice_width
    output = lax.dynamic_slice_in_dim(resid, my_cols, slice_width, 1) + after(y_parts[0], dq_pre).astype(F32)
    for got in y_got:
        output = output + got.astype(F32)
    output = output.astype(BF16)
    last = output
    for slot in range(1, reach):
        dkv = back(slot, (False, slot == reach - 1), True, (False, dkv), last)[0]
        last = dkv
        if slot == 1:
            u_sums = after(u_sums, dkv)
    u_total = scatter_rows(after(u_sums, g_total, *grad_slots))
    dkv_pre = dkv

    oqkv_pairs = [(branch, head_out), (normed_in, dq_pre), (normed_in, dkv_pre)]
    oqkv_theirs = outer_kernel(oqkv_pairs, other_side, None, "oqkv_grads_theirs")
    oqkv_got = core_swap(oqkv_theirs)
    in_parts = quarters_kernel(
        [(dq_pre, kvqo_w, 2 * cols), (dkv_pre, kvqo_w, 0)],
        after(spot, oqkv_theirs),
        n_head,
        "in_back",
        norm=(x_full, inv_in, gain_in),
    )
    oqkv_sums = outer_kernel(oqkv_pairs, after(my_side, in_parts[0]), oqkv_got, "oqkv_grads")
    oqkv_total = scatter_rows(after(oqkv_sums, u_total))
    oq_total, kv_total = oqkv_total[:, : 2 * cols], oqkv_total[:, 2 * cols :]
    head_sums = jnp.sum(head_sums.reshape(heads, VD, 128), axis=0)
    small = jnp.concatenate(
        [
            in_parts[n_head][0],
            ffn_gain_term[0],
            head_sums[:, 0],
            jnp.full((128,), jnp.sum(head_sums[:, 1]), F32),
        ]
    ).reshape(-1, 128)
    small = line_sum(small)
    in_got = [head_move(in_parts[k], k) for k in range(1, n_head)]
    grad_in = jnp.zeros((rows + 16, slice_width), F32)
    for got in [in_parts[0]] + in_got:
        grad_in = grad_in + got.astype(F32)
    count = rows // slice_width
    row_sums = (grad_in[rows : rows + count] + grad_in[rows + count : rows + 2 * count]).reshape(rows, 1)
    grad_in = grad_in[:rows]
    my_gain = lax.dynamic_slice_in_dim(gain_in, my_cols, slice_width, 1)
    my_branch = lax.dynamic_slice_in_dim(branch, my_cols, slice_width, 1).astype(F32)
    unit_in = tokens.astype(F32) * inv_in
    grad_tokens = my_branch + inv_in * (grad_in * my_gain - unit_in * (row_sums / wide))

    small = head_sum(after(small, *in_got)).reshape(-1)
    attn_gain_grad = small[:wide]
    ffn_gain_grad = small[wide : 2 * wide]
    heads_gain_grad = small[2 * wide : 2 * wide + VD]
    lambda_scalar = small[2 * wide + VD]
    grad_lambda = jnp.stack(
        [
            lambda_scalar * exp_one * lambda_vec[1],
            lambda_scalar * exp_one * lambda_vec[0],
            -lambda_scalar * exp_two * lambda_vec[3],
            -lambda_scalar * exp_two * lambda_vec[2],
        ],
        axis=0,
    )
    grad_kv = kv_total.astype(F32)
    grad_key = jnp.concatenate([grad_kv[:, 2 * h * VD : (2 * h + 1) * VD] for h in range(heads)], axis=1)
    grad_value = jnp.concatenate(
        [grad_kv[:, (2 * h + 1) * VD : (2 * h + 2) * VD] for h in range(heads)], axis=1
    )
    return (
        output,
        grad_tokens,
        attn_gain_grad,
        oq_total[:, cols:].astype(F32),
        grad_key,
        grad_value,
        oq_total[:, :cols].astype(F32).T,
        grad_lambda,
        heads_gain_grad,
        ffn_gain_grad,
        g_total.astype(F32),
        u_total.astype(F32),
        d_total.astype(F32).T,
    )


def solution(mesh):
    split = P(("dp", "ctx"), "head")
    turned = P("head", ("dp", "ctx"))
    in_specs = (
        split,
        P("dp"),
        P(),
        split,
        split,
        split,
        turned,
        P(),
        P(),
        P(),
        split,
        split,
        turned,
        split,
    )
    out_specs = (
        split,
        split,
        P(),
        split,
        split,
        split,
        turned,
        P(),
        P(),
        P(),
        split,
        split,
        turned,
    )
    return jax.shard_map(
        per_device, mesh=mesh, in_specs=in_specs, out_specs=out_specs, check_vma=False
    )
```

time: 558 us -> 455 us (0.82)
  waiting for transfers between devices: 236 us -> 102 us
  Pallas kernels: 203 us -> 220 us
  starting transfers between devices: 44.2 us -> 58.5 us
    ppermute x6 -> x8, waiting for transfers between devices: 85.1 us -> 9.94 us  [the longest x2 4.42 us: per_device(): lax.ppermute(token_slots[-1], 'ctx', [(i, i + 1) for i in range(slot - 1,...]
    ppermute x28 -> x32, waiting for transfers between devices: 116 us -> 81.8 us  [head_move(): return lax.ppermute(value, 'head', xor_pairs(lax.axis_size('head'), step))]
    all_gather x4 -> x2, waiting for transfers between devices: 31.9 us -> 0.02 us  [gather_rows(): return lax.all_gather(unit, ('dp', 'ctx'), axis=0, tiled=True)]
    pallas_call x20 -> x23, Pallas kernels: 158 us -> 176 us  [call(): pl.pallas_call(body, out_shape=list(outs), in_specs=in_specs, out_specs=o...]
    ppermute x6 -> x8, starting transfers between devices: 10.2 us -> 20.6 us  [the longest x2 6.59 us: per_device(): lax.ppermute(sent, 'ctx', [(i, i - 1) for i in range(1, n_ctx + 1 - slot)])]
    reduce_scatter x3 -> x4, waiting for transfers between devices: 0.02 us -> 9.4 us  [scatter_rows(): return lax.psum_scatter(sums, 'ctx', scatter_dimension=0, tiled=True)]
    unnamed x95 -> x106, local copies, waits for them, and re-layouts: 15 us -> 9.83 us
    ppermute x28 -> x32, starting transfers between devices: 32.7 us -> 36.8 us  [head_move(): return lax.ppermute(value, 'head', xor_pairs(lax.axis_size('head'), step))]
  transfers between devices with their start and end apart: 46 -> 54, of which waited for: 22 -> 22; matrix products, arithmetic and copies ran while one was open for 6% -> 8% of each run, Pallas kernels for 29% -> 46%
where the time goes in v2:
time: 455 us; the launch traced here: 448 us
  Pallas kernels  220 us (48%)
  waiting for transfers between devices  102 us (22%)
  starting transfers between devices  58.5 us (13%)
  other arithmetic  30.7 us (7%)
  local copies, waits for them, and re-layouts  19.6 us (4%)
  between operations  17.8 us (4%)
    pallas_call x23, Pallas kernels, call(): pl.pallas_call(body, out_shape=list(outs), in_specs=in_specs, out_specs=o...  176 us
    ppermute x32, waiting for transfers between devices, head_move(): return lax.ppermute(value, 'head', xor_pairs(lax.axis_size('head'), step))  81.8 us
    pallas_call x6, Pallas kernels, outer_kernel(): pl.pallas_call(body, out_shape=[shape((half, w), BF16) for w in widths] i...  39 us
    ppermute x32, starting transfers between devices, head_move(): return lax.ppermute(value, 'head', xor_pairs(lax.axis_size('head'), step))  36.8 us
    unnamed x106, local copies, waits for them, and re-layouts  9.83 us
    reduce_scatter x4, waiting for transfers between devices, scatter_rows(): return lax.psum_scatter(sums, 'ctx', scatter_dimension=0, tiled=True)  9.4 us
  transfers between devices with their start and end apart: 54, of which 22 were waited for; matrix products, arithmetic and copies ran while one was open for 8% of the time, Pallas kernels for 46%

profile of v2, /device:TPU:16, one launch (start us, length us, event | category | flops | bytes accessed | tf_op | source)
XLA Modules:
  0.0 448.1 jit_solution(2026093157736965238)
XLA Ops:
  19.2 5.6 %convert_reduce_fusion = (s32[768]{0:T(1024)}, s32[768]{0:T(1024)S(1)}, s32[768]{0:T(1024)S(1)}, s32[768]{0:T(1024)}, s32[768]{0:T(1024)S(1)}) fusion(s32[3072]{0:T(1024)S(1)} %copy-done.42, s32[768]{0:T(1024)S(1)} %get-tuple-element.185, s32[768]{0:T(1024)S(1)} %get-tuple-element.184, s32[768]{0:T(1024)S(1)} %get-tuple-element.183, ...), kind=kLoop, calls=%fused_computation | loop fusion | flops 35385600 | bytes 43008 | tf_op jit(solution)/shard_map/reduce_sum | solution.py:853
  24.8 5.9 %fusion.5 = (f32[768,128]{1,0:T(8,128)}, f32[768,128]{1,0:T(8,128)}, f32[768,128]{1,0:T(8,128)}, f32[768,128]{1,0:T(8,128)}, f32[768,128]{1,0:T(8,128)}, /*index=5*/f32[768,128]{1,0:T(8,128)}) fusion(f32[768]{0:T(1024)S(1)} %get-tuple-element.205, f32[128]{0:T(128)S(1)} %get-tuple-element.203, f32[128]{0:T(128)S(1)} %get-tuple-element.204, ...), kind=kLoop, calls=%fused_computation.21 | loop fusion | flops 589824 | bytes 2369536 | tf_op jit(solution)/shard_map/mul | solution.py:858
  31.3 8.4 %collective-permute-done.1.refs_2_ = bf16[768,384]{1,0:T(8,128)(2,1)S(1)} collective-permute-done((bf16[768,384]{1,0:T(8,128)(2,1)S(1)}, bf16[768,384]{1,0:T(8,128)(2,1)S(1)}, u32[]{:S(2)}, u32[]{:S(2)}) %collective-permute-start.1) | collective-permute-done | bytes 589856 | tf_op jit(solution)/shard_map/ppermute | solution.py:81
  41.3 5.4 %norm_in.3 = (bf16[768,1536]{1,0:T(8,128)(2,1)}, bf16[768,1536]{1,0:T(8,128)(2,1)}, f32[768,1]{1,0:T(8,128)}) custom-call(s32[2]{0:T(128)} %pad_add_fusion.spot_ref.at_ref, f32[1,1536]{1,0:T(1,128)} %broadcast_in_dim.30.gain_ref.refs_6_, bf16[768,384]{1,0:T(8,128)(2,1)} %refs_0_.1, bf16[768,384]{1,0:T(8,128)(2,1)} %copy-done.28, ...), custom_call_target="tpu_custom_call" | custom-call | flops 1 | bytes 1 | tf_op jit(solution)/shard_map/norm_in/pallas_call | solution.py:57
  57.1 6.0 %collective-permute-done.3.refs_1_ = bf16[768,384]{1,0:T(8,128)(2,1)S(1)} collective-permute-done((bf16[768,384]{1,0:T(8,128)(2,1)S(1)}, bf16[768,384]{1,0:T(8,128)(2,1)S(1)}, u32[]{:S(2)}, u32[]{:S(2)}) %collective-permute-start.3) | collective-permute-done | bytes 589856 | tf_op jit(solution)/shard_map/ppermute | solution.py:81
  65.1 10.2 %collective-permute-done.4.refs_2_ = bf16[768,384]{1,0:T(8,128)(2,1)S(1)} collective-permute-done((bf16[768,384]{1,0:T(8,128)(2,1)S(1)}, bf16[768,384]{1,0:T(8,128)(2,1)S(1)}, u32[]{:S(2)}, u32[]{:S(2)}) %collective-permute-start.4) | collective-permute-done | bytes 589856 | tf_op jit(solution)/shard_map/ppermute | solution.py:81
  82.3 7.1 %project.3 = (bf16[768,768]{1,0:T(8,128)(2,1)}, bf16[768,384]{1,0:T(8,128)(2,1)}) custom-call(bf16[768,1536]{1,0:T(8,128)(2,1)} %get-tuple-element.90.x_ref.refs_1_, bf16[1536,1536]{1,0:T(8,128)(2,1)} %all-gather.3.cloned.1.call-done.weight_ref.refs_2_.refs_3_, f32[768,128]{1,0:T(8,128)} %get-tuple-element.201.cos_ref, f32[768,128]{1,0:T(8,128)} %get-tuple-element.202.sin_ref), custom_call_target="tpu_custom_call" | custom-call | flops 1 | bytes 1 | tf_op jit(solution)/shard_map/project/pallas_call | solution.py:57
  90.0 10.1 %attend_0.1 = (f32[768,768]{1,0:T(8,128)}, f32[24,768]{1,0:T(8,128)}) custom-call(s32[3]{0:T(128)} %pad_add_fusion.1.meta_ref, f32[1,1]{1,0:T(1,128)} %bitcast.3.lam_ref, bf16[768,384]{1,0:T(8,128)(2,1)} %get-tuple-element.122.q_ref, bf16[768,768]{1,0:T(8,128)(2,1)} %get-tuple-element.94.k_ref.v_ref, bf16[768,768]{1,0:T(8,128)(2,1)} %get-tuple-element.94.k_ref.v_ref, ...), custom_call_target="tpu_custom_call" | custom-call | flops 1 | bytes 1 | tf_op jit(solution)/shard_map/attend_0/pallas_call | solution.py:57
  108.6 6.1 %project.4.k_ref.v_ref = bf16[768,768]{1,0:T(8,128)(2,1)} custom-call(bf16[768,1536]{1,0:T(8,128)(2,1)} %norm_in.4.x_ref, bf16[1536,1536]{1,0:T(8,128)(2,1)} %all-gather.3.cloned.1.call-done.weight_ref.refs_2_.refs_3_, f32[768,128]{1,0:T(8,128)} %get-tuple-element.199.cos_ref, f32[768,128]{1,0:T(8,128)} %get-tuple-element.200.sin_ref), custom_call_target="tpu_custom_call" | custom-call | flops 1 | bytes 1 | tf_op jit(solution)/shard_map/project/pallas_call | solution.py:57
  114.7 11.6 %attend_1.1 = (f32[768,768]{1,0:T(8,128)}, f32[24,768]{1,0:T(8,128)}) custom-call(s32[3]{0:T(128)} %pad_add_fusion.1.meta_ref, f32[1,1]{1,0:T(1,128)} %bitcast.3.lam_ref, bf16[768,384]{1,0:T(8,128)(2,1)} %get-tuple-element.122.q_ref, bf16[768,768]{1,0:T(8,128)(2,1)} %project.4.k_ref.v_ref, bf16[768,768]{1,0:T(8,128)(2,1)} %project.4.k_ref.v_ref, ...), custom_call_target="tpu_custom_call" | custom-call | flops 1 | bytes 1 | tf_op jit(solution)/shard_map/attend_1/pallas_call | solution.py:57
  135.9 6.1 %project.5.k_ref.v_ref = bf16[768,768]{1,0:T(8,128)(2,1)} custom-call(bf16[768,1536]{1,0:T(8,128)(2,1)} %norm_in.5.x_ref, bf16[1536,1536]{1,0:T(8,128)(2,1)} %all-gather.3.cloned.1.call-done.weight_ref.refs_2_.refs_3_, f32[768,128]{1,0:T(8,128)} %get-tuple-element.188.cos_ref, f32[768,128]{1,0:T(8,128)} %get-tuple-element.187.sin_ref), custom_call_target="tpu_custom_call" | custom-call | flops 1 | bytes 1 | tf_op jit(solution)/shard_map/project/pallas_call | solution.py:57
  142.0 5.4 %attend_2.1 = (bf16[768,384]{1,0:T(8,128)(2,1)}, f32[384,768]{1,0:T(8,128)}, f32[384,768]{1,0:T(8,128)}, f32[24,768]{1,0:T(8,128)}) custom-call(s32[3]{0:T(128)} %pad_add_fusion.1.meta_ref, f32[1,1]{1,0:T(1,128)} %bitcast.3.lam_ref, bf16[768,384]{1,0:T(8,128)(2,1)} %get-tuple-element.122.q_ref, bf16[768,768]{1,0:T(8,128)(2,1)} %project.5.k_ref.v_ref, ...), custom_call_target="tpu_custom_call" | custom-call | flops 1 | bytes 1 | tf_op jit(solution)/shard_map/attend_2/pallas_call | solution.py:57
  151.1 6.4 %collective-permute-done.19.refs_7_ = bf16[768,384]{1,0:T(8,128)(2,1)S(1)} collective-permute-done((bf16[768,384]{1,0:T(8,128)(2,1)S(1)}, bf16[768,384]{1,0:T(8,128)(2,1)S(1)}, u32[]{:S(2)}, u32[]{:S(2)}) %collective-permute-start.19) | collective-permute-done | bytes 589856 | tf_op jit(solution)/shard_map/ppermute | solution.py:81
  157.5 10.1 %collective-permute-done.14.refs_1_ = bf16[768,384]{1,0:T(8,128)(2,1)S(1)} collective-permute-done((bf16[768,384]{1,0:T(8,128)(2,1)}, bf16[768,384]{1,0:T(8,128)(2,1)S(1)}, u32[]{:S(2)}, u32[]{:S(2)}) %collective-permute-start.14) | collective-permute-done | bytes 589856 | tf_op jit(solution)/shard_map/ppermute | solution.py:81
  167.6 8.0 %collective-permute-done.15.refs_2_ = bf16[768,384]{1,0:T(8,128)(2,1)S(1)} collective-permute-done((bf16[768,384]{1,0:T(8,128)(2,1)}, bf16[768,384]{1,0:T(8,128)(2,1)S(1)}, u32[]{:S(2)}, u32[]{:S(2)}) %collective-permute-start.15) | collective-permute-done | bytes 589856 | tf_op jit(solution)/shard_map/ppermute | solution.py:81
  179.0 10.6 %middle.1 = (f32[768,1536]{1,0:T(8,128)}, bf16[768,1536]{1,0:T(8,128)(2,1)}, f32[768,1]{1,0:T(8,128)}) custom-call(s32[2]{0:T(128)} %pad_add_fusion.spot_ref.at_ref, bf16[768,1536]{1,0:T(8,128)(2,1)} %get-tuple-element.89.x_ref.refs_4_, f32[1,1536]{1,0:T(1,128)} %broadcast_in_dim.33.gain_ref, bf16[768,384]{1,0:T(8,128)(2,1)} %get-tuple-element.103.refs_0_.refs_2_, ...), custom_call_target="tpu_custom_call" | custom-call | flops 1 | bytes 1 | tf_op jit(solution)/shard_map/middle/pallas_call | solution.py:57
  189.6 13.0 %ffn.1 = (bf16[768,1024]{1,0:T(8,128)(2,1)}, bf16[768,1024]{1,0:T(8,128)(2,1)}, bf16[768,1024]{1,0:T(8,128)(2,1)}) custom-call(bf16[768,1536]{1,0:T(8,128)(2,1)} %get-tuple-element.110.x_ref.refs_0_, bf16[768,1536]{1,0:T(8,128)(2,1)} %place_cols.1.dy_ref.refs_0_, bf16[1536,3072]{1,0:T(8,128)(2,1)} %all-gather.5.cloned.1.call-done.gate_w.up_w.down_w.g_ref.u_ref.refs_1_, ...), custom_call_target="tpu_custom_call" | custom-call | flops 1 | bytes 1 | tf_op jit(solution)/shard_map/ffn/pallas_call | solution.py:57
  206.1 11.3 %mid_back.1 = (bf16[192,1536]{1,0:T(8,128)(2,1)}, bf16[192,1536]{1,0:T(8,128)(2,1)}, bf16[192,1536]{1,0:T(8,128)(2,1)}, bf16[192,1536]{1,0:T(8,128)(2,1)}) custom-call(s32[2]{0:T(128)} %pad_add_fusion.spot_ref.at_ref, bf16[768,1024]{1,0:T(8,128)(2,1)} %get-tuple-element.111.dgate_ref.refs_1_, bf16[768,1024]{1,0:T(8,128)(2,1)} %get-tuple-element.112.dup_ref.refs_2_, ...), custom_call_target="tpu_custom_call" | custom-call | flops 1 | bytes 1 | tf_op jit(solution)/shard_map/mid_back/pallas_call | solution.py:57
  228.6 7.9 %down.1 = (bf16[768,384]{1,0:T(8,128)(2,1)}, bf16[768,384]{1,0:T(8,128)(2,1)}, bf16[768,384]{1,0:T(8,128)(2,1)}, bf16[768,384]{1,0:T(8,128)(2,1)}) custom-call(s32[2]{0:T(128)} %pad_add_fusion.spot_ref.at_ref, bf16[768,1024]{1,0:T(8,128)(2,1)} %get-tuple-element.115.refs_1_.refs_0_, ...), custom_call_target="tpu_custom_call" | custom-call | flops 999999995904 | bytes 1 | tf_op jit(solution)/shard_map/down/pallas_call | solution.py:57
  241.3 6.9 %gu_grads_theirs.1 = bf16[768,2048]{1,0:T(8,128)(2,1)} custom-call(s32[1]{0:T(128)S(6)} %sub.44.side_ref, bf16[768,1536]{1,0:T(8,128)(2,1)} %get-tuple-element.110.x_ref.refs_0_, bf16[768,1024]{1,0:T(8,128)(2,1)} %get-tuple-element.111.dgate_ref.refs_1_, bf16[768,1024]{1,0:T(8,128)(2,1)} %get-tuple-element.112.dup_ref.refs_2_), custom_call_target="tpu_custom_call" | custom-call | flops 1 | bytes 1 | tf_op jit(solution)/shard_map/gu_grads_theirs/pallas_call | solution.py:789
  261.4 7.6 %gu_grads.1 = (bf16[768,1024]{1,0:T(8,128)(2,1)}, bf16[768,1024]{1,0:T(8,128)(2,1)}) custom-call(s32[1]{0:T(128)} %bitcast.1.side_ref, bf16[768,1536]{1,0:T(8,128)(2,1)} %get-tuple-element.110.x_ref.refs_0_, bf16[768,1024]{1,0:T(8,128)(2,1)} %get-tuple-element.111.dgate_ref.refs_1_, bf16[768,1024]{1,0:T(8,128)(2,1)} %get-tuple-element.112.dup_ref.refs_2_, ...), custom_call_target="tpu_custom_call" | custom-call | flops 1 | bytes 1 | tf_op jit(solution)/shard_map/gu_grads/pallas_call | solution.py:789
  269.0 5.9 %reduce-scatter.5.cloned.1.call-done = bf16[192,1024]{1,0:T(8,128)(2,1)} async-done(((bf16[768,1024]{1,0:T(8,128)(2,1)}), bf16[192,1024]{1,0:T(8,128)(2,1)}) %reduce-scatter.5.cloned.1.call-update) | async-done | bytes 393232 | tf_op jit(solution)/shard_map/reduce_scatter | solution.py:115
  275.0 9.3 %collective-permute-done.31.refs_2_ = bf16[192,1536]{1,0:T(8,128)(2,1)S(1)} collective-permute-done((bf16[192,1536]{1,0:T(8,128)(2,1)}, bf16[192,1536]{1,0:T(8,128)(2,1)S(1)}, u32[]{:S(2)}, u32[]{:S(2)}) %collective-permute-start.31) | collective-permute-done | bytes 589856 | tf_op jit(solution)/shard_map/ppermute | solution.py:81
  289.1 6.3 %head_back.1 = (bf16[432,768]{1,0:T(8,128)(2,1)}, f32[384,128]{1,0:T(8,128)}) custom-call(f32[1,1]{1,0:T(1,128)} %bitcast.3.lam_ref, bf16[768,1536]{1,0:T(8,128)(2,1)} %place_rows.1.b_ref.refs_0_, bf16[1536,1536]{1,0:T(8,128)(2,1)} %all-gather.3.cloned.1.call-done.weight_ref.refs_2_.refs_3_, f32[384,768]{1,0:T(8,128)} %get-tuple-element.129.unit_ref, ...), custom_call_target="tpu_custom_call" | custom-call | flops 1 | bytes 1 | tf_op jit(solution)/shard_map/head_back/pallas_call | solution.py:57
  302.9 12.9 %attend_back_qk0.1 = (f32[768,384]{1,0:T(8,128)}, f32[768,768]{1,0:T(8,128)}) custom-call(s32[3]{0:T(128)} %pad_add_fusion.1.meta_ref, f32[1,1]{1,0:T(1,128)} %bitcast.3.lam_ref, bf16[768,384]{1,0:T(8,128)(2,1)} %get-tuple-element.122.q_ref, bf16[768,768]{1,0:T(8,128)(2,1)} %get-tuple-element.94.k_ref.v_ref, bf16[768,768]{1,0:T(8,128)(2,1)} %get-tuple-element.94.k_ref.v_ref, ...), custom_call_target="tpu_custom_call" | custom-call | flops 1 | bytes 1 | tf_op jit(solution)/shard_map/attend_back_qk0/pallas_call | solution.py:57
  325.8 12.2 %attend_back_q1.1.refs_3_.refs_0_ = bf16[768,384]{1,0:T(8,128)(2,1)} custom-call(s32[3]{0:T(128)} %pad_add_fusion.1.meta_ref, f32[1,1]{1,0:T(1,128)} %bitcast.3.lam_ref, bf16[768,384]{1,0:T(8,128)(2,1)} %get-tuple-element.122.q_ref, bf16[768,768]{1,0:T(8,128)(2,1)} %project.4.k_ref.v_ref, bf16[768,768]{1,0:T(8,128)(2,1)} %project.4.k_ref.v_ref, ...), custom_call_target="tpu_custom_call" | custom-call | flops 1 | bytes 1 | tf_op jit(solution)/shard_map/attend_back_q1/pallas_call | solution.py:57
  341.2 11.8 %attend_back_k1.1.refs_0_ = f32[768,768]{1,0:T(8,128)} custom-call(s32[3]{0:T(128)} %pad_add_fusion.4.meta_ref, f32[1,1]{1,0:T(1,128)} %bitcast.3.lam_ref, bf16[768,384]{1,0:T(8,128)(2,1)} %collective-permute-done.26.q_ref, bf16[768,768]{1,0:T(8,128)(2,1)} %get-tuple-element.94.k_ref.v_ref, bf16[768,768]{1,0:T(8,128)(2,1)} %get-tuple-element.94.k_ref.v_ref, ...), custom_call_target="tpu_custom_call" | custom-call | flops 1 | bytes 1 | tf_op jit(solution)/shard_map/attend_back_k1/pallas_call | solution.py:57
  355.0 5.6 %attend_back_k2.1.refs_4_.refs_1_ = bf16[768,768]{1,0:T(8,128)(2,1)} custom-call(s32[3]{0:T(128)} %pad_add_fusion.3.meta_ref, f32[1,1]{1,0:T(1,128)} %bitcast.3.lam_ref, bf16[768,384]{1,0:T(8,128)(2,1)} %collective-permute-done.27.q_ref, bf16[768,768]{1,0:T(8,128)(2,1)} %get-tuple-element.94.k_ref.v_ref, bf16[768,768]{1,0:T(8,128)(2,1)} %get-tuple-element.94.k_ref.v_ref, ...), custom_call_target="tpu_custom_call" | custom-call | flops 1 | bytes 1 | tf_op jit(solution)/shard_map/attend_back_k2/pallas_call | solution.py:57
  360.6 7.5 %oqkv_grads_theirs.1 = bf16[768,1536]{1,0:T(8,128)(2,1)} custom-call(s32[1]{0:T(128)S(6)} %sub.44.side_ref, bf16[768,1536]{1,0:T(8,128)(2,1)} %place_rows.1.b_ref.refs_0_, bf16[768,1536]{1,0:T(8,128)(2,1)} %get-tuple-element.90.x_ref.refs_1_, bf16[768,384]{1,0:T(8,128)(2,1)} %get-tuple-element.103.refs_0_.refs_2_, ...), custom_call_target="tpu_custom_call" | custom-call | flops 1 | bytes 1 | tf_op jit(solution)/shard_map/oqkv_grads_theirs/pallas_call | solution.py:789
  368.1 9.7 %in_back.1 = (bf16[784,384]{1,0:T(8,128)(2,1)}, bf16[784,384]{1,0:T(8,128)(2,1)}, bf16[784,384]{1,0:T(8,128)(2,1)}, bf16[784,384]{1,0:T(8,128)(2,1)}, f32[1,1536]{1,0:T(1,128)}) custom-call(s32[2]{0:T(128)} %pad_add_fusion.spot_ref.at_ref, bf16[768,384]{1,0:T(8,128)(2,1)} %attend_back_q1.1.refs_3_.refs_0_, bf16[768,768]{1,0:T(8,128)(2,1)} %attend_back_k2.1.refs_4_.refs_1_, ...), custom_call_target="tpu_custom_call" | custom-call | flops 1 | bytes 1 | tf_op jit(solution)/shard_map/in_back/pallas_call | solution.py:57
  379.2 7.9 %oqkv_grads.1 = bf16[768,1536]{1,0:T(8,128)(2,1)} custom-call(s32[1]{0:T(128)} %bitcast.1.side_ref, bf16[768,1536]{1,0:T(8,128)(2,1)} %place_rows.1.b_ref.refs_0_, bf16[768,1536]{1,0:T(8,128)(2,1)} %get-tuple-element.90.x_ref.refs_1_, bf16[768,384]{1,0:T(8,128)(2,1)} %get-tuple-element.103.refs_0_.refs_2_, bf16[768,384]{1,0:T(8,128)(2,1)} %attend_back_q1.1.refs_3_.refs_0_, ...), custom_call_target="tpu_custom_call" | custom-call | flops 1 | bytes 1 | tf_op jit(solution)/shard_map/oqkv_grads/pallas_call | solution.py:789
  407.6 12.0 %collective-permute-done.39 = bf16[784,384]{1,0:T(8,128)(2,1)S(1)} collective-permute-done((bf16[784,384]{1,0:T(8,128)(2,1)}, bf16[784,384]{1,0:T(8,128)(2,1)S(1)}, u32[]{:S(2)}, u32[]{:S(2)}) %collective-permute-start.39) | collective-permute-done | bytes 602144 | tf_op jit(solution)/shard_map/ppermute | solution.py:81
  (274 shorter events, 159.7 us)
Async XLA Ops:
  7.2 75.1 %all-gather.3.cloned.1.call-start = ((), (), s32[]{:S(2)}) async-start(), calls=%async_computation.4 | async-start | bytes 5308416 | tf_op jit(solution)/shard_map/all_gather | solution.py:111
  9.4 180.2 %all-gather.5.cloned.1.call-start = ((), (), s32[]{:S(2)}) async-start(), calls=%async_computation.5 | async-start | bytes 10616832 | tf_op jit(solution)/shard_map/all_gather | solution.py:111
  10.6 264.3 %reduce-scatter.5.cloned.1.call-start = ((), (), s32[]{:S(2)}) async-start(), calls=%async_computation.6 | async-start | bytes 1966080 | tf_op jit(solution)/shard_map/reduce_scatter | solution.py:115
  12.3 27.4 %collective-permute-start.1 = (bf16[768,384]{1,0:T(8,128)(2,1)S(1)}, bf16[768,384]{1,0:T(8,128)(2,1)S(1)}, u32[]{:S(2)}, u32[]{:S(2)}) collective-permute-start(bf16[768,384]{1,0:T(8,128)(2,1)S(1)} %copy-done.2), channel_id=1, source_target_pairs={{0,2},{1,3},{2,0},{3,1},{4,6},{5,7},{6,4},{7,5},{8,10},{9,11},{10,... | collective-permute-start | bytes 1769480 | tf_op jit(solution)/shard_map/ppermute | solution.py:81
  13.8 25.9 %collective-permute-start.2 = (bf16[768,384]{1,0:T(8,128)(2,1)S(1)}, bf16[768,384]{1,0:T(8,128)(2,1)S(1)}, u32[]{:S(2)}, u32[]{:S(2)}) collective-permute-start(bf16[768,384]{1,0:T(8,128)(2,1)S(1)} %copy-done.2), channel_id=1, source_target_pairs={{0,3},{1,2},{2,1},{3,0},{4,7},{5,6},{6,5},{7,4},{8,11},{9,10},{10,... | collective-permute-start | bytes 1769480 | tf_op jit(solution)/shard_map/ppermute | solution.py:81
  14.3 40.5 %collective-permute-start.6 = (bf16[768,384]{1,0:T(8,128)(2,1)S(1)}, bf16[768,384]{1,0:T(8,128)(2,1)S(1)}, u32[]{:S(2)}, u32[]{:S(2)}) collective-permute-start(bf16[768,384]{1,0:T(8,128)(2,1)S(1)} %copy-done.2), channel_id=1, source_target_pairs={{0,4},{4,8},{8,12},{1,5},{5,9},{9,13},{2,6},{6,10},{10,14},{3,7},{... | collective-permute-start | bytes 1769480 | tf_op jit(solution)/shard_map/ppermute | solution.py:873
  47.2 28.1 %collective-permute-start.4 = (bf16[768,384]{1,0:T(8,128)(2,1)S(1)}, bf16[768,384]{1,0:T(8,128)(2,1)S(1)}, u32[]{:S(2)}, u32[]{:S(2)}) collective-permute-start(bf16[768,384]{1,0:T(8,128)(2,1)S(1)} %copy-done.11), channel_id=1, source_target_pairs={{0,2},{1,3},{2,0},{3,1},{4,6},{5,7},{6,4},{7,5},{8,10},{9,11},{10,... | collective-permute-start | bytes 1769480 | tf_op jit(solution)/shard_map/ppermute | solution.py:81
  48.8 29.2 %collective-permute-start.5 = (bf16[768,384]{1,0:T(8,128)(2,1)S(1)}, bf16[768,384]{1,0:T(8,128)(2,1)S(1)}, u32[]{:S(2)}, u32[]{:S(2)}) collective-permute-start(bf16[768,384]{1,0:T(8,128)(2,1)S(1)} %copy-done.11), channel_id=1, source_target_pairs={{0,3},{1,2},{2,1},{3,0},{4,7},{5,6},{6,5},{7,4},{8,11},{9,10},{10,... | collective-permute-start | bytes 1769480 | tf_op jit(solution)/shard_map/ppermute | solution.py:81
  54.7 45.4 %collective-permute-start.7 = (bf16[768,384]{1,0:T(8,128)(2,1)S(1)}, bf16[768,384]{1,0:T(8,128)(2,1)}, u32[]{:S(2)}, u32[]{:S(2)}) collective-permute-start(bf16[768,384]{1,0:T(8,128)(2,1)S(1)} %collective-permute-done.6.refs_0_), channel_id=1, source_target_pairs={{4,8},{8,12},{5,9},{9,13},{6,10},{10,14},{7,11},{11,15},{20,24},{2... | collective-permute-start | bytes 1769480 | tf_op jit(solution)/shard_map/ppermute | solution.py:873
  63.1 37.1 %collective-permute-start.8 = (bf16[768,384]{1,0:T(8,128)(2,1)S(1)}, bf16[768,384]{1,0:T(8,128)(2,1)S(1)}, u32[]{:S(2)}, u32[]{:S(2)}) collective-permute-start(bf16[768,384]{1,0:T(8,128)(2,1)S(1)} %collective-permute-done.6.refs_0_), channel_id=1, source_target_pairs={{0,1},{1,0},{2,3},{3,2},{4,5},{5,4},{6,7},{7,6},{8,9},{9,8},{10,11... | collective-permute-start | bytes 1769480 | tf_op jit(solution)/shard_map/ppermute | solution.py:81
  63.5 36.7 %collective-permute-start.9 = (bf16[768,384]{1,0:T(8,128)(2,1)S(1)}, bf16[768,384]{1,0:T(8,128)(2,1)}, u32[]{:S(2)}, u32[]{:S(2)}) collective-permute-start(bf16[768,384]{1,0:T(8,128)(2,1)S(1)} %collective-permute-done.6.refs_0_), channel_id=1, source_target_pairs={{0,2},{1,3},{2,0},{3,1},{4,6},{5,7},{6,4},{7,5},{8,10},{9,11},{10,... | collective-permute-start | bytes 1769480 | tf_op jit(solution)/shard_map/ppermute | solution.py:81
  75.3 24.9 %collective-permute-start.10 = (bf16[768,384]{1,0:T(8,128)(2,1)S(1)}, bf16[768,384]{1,0:T(8,128)(2,1)}, u32[]{:S(2)}, u32[]{:S(2)}) collective-permute-start(bf16[768,384]{1,0:T(8,128)(2,1)S(1)} %collective-permute-done.6.refs_0_), channel_id=1, source_target_pairs={{0,3},{1,2},{2,1},{3,0},{4,7},{5,6},{6,5},{7,4},{8,11},{9,10},{10,... | collective-permute-start | bytes 1769480 | tf_op jit(solution)/shard_map/ppermute | solution.py:81
  100.2 27.2 %collective-permute-start.11 = (bf16[768,384]{1,0:T(8,128)(2,1)}, bf16[768,384]{1,0:T(8,128)(2,1)S(1)}, u32[]{:S(2)}, u32[]{:S(2)}) collective-permute-start(bf16[768,384]{1,0:T(8,128)(2,1)} %collective-permute-done.7.refs_0_), channel_id=1, source_target_pairs={{0,1},{1,0},{2,3},{3,2},{4,5},{5,4},{6,7},{7,6},{8,9},{9,8},{10,11... | collective-permute-start | bytes 1769480 | tf_op jit(solution)/shard_map/ppermute | solution.py:81
  100.7 26.8 %collective-permute-start.12 = (bf16[768,384]{1,0:T(8,128)(2,1)}, bf16[768,384]{1,0:T(8,128)(2,1)S(1)}, u32[]{:S(2)}, u32[]{:S(2)}) collective-permute-start(bf16[768,384]{1,0:T(8,128)(2,1)} %collective-permute-done.7.refs_0_), channel_id=1, source_target_pairs={{0,2},{1,3},{2,0},{3,1},{4,6},{5,7},{6,4},{7,5},{8,10},{9,11},{10,... | collective-permute-start | bytes 1769480 | tf_op jit(solution)/shard_map/ppermute | solution.py:81
  103.7 23.8 %collective-permute-start.13 = (bf16[768,384]{1,0:T(8,128)(2,1)}, bf16[768,384]{1,0:T(8,128)(2,1)S(1)}, u32[]{:S(2)}, u32[]{:S(2)}) collective-permute-start(bf16[768,384]{1,0:T(8,128)(2,1)} %collective-permute-done.7.refs_0_), channel_id=1, source_target_pairs={{0,3},{1,2},{2,1},{3,0},{4,7},{5,6},{6,5},{7,4},{8,11},{9,10},{10,... | collective-permute-start | bytes 1769480 | tf_op jit(solution)/shard_map/ppermute | solution.py:81
  131.1 26.4 %collective-permute-start.19 = (bf16[768,384]{1,0:T(8,128)(2,1)S(1)}, bf16[768,384]{1,0:T(8,128)(2,1)S(1)}, u32[]{:S(2)}, u32[]{:S(2)}) collective-permute-start(bf16[768,384]{1,0:T(8,128)(2,1)S(1)} %constant_dynamic-slice_fusion.refs_4_), channel_id=1, source_target_pairs={{0,3},{1,2},{2,1},{3,0},{4,7},{5,6},{6,5},{7,4},{8,11},{9,10},{10,... | collective-permute-start | bytes 1769480 | tf_op jit(solution)/shard_map/ppermute | solution.py:81
  148.9 26.6 %collective-permute-start.15 = (bf16[768,384]{1,0:T(8,128)(2,1)}, bf16[768,384]{1,0:T(8,128)(2,1)S(1)}, u32[]{:S(2)}, u32[]{:S(2)}) collective-permute-start(bf16[768,384]{1,0:T(8,128)(2,1)} %get-tuple-element.103.refs_0_.refs_2_), channel_id=1, source_target_pairs={{0,2},{1,3},{2,0},{3,1},{4,6},{5,7},{6,4},{7,5},{8,10},{9,11},{10,... | collective-permute-start | bytes 1769480 | tf_op jit(solution)/shard_map/ppermute | solution.py:81
  150.9 26.0 %collective-permute-start.16 = (bf16[768,384]{1,0:T(8,128)(2,1)}, bf16[768,384]{1,0:T(8,128)(2,1)S(1)}, u32[]{:S(2)}, u32[]{:S(2)}) collective-permute-start(bf16[768,384]{1,0:T(8,128)(2,1)} %get-tuple-element.103.refs_0_.refs_2_), channel_id=1, source_target_pairs={{0,3},{1,2},{2,1},{3,0},{4,7},{5,6},{6,5},{7,4},{8,11},{9,10},{10,... | collective-permute-start | bytes 1769480 | tf_op jit(solution)/shard_map/ppermute | solution.py:81
  151.0 25.9 %collective-permute-start.20 = (bf16[768,384]{1,0:T(8,128)(2,1)S(1)}, bf16[768,384]{1,0:T(8,128)(2,1)S(1)}, u32[]{:S(2)}, u32[]{:S(2)}) collective-permute-start(bf16[768,384]{1,0:T(8,128)(2,1)S(1)} %constant_dynamic-slice_fusion.refs_4_), channel_id=1, source_target_pairs={{0,16},{16,0},{1,17},{17,1},{2,18},{18,2},{3,19},{19,3},{4,20},{20... | collective-permute-start | bytes 1769480 | tf_op jit(solution)/shard_map/ppermute | solution.py:85
  222.0 26.2 %collective-permute-start.24 = (bf16[192,1536]{1,0:T(8,128)(2,1)}, bf16[192,1536]{1,0:T(8,128)(2,1)}, u32[]{:S(2)}, u32[]{:S(2)}) collective-permute-start(bf16[192,1536]{1,0:T(8,128)(2,1)} %get-tuple-element.119), channel_id=1, source_target_pairs={{0,1},{1,0},{2,3},{3,2},{4,5},{5,4},{6,7},{7,6},{8,9},{9,8},{10,11... | collective-permute-start | bytes 1769480 | tf_op jit(solution)/shard_map/ppermute | solution.py:81
  222.0 27.8 %collective-permute-start.28 = (bf16[192,1536]{1,0:T(8,128)(2,1)}, bf16[192,1536]{1,0:T(8,128)(2,1)}, u32[]{:S(2)}, u32[]{:S(2)}) collective-permute-start(bf16[192,1536]{1,0:T(8,128)(2,1)} %get-tuple-element.125), channel_id=1, source_target_pairs={{0,2},{1,3},{2,0},{3,1},{4,6},{5,7},{6,4},{7,5},{8,10},{9,11},{10,... | collective-permute-start | bytes 1769480 | tf_op jit(solution)/shard_map/ppermute | solution.py:81
  224.1 27.6 %collective-permute-start.29 = (bf16[192,1536]{1,0:T(8,128)(2,1)}, bf16[192,1536]{1,0:T(8,128)(2,1)}, u32[]{:S(2)}, u32[]{:S(2)}) collective-permute-start(bf16[192,1536]{1,0:T(8,128)(2,1)} %get-tuple-element.126), channel_id=1, source_target_pairs={{0,3},{1,2},{2,1},{3,0},{4,7},{5,6},{6,5},{7,4},{8,11},{9,10},{10,... | collective-permute-start | bytes 1769480 | tf_op jit(solution)/shard_map/ppermute | solution.py:81
  241.3 111.8 %reduce-scatter.7.cloned.1.call-start = ((), (), s32[]{:S(2)}) async-start(), calls=%async_computation.7 | async-start | bytes 1966080 | tf_op jit(solution)/shard_map/reduce_scatter | solution.py:115
  257.2 27.1 %collective-permute-start.31 = (bf16[192,1536]{1,0:T(8,128)(2,1)}, bf16[192,1536]{1,0:T(8,128)(2,1)S(1)}, u32[]{:S(2)}, u32[]{:S(2)}) collective-permute-start(bf16[192,1536]{1,0:T(8,128)(2,1)} %get-tuple-element.128.refs_0_), channel_id=1, source_target_pairs={{0,2},{1,3},{2,0},{3,1},{4,6},{5,7},{6,4},{7,5},{8,10},{9,11},{10,... | collective-permute-start | bytes 1769480 | tf_op jit(solution)/shard_map/ppermute | solution.py:81
  258.8 25.4 %collective-permute-start.32 = (bf16[192,1536]{1,0:T(8,128)(2,1)}, bf16[192,1536]{1,0:T(8,128)(2,1)S(1)}, u32[]{:S(2)}, u32[]{:S(2)}) collective-permute-start(bf16[192,1536]{1,0:T(8,128)(2,1)} %get-tuple-element.128.refs_0_), channel_id=1, source_target_pairs={{0,3},{1,2},{2,1},{3,0},{4,7},{5,6},{6,5},{7,4},{8,11},{9,10},{10,... | collective-permute-start | bytes 1769480 | tf_op jit(solution)/shard_map/ppermute | solution.py:81
  274.9 112.5 %reduce-scatter.9.cloned.1.call-start = ((), (), s32[]{:S(2)}) async-start(), calls=%async_computation.8 | async-start | bytes 1966080 | tf_op jit(solution)/shard_map/reduce_scatter | solution.py:115
  295.4 30.4 %collective-permute-start.33 = (bf16[432,768]{1,0:T(8,128)(2,1)}, bf16[432,768]{1,0:T(8,128)(2,1)S(1)}, u32[]{:S(2)}, u32[]{:S(2)}) collective-permute-start(bf16[432,768]{1,0:T(8,128)(2,1)} %get-tuple-element.132.grad_ref), channel_id=1, source_target_pairs={{4,0},{8,4},{12,8},{5,1},{9,5},{13,9},{6,2},{10,6},{14,10},{7,3},{... | collective-permute-start | bytes 1990664 | tf_op jit(solution)/shard_map/ppermute | solution.py:960
  299.0 24.8 %collective-permute-start.35 = (bf16[768,384]{1,0:T(8,128)(2,1)}, bf16[768,384]{1,0:T(8,128)(2,1)S(1)}, u32[]{:S(2)}, u32[]{:S(2)}) collective-permute-start(bf16[768,384]{1,0:T(8,128)(2,1)} %get-tuple-element.138), channel_id=1, source_target_pairs={{0,2},{1,3},{2,0},{3,1},{4,6},{5,7},{6,4},{7,5},{8,10},{9,11},{10,... | collective-permute-start | bytes 1769480 | tf_op jit(solution)/shard_map/ppermute | solution.py:81
  300.8 52.2 %collective-permute-start.37 = (bf16[432,768]{1,0:T(8,128)(2,1)}, bf16[432,768]{1,0:T(8,128)(2,1)S(1)}, u32[]{:S(2)}, u32[]{:S(2)}) collective-permute-start(bf16[432,768]{1,0:T(8,128)(2,1)} %get-tuple-element.132.grad_ref), channel_id=1, source_target_pairs={{8,0},{12,4},{9,1},{13,5},{10,2},{14,6},{11,3},{15,7},{24,16},{28,... | collective-permute-start | bytes 1990664 | tf_op jit(solution)/shard_map/ppermute | solution.py:960
  353.1 84.5 %reduce-scatter.11.cloned.1.call-start = ((), (), s32[]{:S(2)}) async-start(), calls=%async_computation.9 | async-start | bytes 2949120 | tf_op jit(solution)/shard_map/reduce_scatter | solution.py:115
  392.3 27.3 %collective-permute-start.39 = (bf16[784,384]{1,0:T(8,128)(2,1)}, bf16[784,384]{1,0:T(8,128)(2,1)S(1)}, u32[]{:S(2)}, u32[]{:S(2)}) collective-permute-start(bf16[784,384]{1,0:T(8,128)(2,1)} %get-tuple-element.150), channel_id=1, source_target_pairs={{0,2},{1,3},{2,0},{3,1},{4,6},{5,7},{6,4},{7,5},{8,10},{9,11},{10,... | collective-permute-start | bytes 1806344 | tf_op jit(solution)/shard_map/ppermute | solution.py:81
  393.0 26.6 %collective-permute-start.38 = (bf16[784,384]{1,0:T(8,128)(2,1)}, bf16[784,384]{1,0:T(8,128)(2,1)S(1)}, u32[]{:S(2)}, u32[]{:S(2)}) collective-permute-start(bf16[784,384]{1,0:T(8,128)(2,1)} %get-tuple-element.149), channel_id=1, source_target_pairs={{0,1},{1,0},{2,3},{3,2},{4,5},{5,4},{6,7},{7,6},{8,9},{9,8},{10,11... | collective-permute-start | bytes 1806344 | tf_op jit(solution)/shard_map/ppermute | solution.py:81
  (75 other events, 788.4 us)
Sparse Core Ops, SparseCore 0:
  10.2 62.8 all-gather.2
  74.7 94.9 all-gather.4
  241.4 33.4 reduce-scatter.4
  277.1 46.0 reduce-scatter.6
  353.2 34.1 reduce-scatter.8
  389.6 47.9 reduce-scatter.10

commit v3 on v2

--- a/solution.py
+++ b/solution.py
@@ -212,7 +212,7 @@
 
 def project_kernel(x, weight, width, more, cosine, sine):
     rows, wide = x.shape
-    tile = 256
+    tile = 384
 
     def body(x_ref, weight_ref, cos_ref, sin_ref, *outs):
         y = dot(x_ref[...], weight_ref[...], 1, 0)
@@ -476,7 +476,7 @@
     half = wide // 2
     count = len(heads_out)
     cols = heads_out[0].shape[1]
-    tile = 256
+    tile = 384
 
     def body(spot_ref, x_ref, gain_ref, *refs):
         ho, wm, wt = refs[:count], refs[count : 2 * count], refs[2 * count : 3 * count]

time: 455 us -> 455 us (level)
  waiting for transfers between devices: 102 us -> 110 us
  Pallas kernels: 220 us -> 213 us
    pallas_call x23, Pallas kernels: 176 us -> 170 us  [call(): pl.pallas_call(body, out_shape=list(outs), in_specs=in_specs, out_specs=o...]
    ppermute x32, waiting for transfers between devices: 81.8 us -> 86.8 us  [head_move(): return lax.ppermute(value, 'head', xor_pairs(lax.axis_size('head'), step))]
  transfers between devices with their start and end apart: 54 -> 54, of which waited for: 22 -> 25; matrix products, arithmetic and copies ran while one was open for 8% -> 8% of each run, Pallas kernels for 46% -> 44%
where the time goes in v3:
time: 455 us; the launch traced here: 447 us
  Pallas kernels  213 us (47%)
  waiting for transfers between devices  110 us (24%)
  starting transfers between devices  56.8 us (12%)
  other arithmetic  30.7 us (7%)
  local copies, waits for them, and re-layouts  18.5 us (4%)
  between operations  17.8 us (4%)
    pallas_call x23, Pallas kernels, call(): pl.pallas_call(body, out_shape=list(outs), in_specs=in_specs, out_specs=o...  170 us
    ppermute x32, waiting for transfers between devices, head_move(): return lax.ppermute(value, 'head', xor_pairs(lax.axis_size('head'), step))  86.8 us
    pallas_call x6, Pallas kernels, outer_kernel(): pl.pallas_call(body, out_shape=[shape((half, w), BF16) for w in widths] i...  39.1 us
    ppermute x32, starting transfers between devices, head_move(): return lax.ppermute(value, 'head', xor_pairs(lax.axis_size('head'), step))  36.8 us
    reduce_scatter x4, waiting for transfers between devices, scatter_rows(): return lax.psum_scatter(sums, 'ctx', scatter_dimension=0, tiled=True)  11.7 us
  transfers between devices with their start and end apart: 54, of which 25 were waited for; matrix products, arithmetic and copies ran while one was open for 8% of the time, Pallas kernels for 44%

profile of v3, /device:TPU:16, one launch (start us, length us, event | category | flops | bytes accessed | tf_op | source)
XLA Modules:
  0.0 447.5 jit_solution(12866838438007853118)
XLA Ops:
  19.2 5.6 %convert_reduce_fusion = (s32[768]{0:T(1024)}, s32[768]{0:T(1024)S(1)}, s32[768]{0:T(1024)S(1)}, s32[768]{0:T(1024)}, s32[768]{0:T(1024)S(1)}) fusion(s32[3072]{0:T(1024)S(1)} %copy-done.42, s32[768]{0:T(1024)S(1)} %get-tuple-element.185, s32[768]{0:T(1024)S(1)} %get-tuple-element.184, s32[768]{0:T(1024)S(1)} %get-tuple-element.183, ...), kind=kLoop, calls=%fused_computation | loop fusion | flops 35385600 | bytes 43008 | tf_op jit(solution)/shard_map/reduce_sum | solution.py:853
  24.8 5.9 %fusion.5 = (f32[768,128]{1,0:T(8,128)}, f32[768,128]{1,0:T(8,128)}, f32[768,128]{1,0:T(8,128)}, f32[768,128]{1,0:T(8,128)}, f32[768,128]{1,0:T(8,128)}, /*index=5*/f32[768,128]{1,0:T(8,128)}) fusion(f32[768]{0:T(1024)S(1)} %get-tuple-element.205, f32[128]{0:T(128)S(1)} %get-tuple-element.203, f32[128]{0:T(128)S(1)} %get-tuple-element.204, ...), kind=kLoop, calls=%fused_computation.21 | loop fusion | flops 589824 | bytes 2369536 | tf_op jit(solution)/shard_map/mul | solution.py:858
  31.3 8.4 %collective-permute-done.1.refs_2_ = bf16[768,384]{1,0:T(8,128)(2,1)S(1)} collective-permute-done((bf16[768,384]{1,0:T(8,128)(2,1)S(1)}, bf16[768,384]{1,0:T(8,128)(2,1)S(1)}, u32[]{:S(2)}, u32[]{:S(2)}) %collective-permute-start.1) | collective-permute-done | bytes 589856 | tf_op jit(solution)/shard_map/ppermute | solution.py:81
  41.3 5.4 %norm_in.3 = (bf16[768,1536]{1,0:T(8,128)(2,1)}, bf16[768,1536]{1,0:T(8,128)(2,1)}, f32[768,1]{1,0:T(8,128)}) custom-call(s32[2]{0:T(128)} %pad_add_fusion.spot_ref.at_ref, f32[1,1536]{1,0:T(1,128)} %broadcast_in_dim.30.gain_ref.refs_6_, bf16[768,384]{1,0:T(8,128)(2,1)} %refs_0_.1, bf16[768,384]{1,0:T(8,128)(2,1)} %copy-done.28, ...), custom_call_target="tpu_custom_call" | custom-call | flops 1 | bytes 1 | tf_op jit(solution)/shard_map/norm_in/pallas_call | solution.py:57
  56.9 6.2 %collective-permute-done.3.refs_1_ = bf16[768,384]{1,0:T(8,128)(2,1)S(1)} collective-permute-done((bf16[768,384]{1,0:T(8,128)(2,1)S(1)}, bf16[768,384]{1,0:T(8,128)(2,1)S(1)}, u32[]{:S(2)}, u32[]{:S(2)}) %collective-permute-start.3) | collective-permute-done | bytes 589856 | tf_op jit(solution)/shard_map/ppermute | solution.py:81
  65.1 10.2 %collective-permute-done.4.refs_2_ = bf16[768,384]{1,0:T(8,128)(2,1)S(1)} collective-permute-done((bf16[768,384]{1,0:T(8,128)(2,1)S(1)}, bf16[768,384]{1,0:T(8,128)(2,1)S(1)}, u32[]{:S(2)}, u32[]{:S(2)}) %collective-permute-start.4) | collective-permute-done | bytes 589856 | tf_op jit(solution)/shard_map/ppermute | solution.py:81
  82.3 7.4 %project.3 = (bf16[768,768]{1,0:T(8,128)(2,1)}, bf16[768,384]{1,0:T(8,128)(2,1)}) custom-call(bf16[768,1536]{1,0:T(8,128)(2,1)} %get-tuple-element.90.x_ref.refs_1_, bf16[1536,1536]{1,0:T(8,128)(2,1)} %all-gather.3.cloned.1.call-done.weight_ref.refs_2_.refs_3_, f32[768,128]{1,0:T(8,128)} %get-tuple-element.201.cos_ref, f32[768,128]{1,0:T(8,128)} %get-tuple-element.202.sin_ref), custom_call_target="tpu_custom_call" | custom-call | flops 1 | bytes 1 | tf_op jit(solution)/shard_map/project/pallas_call | solution.py:57
  90.3 10.1 %attend_0.1 = (f32[768,768]{1,0:T(8,128)}, f32[24,768]{1,0:T(8,128)}) custom-call(s32[3]{0:T(128)} %pad_add_fusion.1.meta_ref, f32[1,1]{1,0:T(1,128)} %bitcast.3.lam_ref, bf16[768,384]{1,0:T(8,128)(2,1)} %get-tuple-element.122.q_ref, bf16[768,768]{1,0:T(8,128)(2,1)} %get-tuple-element.94.k_ref.v_ref, bf16[768,768]{1,0:T(8,128)(2,1)} %get-tuple-element.94.k_ref.v_ref, ...), custom_call_target="tpu_custom_call" | custom-call | flops 1 | bytes 1 | tf_op jit(solution)/shard_map/attend_0/pallas_call | solution.py:57
  108.9 5.7 %project.4.k_ref.v_ref = bf16[768,768]{1,0:T(8,128)(2,1)} custom-call(bf16[768,1536]{1,0:T(8,128)(2,1)} %norm_in.4.x_ref, bf16[1536,1536]{1,0:T(8,128)(2,1)} %all-gather.3.cloned.1.call-done.weight_ref.refs_2_.refs_3_, f32[768,128]{1,0:T(8,128)} %get-tuple-element.199.cos_ref, f32[768,128]{1,0:T(8,128)} %get-tuple-element.200.sin_ref), custom_call_target="tpu_custom_call" | custom-call | flops 1 | bytes 1 | tf_op jit(solution)/shard_map/project/pallas_call | solution.py:57
  114.6 8.8 %attend_1.1 = (f32[768,768]{1,0:T(8,128)}, f32[24,768]{1,0:T(8,128)}) custom-call(s32[3]{0:T(128)} %pad_add_fusion.1.meta_ref, f32[1,1]{1,0:T(1,128)} %bitcast.3.lam_ref, bf16[768,384]{1,0:T(8,128)(2,1)} %get-tuple-element.122.q_ref, bf16[768,768]{1,0:T(8,128)(2,1)} %project.4.k_ref.v_ref, bf16[768,768]{1,0:T(8,128)(2,1)} %project.4.k_ref.v_ref, ...), custom_call_target="tpu_custom_call" | custom-call | flops 1 | bytes 1 | tf_op jit(solution)/shard_map/attend_1/pallas_call | solution.py:57
  135.2 5.7 %project.5.k_ref.v_ref = bf16[768,768]{1,0:T(8,128)(2,1)} custom-call(bf16[768,1536]{1,0:T(8,128)(2,1)} %norm_in.5.x_ref, bf16[1536,1536]{1,0:T(8,128)(2,1)} %all-gather.3.cloned.1.call-done.weight_ref.refs_2_.refs_3_, f32[768,128]{1,0:T(8,128)} %get-tuple-element.188.cos_ref, f32[768,128]{1,0:T(8,128)} %get-tuple-element.187.sin_ref), custom_call_target="tpu_custom_call" | custom-call | flops 1 | bytes 1 | tf_op jit(solution)/shard_map/project/pallas_call | solution.py:57
  140.9 5.4 %attend_2.1 = (bf16[768,384]{1,0:T(8,128)(2,1)}, f32[384,768]{1,0:T(8,128)}, f32[384,768]{1,0:T(8,128)}, f32[24,768]{1,0:T(8,128)}) custom-call(s32[3]{0:T(128)} %pad_add_fusion.1.meta_ref, f32[1,1]{1,0:T(1,128)} %bitcast.3.lam_ref, bf16[768,384]{1,0:T(8,128)(2,1)} %get-tuple-element.122.q_ref, bf16[768,768]{1,0:T(8,128)(2,1)} %project.5.k_ref.v_ref, ...), custom_call_target="tpu_custom_call" | custom-call | flops 1 | bytes 1 | tf_op jit(solution)/shard_map/attend_2/pallas_call | solution.py:57
  149.9 6.5 %collective-permute-done.19.refs_7_ = bf16[768,384]{1,0:T(8,128)(2,1)S(1)} collective-permute-done((bf16[768,384]{1,0:T(8,128)(2,1)S(1)}, bf16[768,384]{1,0:T(8,128)(2,1)S(1)}, u32[]{:S(2)}, u32[]{:S(2)}) %collective-permute-start.19) | collective-permute-done | bytes 589856 | tf_op jit(solution)/shard_map/ppermute | solution.py:81
  156.4 11.2 %collective-permute-done.14.refs_1_ = bf16[768,384]{1,0:T(8,128)(2,1)S(1)} collective-permute-done((bf16[768,384]{1,0:T(8,128)(2,1)}, bf16[768,384]{1,0:T(8,128)(2,1)S(1)}, u32[]{:S(2)}, u32[]{:S(2)}) %collective-permute-start.14) | collective-permute-done | bytes 589856 | tf_op jit(solution)/shard_map/ppermute | solution.py:81
  167.6 8.2 %collective-permute-done.15.refs_2_ = bf16[768,384]{1,0:T(8,128)(2,1)S(1)} collective-permute-done((bf16[768,384]{1,0:T(8,128)(2,1)}, bf16[768,384]{1,0:T(8,128)(2,1)S(1)}, u32[]{:S(2)}, u32[]{:S(2)}) %collective-permute-start.15) | collective-permute-done | bytes 589856 | tf_op jit(solution)/shard_map/ppermute | solution.py:81
  179.3 10.8 %middle.1 = (f32[768,1536]{1,0:T(8,128)}, bf16[768,1536]{1,0:T(8,128)(2,1)}, f32[768,1]{1,0:T(8,128)}) custom-call(s32[2]{0:T(128)} %pad_add_fusion.spot_ref.at_ref, bf16[768,1536]{1,0:T(8,128)(2,1)} %get-tuple-element.89.x_ref.refs_4_, f32[1,1536]{1,0:T(1,128)} %broadcast_in_dim.33.gain_ref, bf16[768,384]{1,0:T(8,128)(2,1)} %get-tuple-element.103.refs_0_.refs_2_, ...), custom_call_target="tpu_custom_call" | custom-call | flops 1 | bytes 1 | tf_op jit(solution)/shard_map/middle/pallas_call | solution.py:57
  190.1 13.0 %ffn.1 = (bf16[768,1024]{1,0:T(8,128)(2,1)}, bf16[768,1024]{1,0:T(8,128)(2,1)}, bf16[768,1024]{1,0:T(8,128)(2,1)}) custom-call(bf16[768,1536]{1,0:T(8,128)(2,1)} %get-tuple-element.110.x_ref.refs_0_, bf16[768,1536]{1,0:T(8,128)(2,1)} %place_cols.1.dy_ref.refs_0_, bf16[1536,3072]{1,0:T(8,128)(2,1)} %all-gather.5.cloned.1.call-done.gate_w.up_w.down_w.g_ref.u_ref.refs_1_, ...), custom_call_target="tpu_custom_call" | custom-call | flops 1 | bytes 1 | tf_op jit(solution)/shard_map/ffn/pallas_call | solution.py:57
  205.9 11.3 %mid_back.1 = (bf16[192,1536]{1,0:T(8,128)(2,1)}, bf16[192,1536]{1,0:T(8,128)(2,1)}, bf16[192,1536]{1,0:T(8,128)(2,1)}, bf16[192,1536]{1,0:T(8,128)(2,1)}) custom-call(s32[2]{0:T(128)} %pad_add_fusion.spot_ref.at_ref, bf16[768,1024]{1,0:T(8,128)(2,1)} %get-tuple-element.111.dgate_ref.refs_1_, bf16[768,1024]{1,0:T(8,128)(2,1)} %get-tuple-element.112.dup_ref.refs_2_, ...), custom_call_target="tpu_custom_call" | custom-call | flops 1 | bytes 1 | tf_op jit(solution)/shard_map/mid_back/pallas_call | solution.py:57
  229.0 7.9 %down.1 = (bf16[768,384]{1,0:T(8,128)(2,1)}, bf16[768,384]{1,0:T(8,128)(2,1)}, bf16[768,384]{1,0:T(8,128)(2,1)}, bf16[768,384]{1,0:T(8,128)(2,1)}) custom-call(s32[2]{0:T(128)} %pad_add_fusion.spot_ref.at_ref, bf16[768,1024]{1,0:T(8,128)(2,1)} %get-tuple-element.115.refs_1_.refs_0_, ...), custom_call_target="tpu_custom_call" | custom-call | flops 999999995904 | bytes 1 | tf_op jit(solution)/shard_map/down/pallas_call | solution.py:57
  241.6 6.9 %gu_grads_theirs.1 = bf16[768,2048]{1,0:T(8,128)(2,1)} custom-call(s32[1]{0:T(128)S(6)} %sub.44.side_ref, bf16[768,1536]{1,0:T(8,128)(2,1)} %get-tuple-element.110.x_ref.refs_0_, bf16[768,1024]{1,0:T(8,128)(2,1)} %get-tuple-element.111.dgate_ref.refs_1_, bf16[768,1024]{1,0:T(8,128)(2,1)} %get-tuple-element.112.dup_ref.refs_2_), custom_call_target="tpu_custom_call" | custom-call | flops 1 | bytes 1 | tf_op jit(solution)/shard_map/gu_grads_theirs/pallas_call | solution.py:789
  261.3 7.5 %gu_grads.1 = (bf16[768,1024]{1,0:T(8,128)(2,1)}, bf16[768,1024]{1,0:T(8,128)(2,1)}) custom-call(s32[1]{0:T(128)} %bitcast.1.side_ref, bf16[768,1536]{1,0:T(8,128)(2,1)} %get-tuple-element.110.x_ref.refs_0_, bf16[768,1024]{1,0:T(8,128)(2,1)} %get-tuple-element.111.dgate_ref.refs_1_, bf16[768,1024]{1,0:T(8,128)(2,1)} %get-tuple-element.112.dup_ref.refs_2_, ...), custom_call_target="tpu_custom_call" | custom-call | flops 1 | bytes 1 | tf_op jit(solution)/shard_map/gu_grads/pallas_call | solution.py:789
  268.8 6.4 %reduce-scatter.5.cloned.1.call-done = bf16[192,1024]{1,0:T(8,128)(2,1)} async-done(((bf16[768,1024]{1,0:T(8,128)(2,1)}), bf16[192,1024]{1,0:T(8,128)(2,1)}) %reduce-scatter.5.cloned.1.call-update) | async-done | bytes 393232 | tf_op jit(solution)/shard_map/reduce_scatter | solution.py:115
  275.4 8.8 %collective-permute-done.31.refs_2_ = bf16[192,1536]{1,0:T(8,128)(2,1)S(1)} collective-permute-done((bf16[192,1536]{1,0:T(8,128)(2,1)}, bf16[192,1536]{1,0:T(8,128)(2,1)S(1)}, u32[]{:S(2)}, u32[]{:S(2)}) %collective-permute-start.31) | collective-permute-done | bytes 589856 | tf_op jit(solution)/shard_map/ppermute | solution.py:81
  289.0 6.2 %head_back.1 = (bf16[432,768]{1,0:T(8,128)(2,1)}, f32[384,128]{1,0:T(8,128)}) custom-call(f32[1,1]{1,0:T(1,128)} %bitcast.3.lam_ref, bf16[768,1536]{1,0:T(8,128)(2,1)} %place_rows.1.b_ref.refs_0_, bf16[1536,1536]{1,0:T(8,128)(2,1)} %all-gather.3.cloned.1.call-done.weight_ref.refs_2_.refs_3_, f32[384,768]{1,0:T(8,128)} %get-tuple-element.129.unit_ref, ...), custom_call_target="tpu_custom_call" | custom-call | flops 1 | bytes 1 | tf_op jit(solution)/shard_map/head_back/pallas_call | solution.py:57
  303.3 12.9 %attend_back_qk0.1 = (f32[768,384]{1,0:T(8,128)}, f32[768,768]{1,0:T(8,128)}) custom-call(s32[3]{0:T(128)} %pad_add_fusion.1.meta_ref, f32[1,1]{1,0:T(1,128)} %bitcast.3.lam_ref, bf16[768,384]{1,0:T(8,128)(2,1)} %get-tuple-element.122.q_ref, bf16[768,768]{1,0:T(8,128)(2,1)} %get-tuple-element.94.k_ref.v_ref, bf16[768,768]{1,0:T(8,128)(2,1)} %get-tuple-element.94.k_ref.v_ref, ...), custom_call_target="tpu_custom_call" | custom-call | flops 1 | bytes 1 | tf_op jit(solution)/shard_map/attend_back_qk0/pallas_call | solution.py:57
  326.1 9.2 %attend_back_q1.1.refs_3_.refs_0_ = bf16[768,384]{1,0:T(8,128)(2,1)} custom-call(s32[3]{0:T(128)} %pad_add_fusion.1.meta_ref, f32[1,1]{1,0:T(1,128)} %bitcast.3.lam_ref, bf16[768,384]{1,0:T(8,128)(2,1)} %get-tuple-element.122.q_ref, bf16[768,768]{1,0:T(8,128)(2,1)} %project.4.k_ref.v_ref, bf16[768,768]{1,0:T(8,128)(2,1)} %project.4.k_ref.v_ref, ...), custom_call_target="tpu_custom_call" | custom-call | flops 1 | bytes 1 | tf_op jit(solution)/shard_map/attend_back_q1/pallas_call | solution.py:57
  338.5 11.8 %attend_back_k1.1.refs_0_ = f32[768,768]{1,0:T(8,128)} custom-call(s32[3]{0:T(128)} %pad_add_fusion.4.meta_ref, f32[1,1]{1,0:T(1,128)} %bitcast.3.lam_ref, bf16[768,384]{1,0:T(8,128)(2,1)} %collective-permute-done.26.q_ref, bf16[768,768]{1,0:T(8,128)(2,1)} %get-tuple-element.94.k_ref.v_ref, bf16[768,768]{1,0:T(8,128)(2,1)} %get-tuple-element.94.k_ref.v_ref, ...), custom_call_target="tpu_custom_call" | custom-call | flops 1 | bytes 1 | tf_op jit(solution)/shard_map/attend_back_k1/pallas_call | solution.py:57
  352.9 5.6 %attend_back_k2.1.refs_4_.refs_1_ = bf16[768,768]{1,0:T(8,128)(2,1)} custom-call(s32[3]{0:T(128)} %pad_add_fusion.3.meta_ref, f32[1,1]{1,0:T(1,128)} %bitcast.3.lam_ref, bf16[768,384]{1,0:T(8,128)(2,1)} %collective-permute-done.27.q_ref, bf16[768,768]{1,0:T(8,128)(2,1)} %get-tuple-element.94.k_ref.v_ref, bf16[768,768]{1,0:T(8,128)(2,1)} %get-tuple-element.94.k_ref.v_ref, ...), custom_call_target="tpu_custom_call" | custom-call | flops 1 | bytes 1 | tf_op jit(solution)/shard_map/attend_back_k2/pallas_call | solution.py:57
  358.5 7.6 %oqkv_grads_theirs.1 = bf16[768,1536]{1,0:T(8,128)(2,1)} custom-call(s32[1]{0:T(128)S(6)} %sub.44.side_ref, bf16[768,1536]{1,0:T(8,128)(2,1)} %place_rows.1.b_ref.refs_0_, bf16[768,1536]{1,0:T(8,128)(2,1)} %get-tuple-element.90.x_ref.refs_1_, bf16[768,384]{1,0:T(8,128)(2,1)} %get-tuple-element.103.refs_0_.refs_2_, ...), custom_call_target="tpu_custom_call" | custom-call | flops 1 | bytes 1 | tf_op jit(solution)/shard_map/oqkv_grads_theirs/pallas_call | solution.py:789
  366.1 9.6 %in_back.1 = (bf16[784,384]{1,0:T(8,128)(2,1)}, bf16[784,384]{1,0:T(8,128)(2,1)}, bf16[784,384]{1,0:T(8,128)(2,1)}, bf16[784,384]{1,0:T(8,128)(2,1)}, f32[1,1536]{1,0:T(1,128)}) custom-call(s32[2]{0:T(128)} %pad_add_fusion.spot_ref.at_ref, bf16[768,384]{1,0:T(8,128)(2,1)} %attend_back_q1.1.refs_3_.refs_0_, bf16[768,768]{1,0:T(8,128)(2,1)} %attend_back_k2.1.refs_4_.refs_1_, ...), custom_call_target="tpu_custom_call" | custom-call | flops 1 | bytes 1 | tf_op jit(solution)/shard_map/in_back/pallas_call | solution.py:57
  377.2 7.9 %oqkv_grads.1 = bf16[768,1536]{1,0:T(8,128)(2,1)} custom-call(s32[1]{0:T(128)} %bitcast.1.side_ref, bf16[768,1536]{1,0:T(8,128)(2,1)} %place_rows.1.b_ref.refs_0_, bf16[768,1536]{1,0:T(8,128)(2,1)} %get-tuple-element.90.x_ref.refs_1_, bf16[768,384]{1,0:T(8,128)(2,1)} %get-tuple-element.103.refs_0_.refs_2_, bf16[768,384]{1,0:T(8,128)(2,1)} %attend_back_q1.1.refs_3_.refs_0_, ...), custom_call_target="tpu_custom_call" | custom-call | flops 1 | bytes 1 | tf_op jit(solution)/shard_map/oqkv_grads/pallas_call | solution.py:789
  406.1 12.4 %collective-permute-done.39 = bf16[784,384]{1,0:T(8,128)(2,1)S(1)} collective-permute-done((bf16[784,384]{1,0:T(8,128)(2,1)}, bf16[784,384]{1,0:T(8,128)(2,1)S(1)}, u32[]{:S(2)}, u32[]{:S(2)}) %collective-permute-start.39) | collective-permute-done | bytes 602144 | tf_op jit(solution)/shard_map/ppermute | solution.py:81
  (274 shorter events, 163.2 us)
Async XLA Ops:
  7.2 75.1 %all-gather.3.cloned.1.call-start = ((), (), s32[]{:S(2)}) async-start(), calls=%async_computation.4 | async-start | bytes 5308416 | tf_op jit(solution)/shard_map/all_gather | solution.py:111
  9.4 180.7 %all-gather.5.cloned.1.call-start = ((), (), s32[]{:S(2)}) async-start(), calls=%async_computation.5 | async-start | bytes 10616832 | tf_op jit(solution)/shard_map/all_gather | solution.py:111
  10.6 264.6 %reduce-scatter.5.cloned.1.call-start = ((), (), s32[]{:S(2)}) async-start(), calls=%async_computation.6 | async-start | bytes 1966080 | tf_op jit(solution)/shard_map/reduce_scatter | solution.py:115
  12.3 27.4 %collective-permute-start.1 = (bf16[768,384]{1,0:T(8,128)(2,1)S(1)}, bf16[768,384]{1,0:T(8,128)(2,1)S(1)}, u32[]{:S(2)}, u32[]{:S(2)}) collective-permute-start(bf16[768,384]{1,0:T(8,128)(2,1)S(1)} %copy-done.2), channel_id=1, source_target_pairs={{0,2},{1,3},{2,0},{3,1},{4,6},{5,7},{6,4},{7,5},{8,10},{9,11},{10,... | collective-permute-start | bytes 1769480 | tf_op jit(solution)/shard_map/ppermute | solution.py:81
  13.8 25.9 %collective-permute-start.2 = (bf16[768,384]{1,0:T(8,128)(2,1)S(1)}, bf16[768,384]{1,0:T(8,128)(2,1)S(1)}, u32[]{:S(2)}, u32[]{:S(2)}) collective-permute-start(bf16[768,384]{1,0:T(8,128)(2,1)S(1)} %copy-done.2), channel_id=1, source_target_pairs={{0,3},{1,2},{2,1},{3,0},{4,7},{5,6},{6,5},{7,4},{8,11},{9,10},{10,... | collective-permute-start | bytes 1769480 | tf_op jit(solution)/shard_map/ppermute | solution.py:81
  14.3 40.5 %collective-permute-start.6 = (bf16[768,384]{1,0:T(8,128)(2,1)S(1)}, bf16[768,384]{1,0:T(8,128)(2,1)S(1)}, u32[]{:S(2)}, u32[]{:S(2)}) collective-permute-start(bf16[768,384]{1,0:T(8,128)(2,1)S(1)} %copy-done.2), channel_id=1, source_target_pairs={{0,4},{4,8},{8,12},{1,5},{5,9},{9,13},{2,6},{6,10},{10,14},{3,7},{... | collective-permute-start | bytes 1769480 | tf_op jit(solution)/shard_map/ppermute | solution.py:873
  47.2 28.1 %collective-permute-start.4 = (bf16[768,384]{1,0:T(8,128)(2,1)S(1)}, bf16[768,384]{1,0:T(8,128)(2,1)S(1)}, u32[]{:S(2)}, u32[]{:S(2)}) collective-permute-start(bf16[768,384]{1,0:T(8,128)(2,1)S(1)} %copy-done.11), channel_id=1, source_target_pairs={{0,2},{1,3},{2,0},{3,1},{4,6},{5,7},{6,4},{7,5},{8,10},{9,11},{10,... | collective-permute-start | bytes 1769480 | tf_op jit(solution)/shard_map/ppermute | solution.py:81
  48.8 29.2 %collective-permute-start.5 = (bf16[768,384]{1,0:T(8,128)(2,1)S(1)}, bf16[768,384]{1,0:T(8,128)(2,1)S(1)}, u32[]{:S(2)}, u32[]{:S(2)}) collective-permute-start(bf16[768,384]{1,0:T(8,128)(2,1)S(1)} %copy-done.11), channel_id=1, source_target_pairs={{0,3},{1,2},{2,1},{3,0},{4,7},{5,6},{6,5},{7,4},{8,11},{9,10},{10,... | collective-permute-start | bytes 1769480 | tf_op jit(solution)/shard_map/ppermute | solution.py:81
  54.7 45.8 %collective-permute-start.7 = (bf16[768,384]{1,0:T(8,128)(2,1)S(1)}, bf16[768,384]{1,0:T(8,128)(2,1)}, u32[]{:S(2)}, u32[]{:S(2)}) collective-permute-start(bf16[768,384]{1,0:T(8,128)(2,1)S(1)} %collective-permute-done.6.refs_0_), channel_id=1, source_target_pairs={{4,8},{8,12},{5,9},{9,13},{6,10},{10,14},{7,11},{11,15},{20,24},{2... | collective-permute-start | bytes 1769480 | tf_op jit(solution)/shard_map/ppermute | solution.py:873
  63.1 37.4 %collective-permute-start.8 = (bf16[768,384]{1,0:T(8,128)(2,1)S(1)}, bf16[768,384]{1,0:T(8,128)(2,1)S(1)}, u32[]{:S(2)}, u32[]{:S(2)}) collective-permute-start(bf16[768,384]{1,0:T(8,128)(2,1)S(1)} %collective-permute-done.6.refs_0_), channel_id=1, source_target_pairs={{0,1},{1,0},{2,3},{3,2},{4,5},{5,4},{6,7},{7,6},{8,9},{9,8},{10,11... | collective-permute-start | bytes 1769480 | tf_op jit(solution)/shard_map/ppermute | solution.py:81
  63.5 37.0 %collective-permute-start.9 = (bf16[768,384]{1,0:T(8,128)(2,1)S(1)}, bf16[768,384]{1,0:T(8,128)(2,1)}, u32[]{:S(2)}, u32[]{:S(2)}) collective-permute-start(bf16[768,384]{1,0:T(8,128)(2,1)S(1)} %collective-permute-done.6.refs_0_), channel_id=1, source_target_pairs={{0,2},{1,3},{2,0},{3,1},{4,6},{5,7},{6,4},{7,5},{8,10},{9,11},{10,... | collective-permute-start | bytes 1769480 | tf_op jit(solution)/shard_map/ppermute | solution.py:81
  75.3 25.2 %collective-permute-start.10 = (bf16[768,384]{1,0:T(8,128)(2,1)S(1)}, bf16[768,384]{1,0:T(8,128)(2,1)}, u32[]{:S(2)}, u32[]{:S(2)}) collective-permute-start(bf16[768,384]{1,0:T(8,128)(2,1)S(1)} %collective-permute-done.6.refs_0_), channel_id=1, source_target_pairs={{0,3},{1,2},{2,1},{3,0},{4,7},{5,6},{6,5},{7,4},{8,11},{9,10},{10,... | collective-permute-start | bytes 1769480 | tf_op jit(solution)/shard_map/ppermute | solution.py:81
  100.5 24.0 %collective-permute-start.11 = (bf16[768,384]{1,0:T(8,128)(2,1)}, bf16[768,384]{1,0:T(8,128)(2,1)S(1)}, u32[]{:S(2)}, u32[]{:S(2)}) collective-permute-start(bf16[768,384]{1,0:T(8,128)(2,1)} %collective-permute-done.7.refs_0_), channel_id=1, source_target_pairs={{0,1},{1,0},{2,3},{3,2},{4,5},{5,4},{6,7},{7,6},{8,9},{9,8},{10,11... | collective-permute-start | bytes 1769480 | tf_op jit(solution)/shard_map/ppermute | solution.py:81
  101.4 24.2 %collective-permute-start.12 = (bf16[768,384]{1,0:T(8,128)(2,1)}, bf16[768,384]{1,0:T(8,128)(2,1)S(1)}, u32[]{:S(2)}, u32[]{:S(2)}) collective-permute-start(bf16[768,384]{1,0:T(8,128)(2,1)} %collective-permute-done.7.refs_0_), channel_id=1, source_target_pairs={{0,2},{1,3},{2,0},{3,1},{4,6},{5,7},{6,4},{7,5},{8,10},{9,11},{10,... | collective-permute-start | bytes 1769480 | tf_op jit(solution)/shard_map/ppermute | solution.py:81
  128.6 27.8 %collective-permute-start.19 = (bf16[768,384]{1,0:T(8,128)(2,1)S(1)}, bf16[768,384]{1,0:T(8,128)(2,1)S(1)}, u32[]{:S(2)}, u32[]{:S(2)}) collective-permute-start(bf16[768,384]{1,0:T(8,128)(2,1)S(1)} %constant_dynamic-slice_fusion.refs_4_), channel_id=1, source_target_pairs={{0,3},{1,2},{2,1},{3,0},{4,7},{5,6},{6,5},{7,4},{8,11},{9,10},{10,... | collective-permute-start | bytes 1769480 | tf_op jit(solution)/shard_map/ppermute | solution.py:81
  148.0 27.8 %collective-permute-start.15 = (bf16[768,384]{1,0:T(8,128)(2,1)}, bf16[768,384]{1,0:T(8,128)(2,1)S(1)}, u32[]{:S(2)}, u32[]{:S(2)}) collective-permute-start(bf16[768,384]{1,0:T(8,128)(2,1)} %get-tuple-element.103.refs_0_.refs_2_), channel_id=1, source_target_pairs={{0,2},{1,3},{2,0},{3,1},{4,6},{5,7},{6,4},{7,5},{8,10},{9,11},{10,... | collective-permute-start | bytes 1769480 | tf_op jit(solution)/shard_map/ppermute | solution.py:81
  148.0 29.1 %collective-permute-start.16 = (bf16[768,384]{1,0:T(8,128)(2,1)}, bf16[768,384]{1,0:T(8,128)(2,1)S(1)}, u32[]{:S(2)}, u32[]{:S(2)}) collective-permute-start(bf16[768,384]{1,0:T(8,128)(2,1)} %get-tuple-element.103.refs_0_.refs_2_), channel_id=1, source_target_pairs={{0,3},{1,2},{2,1},{3,0},{4,7},{5,6},{6,5},{7,4},{8,11},{9,10},{10,... | collective-permute-start | bytes 1769480 | tf_op jit(solution)/shard_map/ppermute | solution.py:81
  149.8 27.3 %collective-permute-start.20 = (bf16[768,384]{1,0:T(8,128)(2,1)S(1)}, bf16[768,384]{1,0:T(8,128)(2,1)S(1)}, u32[]{:S(2)}, u32[]{:S(2)}) collective-permute-start(bf16[768,384]{1,0:T(8,128)(2,1)S(1)} %constant_dynamic-slice_fusion.refs_4_), channel_id=1, source_target_pairs={{0,16},{16,0},{1,17},{17,1},{2,18},{18,2},{3,19},{19,3},{4,20},{20... | collective-permute-start | bytes 1769480 | tf_op jit(solution)/shard_map/ppermute | solution.py:85
  221.9 26.6 %collective-permute-start.24 = (bf16[192,1536]{1,0:T(8,128)(2,1)}, bf16[192,1536]{1,0:T(8,128)(2,1)}, u32[]{:S(2)}, u32[]{:S(2)}) collective-permute-start(bf16[192,1536]{1,0:T(8,128)(2,1)} %get-tuple-element.119), channel_id=1, source_target_pairs={{0,1},{1,0},{2,3},{3,2},{4,5},{5,4},{6,7},{7,6},{8,9},{9,8},{10,11... | collective-permute-start | bytes 1769480 | tf_op jit(solution)/shard_map/ppermute | solution.py:81
  221.9 27.8 %collective-permute-start.28 = (bf16[192,1536]{1,0:T(8,128)(2,1)}, bf16[192,1536]{1,0:T(8,128)(2,1)}, u32[]{:S(2)}, u32[]{:S(2)}) collective-permute-start(bf16[192,1536]{1,0:T(8,128)(2,1)} %get-tuple-element.125), channel_id=1, source_target_pairs={{0,2},{1,3},{2,0},{3,1},{4,6},{5,7},{6,4},{7,5},{8,10},{9,11},{10,... | collective-permute-start | bytes 1769480 | tf_op jit(solution)/shard_map/ppermute | solution.py:81
  224.0 27.6 %collective-permute-start.29 = (bf16[192,1536]{1,0:T(8,128)(2,1)}, bf16[192,1536]{1,0:T(8,128)(2,1)}, u32[]{:S(2)}, u32[]{:S(2)}) collective-permute-start(bf16[192,1536]{1,0:T(8,128)(2,1)} %get-tuple-element.126), channel_id=1, source_target_pairs={{0,3},{1,2},{2,1},{3,0},{4,7},{5,6},{6,5},{7,4},{8,11},{9,10},{10,... | collective-permute-start | bytes 1769480 | tf_op jit(solution)/shard_map/ppermute | solution.py:81
  241.6 109.9 %reduce-scatter.7.cloned.1.call-start = ((), (), s32[]{:S(2)}) async-start(), calls=%async_computation.7 | async-start | bytes 1966080 | tf_op jit(solution)/shard_map/reduce_scatter | solution.py:115
  257.1 27.1 %collective-permute-start.31 = (bf16[192,1536]{1,0:T(8,128)(2,1)}, bf16[192,1536]{1,0:T(8,128)(2,1)S(1)}, u32[]{:S(2)}, u32[]{:S(2)}) collective-permute-start(bf16[192,1536]{1,0:T(8,128)(2,1)} %get-tuple-element.128.refs_0_), channel_id=1, source_target_pairs={{0,2},{1,3},{2,0},{3,1},{4,6},{5,7},{6,4},{7,5},{8,10},{9,11},{10,... | collective-permute-start | bytes 1769480 | tf_op jit(solution)/shard_map/ppermute | solution.py:81
  258.8 25.4 %collective-permute-start.32 = (bf16[192,1536]{1,0:T(8,128)(2,1)}, bf16[192,1536]{1,0:T(8,128)(2,1)S(1)}, u32[]{:S(2)}, u32[]{:S(2)}) collective-permute-start(bf16[192,1536]{1,0:T(8,128)(2,1)} %get-tuple-element.128.refs_0_), channel_id=1, source_target_pairs={{0,3},{1,2},{2,1},{3,0},{4,7},{5,6},{6,5},{7,4},{8,11},{9,10},{10,... | collective-permute-start | bytes 1769480 | tf_op jit(solution)/shard_map/ppermute | solution.py:81
  275.3 111.6 %reduce-scatter.9.cloned.1.call-start = ((), (), s32[]{:S(2)}) async-start(), calls=%async_computation.8 | async-start | bytes 1966080 | tf_op jit(solution)/shard_map/reduce_scatter | solution.py:115
  295.2 30.9 %collective-permute-start.33 = (bf16[432,768]{1,0:T(8,128)(2,1)}, bf16[432,768]{1,0:T(8,128)(2,1)S(1)}, u32[]{:S(2)}, u32[]{:S(2)}) collective-permute-start(bf16[432,768]{1,0:T(8,128)(2,1)} %get-tuple-element.132.grad_ref), channel_id=1, source_target_pairs={{4,0},{8,4},{12,8},{5,1},{9,5},{13,9},{6,2},{10,6},{14,10},{7,3},{... | collective-permute-start | bytes 1990664 | tf_op jit(solution)/shard_map/ppermute | solution.py:960
  299.4 24.8 %collective-permute-start.35 = (bf16[768,384]{1,0:T(8,128)(2,1)}, bf16[768,384]{1,0:T(8,128)(2,1)S(1)}, u32[]{:S(2)}, u32[]{:S(2)}) collective-permute-start(bf16[768,384]{1,0:T(8,128)(2,1)} %get-tuple-element.138), channel_id=1, source_target_pairs={{0,2},{1,3},{2,0},{3,1},{4,6},{5,7},{6,4},{7,5},{8,10},{9,11},{10,... | collective-permute-start | bytes 1769480 | tf_op jit(solution)/shard_map/ppermute | solution.py:81
  300.3 23.9 %collective-permute-start.34 = (bf16[768,384]{1,0:T(8,128)(2,1)}, bf16[768,384]{1,0:T(8,128)(2,1)}, u32[]{:S(2)}, u32[]{:S(2)}) collective-permute-start(bf16[768,384]{1,0:T(8,128)(2,1)} %get-tuple-element.136), channel_id=1, source_target_pairs={{0,1},{1,0},{2,3},{3,2},{4,5},{5,4},{6,7},{7,6},{8,9},{9,8},{10,11... | collective-permute-start | bytes 1769480 | tf_op jit(solution)/shard_map/ppermute | solution.py:81
  301.3 50.3 %collective-permute-start.37 = (bf16[432,768]{1,0:T(8,128)(2,1)}, bf16[432,768]{1,0:T(8,128)(2,1)S(1)}, u32[]{:S(2)}, u32[]{:S(2)}) collective-permute-start(bf16[432,768]{1,0:T(8,128)(2,1)} %get-tuple-element.132.grad_ref), channel_id=1, source_target_pairs={{8,0},{12,4},{9,1},{13,5},{10,2},{14,6},{11,3},{15,7},{24,16},{28,... | collective-permute-start | bytes 1990664 | tf_op jit(solution)/shard_map/ppermute | solution.py:960
  351.6 85.3 %reduce-scatter.11.cloned.1.call-start = ((), (), s32[]{:S(2)}) async-start(), calls=%async_computation.9 | async-start | bytes 2949120 | tf_op jit(solution)/shard_map/reduce_scatter | solution.py:115
  390.9 27.6 %collective-permute-start.39 = (bf16[784,384]{1,0:T(8,128)(2,1)}, bf16[784,384]{1,0:T(8,128)(2,1)S(1)}, u32[]{:S(2)}, u32[]{:S(2)}) collective-permute-start(bf16[784,384]{1,0:T(8,128)(2,1)} %get-tuple-element.150), channel_id=1, source_target_pairs={{0,2},{1,3},{2,0},{3,1},{4,6},{5,7},{6,4},{7,5},{8,10},{9,11},{10,... | collective-permute-start | bytes 1806344 | tf_op jit(solution)/shard_map/ppermute | solution.py:81
  391.5 27.1 %collective-permute-start.38 = (bf16[784,384]{1,0:T(8,128)(2,1)}, bf16[784,384]{1,0:T(8,128)(2,1)S(1)}, u32[]{:S(2)}, u32[]{:S(2)}) collective-permute-start(bf16[784,384]{1,0:T(8,128)(2,1)} %get-tuple-element.149), channel_id=1, source_target_pairs={{0,1},{1,0},{2,3},{3,2},{4,5},{5,4},{6,7},{7,6},{8,9},{9,8},{10,11... | collective-permute-start | bytes 1806344 | tf_op jit(solution)/shard_map/ppermute | solution.py:81
  (75 other events, 795.4 us)
Sparse Core Ops, SparseCore 0:
  10.2 62.8 all-gather.2
  74.7 94.8 all-gather.4
  241.7 33.5 reduce-scatter.4
  277.4 46.4 reduce-scatter.6
  351.7 35.1 reduce-scatter.8
  389.0 47.8 reduce-scatter.10
